TPU v7x, 256 devices: a whole 4x4x8 slice. The times are simulated.
256 devices in a mesh: dcn: 2 (over core), gx: 8 (over z), gy: 16 (over x, y).
Axes of the slice: x: 4, y: 4, z: 8, core: 2. Of those that a mesh axis runs over, the one named last changes fastest.
Arguments:
- features: bfloat16 [2, 128, 256, 2, 8, 128], P('dcn', 'gx', 'gy'), may hold values from -6 to 6
- grad_out: bfloat16 [2, 128, 256, 2, 8, 128], P('dcn', 'gx', 'gy'), may hold values from -6 to 6
- occupancy: int32 [2, 128, 256, 2, 8], P('dcn', 'gx', 'gy'), may hold values from 0 to 1, as said below
- leaf_z: int32 [2, 16, 32, 2], P('dcn', 'gx', 'gy'), may hold values from -1 to 2, as said below
- neighbours: int32 [2, 16, 32, 2, 27], P('dcn', 'gx', 'gy'), may hold values from 0 to 2, as said below
- kernel: bfloat16 [27, 128, 128], replicated, may hold values from -0.15625 to 0.15625
Outputs:
- grad_features: bfloat16 [2, 128, 256, 2, 8, 128], P('dcn', 'gx', 'gy')
- kernel_grad: float32 [27, 128, 128], replicated
Inputs may be any that keep to these rules, and one draw needn't show every extreme that they name: `leaf_z`: in every leaf column the active slots come first, with distinct z positions in rising order below 3; the other slots hold -1. Every scene has a leaf column with all 2 slots active. `neighbours`: for an active slot holding z position h and offset k = 9 (p + 1) + 3 (q + 1) + (r + 1), the slot of the active leaf at z position h + r in the column p, q away, or 2 if there is none; slots that are not active hold 2 at every offset. `occupancy`: zero at every voxel of a slot that is not active.
All inputs are finite; a program needn't handle non-finite values.
Results may differ from a plain program's by a relative error of at most 0.001.
Values may be sent and summed in bfloat16 or wider, within the bound.
No kernel may reach another device: no remote copies, remote signals or barrier semaphores. Data moves between devices by JAX's collectives and lax.ppermute only.
A program may use at most 64 MiB of HBM per device.

v0:
```python
import math

import jax
import jax.numpy as jnp
from jax import lax
from jax.sharding import PartitionSpec as P


def padded_2(cells, sides, width):
    for axis, dim in sides:
        count = lax.axis_size(axis)
        ends = count - 1
        head = lax.slice_in_dim(cells, 0, width, axis=dim)
        tail = lax.slice_in_dim(cells, cells.shape[dim] - width, cells.shape[dim], axis=dim)
        cells = jnp.concatenate(
            [
                lax.ppermute(tail, axis, [(i, (i + 1) % count) for i in range(ends)]),
                cells,
                lax.ppermute(head, axis, [((i + 1) % count, i) for i in range(ends)]),
            ],
            axis=dim,
        )
    return cells


def leaf_columns(padded, adjacent_row, edge):
    width = padded.shape[-1]
    spots = jnp.arange(edge + 2, dtype=jnp.int32)
    region = (spots > 0).astype(jnp.int32) + (spots > edge).astype(jnp.int32)
    base_index = region[:, None] * 9 + region[None, :] * 3
    rows_x = spots[:, None]
    rows_y = spots[None, :]
    planes = []
    for layer in range(3):
        chosen_slot = jnp.take(adjacent_row, base_index + layer)
        planes.append(padded[rows_x, rows_y, chosen_slot])
    column = jnp.concatenate([planes[0][:, :, edge - 1 :], planes[1], planes[2][:, :, :1]], axis=2)
    pieces = []
    for step_x in (-1, 0, 1):
        for step_y in (-1, 0, 1):
            for step_z in (-1, 0, 1):
                pieces.append(
                    column[
                        1 - step_x : 1 - step_x + edge,
                        1 - step_y : 1 - step_y + edge,
                        1 - step_z : 1 - step_z + edge,
                    ]
                )
    stacked = jnp.stack(pieces, axis=3)
    return stacked.reshape(edge * edge * edge, 27 * width)


def reduce_kernel(kernel_acc, width, scale):
    flat_terms = kernel_acc.reshape(-1)
    summed = lax.psum(flat_terms, ("dcn", "gx", "gy"))
    return jnp.transpose(summed.reshape(width, 27, width), (1, 0, 2)) * scale


def local(features, grad_out, occupancy, leaf_z, neighbours, kernel):
    edge = features.shape[4]
    leaves = features.shape[3]
    width = features.shape[-1]
    cols_x = leaf_z.shape[1]
    cols_y = leaf_z.shape[2]
    active = (leaf_z[0] >= 0).astype(jnp.int32)
    active_vox = jnp.repeat(jnp.repeat(active, edge, axis=0), edge, axis=1)
    keep = occupancy[0] * active_vox[..., None]
    keep_b = keep.astype(jnp.bfloat16)[..., None]
    masked = grad_out[0] * keep_b
    masked_in = features[0] * keep_b
    halo = padded_2(masked[None], (("gx", 1), ("gy", 2)), 1)[0]
    halo_zero = jnp.concatenate(
        [halo, jnp.zeros((halo.shape[0], halo.shape[1], 1, edge, width), jnp.bfloat16)], axis=2
    )
    wrows = jnp.transpose(kernel, (0, 2, 1)).reshape(27 * width, width)
    voxels = edge * edge * edge
    scale = 1.0 / math.sqrt(
        lax.axis_size("dcn")
        * lax.axis_size("gx")
        * lax.axis_size("gy")
        * cols_x
        * cols_y
        * voxels
        * leaves
    )
    grad_start = jnp.zeros((edge, edge, leaves, edge, width), jnp.bfloat16)
    kernel_start = jnp.zeros((width, 27 * width), jnp.float32)

    def grad_update(leaf, grad_tile, columns, column_keep):
        leaf_keep = lax.dynamic_index_in_dim(column_keep, leaf, 2, keepdims=False).reshape(voxels)
        result = jnp.dot(columns, wrows, preferred_element_type=jnp.float32) * leaf_keep[
            :, None
        ].astype(jnp.float32)
        return lax.dynamic_update_slice_in_dim(
            grad_tile, result.astype(jnp.bfloat16).reshape(edge, edge, 1, edge, width), leaf, 2
        )

    def kernel_update(leaf, kernel_acc, columns, column_in):
        own = lax.dynamic_index_in_dim(column_in, leaf, 2, keepdims=False).reshape(voxels, width)
        return kernel_acc + jnp.dot(own.T, columns, preferred_element_type=jnp.float32)

    tiles = []
    kernel_acc = kernel_start
    for column_x in range(cols_x):
        row_tiles = []
        for column_y in range(cols_y):
            window = halo_zero[
                column_x * edge : column_x * edge + edge + 2,
                column_y * edge : column_y * edge + edge + 2,
            ]
            column_column_keep = keep[
                column_x * edge : (column_x + 1) * edge, column_y * edge : (column_y + 1) * edge
            ]
            column_column_in = masked_in[
                column_x * edge : (column_x + 1) * edge, column_y * edge : (column_y + 1) * edge
            ]
            adjacent = neighbours[0, column_x, column_y]
            leaf_total = jnp.sum(active[column_x, column_y])
            joint_window = window
            joint_column_keep = column_column_keep
            joint_column_in = column_column_in
            joint_adjacent = adjacent

            def joint_step(leaf, carry):
                columns = leaf_columns(joint_window, joint_adjacent[leaf], edge)
                return (
                    grad_update(leaf, carry[0], columns, joint_column_keep),
                    kernel_update(leaf, carry[1], columns, joint_column_in),
                )

            grad_tile, kernel_acc = lax.fori_loop(
                0, leaf_total, joint_step, (grad_start, kernel_acc)
            )
            row_tiles.append(grad_tile)
        tiles.append(row_tiles)
    kernel_grad = reduce_kernel(kernel_acc, width, scale)
    block = jnp.concatenate([jnp.concatenate(row_tiles, axis=1) for row_tiles in tiles], axis=0)
    return (block[None], kernel_grad)


def solution(mesh):
    return jax.shard_map(
        local,
        mesh=mesh,
        in_specs=(
            P("dcn", "gx", "gy", None, None, None),
            P("dcn", "gx", "gy", None, None, None),
            P("dcn", "gx", "gy", None, None),
            P("dcn", "gx", "gy", None),
            P("dcn", "gx", "gy", None, None),
            P(),
        ),
        out_specs=(P("dcn", "gx", "gy", None, None, None), P()),
        check_vma=False,
    )
```

profile of v0, /device:TPU:1, one launch (start us, length us, event | category | flops | bytes accessed | tf_op | source)
XLA Modules:
  0.0 502.2 jit_solution(10887460242859021505)
XLA Ops:
  8.0 1.1 copy.120
  9.4 1.7 broadcast_multiply_fusion.9
  11.2 4.4 collective-permute-start
  15.6 1.3 collective-permute-start.1
  17.6 1.1 fusion.306
  19.9 2.2 copy.123
  22.2 3.2 collective-permute-start.2
  25.4 1.3 collective-permute-start.3
  27.4 3.1 collective-permute-done.3
  30.7 1.4 pad_slice_fusion.128
  33.0 40.5 %while.48 = (s32[]{:T(128)}, bf16[8,8,2,8,128]{4,3,1,0,2:T(8,128)(2,1)}, f32[128,3456]{1,0:T(8,128)S(1)}, s32[]{:T(128)}, s32[2,27]{1,0:T(2,128)S(1)}, /*index=5...) while((s32[]{:T(128)}, ...), condition=%wide.region_2.4_spmd, body=%wide.region_1.3_spmd.sunk | while | flops 911271296 | bytes 25689568 | solution.py:131
  33.8 1.2 gather_fusion.1
  35.2 1.2 gather_fusion.2
  36.7 1.2 gather_fusion
  38.2 2.5 gather_fusion.3
  40.7 2.5 gather_fusion.4
  44.8 2.5 gather_fusion.5
  56.8 0.8 fusion.482
  58.3 0.8 fusion.484
  61.2 0.8 fusion.488
  65.6 3.0 convolution_add_fusion.8
  68.8 3.3 fusion.494
  74.2 37.5 %while.49 = (s32[]{:T(128)}, bf16[8,8,2,8,128]{4,3,1,0,2:T(8,128)(2,1)}, f32[128,3456]{1,0:T(8,128)S(1)}, s32[]{:T(128)}, s32[2,27]{1,0:T(2,128)S(1)}, /*index=5...) while((s32[]{:T(128)}, ...), condition=%wide.region_5.7_spmd, body=%wide.region_4.6_spmd.sunk | while | flops 911271296 | bytes 25689568 | solution.py:131
  75.3 1.2 gather_fusion.7
  76.7 1.2 gather_fusion.8
  78.1 1.2 gather_fusion.6
  79.6 1.4 gather_fusion.9
  81.1 1.4 gather_fusion.10
  84.1 1.4 gather_fusion.11
  95.0 0.8 fusion.516
  96.5 0.8 fusion.518
  99.5 0.8 fusion.522
  103.8 3.0 convolution_add_fusion.9
  107.0 3.3 fusion.528
  112.5 37.7 %while.50 = (s32[]{:T(128)}, bf16[8,8,2,8,128]{4,3,1,0,2:T(8,128)(2,1)}, f32[128,3456]{1,0:T(8,128)S(1)}, s32[]{:T(128)}, s32[2,27]{1,0:T(2,128)S(1)}, /*index=5...) while((s32[]{:T(128)}, ...), condition=%wide.region_8.10_spmd, body=%wide.region_7.9_spmd.sunk | while | flops 911271296 | bytes 25689568 | solution.py:131
  113.7 1.2 gather_fusion.13
  115.1 1.2 gather_fusion.14
  116.5 1.2 gather_fusion.12
  118.0 1.4 gather_fusion.15
  119.5 1.4 gather_fusion.16
  122.5 1.4 gather_fusion.17
  133.4 0.8 fusion.550
  134.9 0.8 fusion.552
  137.9 0.8 fusion.556
  142.2 3.0 convolution_add_fusion.10
  145.4 3.3 fusion.562
  150.3 36.8 %while.51 = (s32[]{:T(128)}, bf16[8,8,2,8,128]{4,3,1,0,2:T(8,128)(2,1)S(1)}, f32[128,3456]{1,0:T(8,128)S(1)}, s32[]{:T(128)}, s32[2,27]{1,0:T(2,128)S(1)}, /*ind...) while((s32[]{:T(128)}, ...), condition=%wide.region_11.13_spmd, body=%wide.region_10.12_spmd.sunk | while | flops 911271296 | bytes 23592360 | solution.py:131
  151.4 1.2 gather_fusion.19
  152.8 1.2 gather_fusion.20
  154.2 1.2 gather_fusion.18
  155.7 1.4 gather_fusion.21
  157.2 1.4 gather_fusion.22
  160.1 1.4 gather_fusion.23
  171.1 0.8 fusion.584
  172.6 0.8 fusion.586
  175.5 0.8 fusion.590
  179.9 3.0 convolution_add_fusion.11
  183.1 3.3 fusion.596
  187.1 1.3 reshape.222
  188.5 1.2 copy_bitcast_fusion
  189.7 298.8 %all-reduce.3.cloned.1.call-done = f32[442368]{0:T(1024)} async-done(((f32[442368]{0:T(1024)}), f32[442368]{0:T(1024)}) %all-reduce.3.cloned.1.call-update) | async-done | bytes 1769488 | tf_op jit(solution)/shard_map/psum | solution.py:55
  488.4 1.6 broadcast_multiply_fusion.8
  490.0 1.5 mul.180
  491.5 3.8 copy.128
  (247 shorter events, 83.2 us)
Async XLA Ops:
  7.2 9.7 %copy-start.5 = (bf16[1,16,16,2,8,128]{5,4,3,2,1,0:T(8,128)(2,1)S(1)}, bf16[1,16,16,2,8,128]{5,4,3,2,1,0:T(8,128)(2,1)}, u32[]{:S(2)}) copy-start(bf16[1,16,16,2,8,128]{5,4,3,2,1,0:T(8,128)(2,1)} %param.16) | copy-start | bytes 3145732
  7.2 481.3 %all-reduce.3.cloned.1.call-start = ((), (), s32[]{:S(2)}) async-start(), calls=%async_computation | async-start | bytes 3538944 | tf_op jit(solution)/shard_map/psum | solution.py:55
  9.4 10.0 %copy-start.19 = (s32[1,2,2,2,27]{4,3,2,1,0:T(2,128)S(1)}, s32[1,2,2,2,27]{4,3,2,1,0:T(2,128)}, u32[]{:S(2)}) copy-start(s32[1,2,2,2,27]{4,3,2,1,0:T(2,128)} %param.20) | copy-start | bytes 2596
  11.2 10.9 %collective-permute-start = (bf16[1,1,16,2,8,128]{5,4,3,2,1,0:T(8,128)(2,1)S(1)}, bf16[1,1,16,2,8,128]{5,4,3,2,1,0:T(8,128)(2,1)S(1)}, u32[]{:S(2)}, u32[]{:S(2)}) collective-permute-start(bf16[1,1,16,2,8,128]{5,4,3,2,1,0:T(8,128)(2,1)S(1)} %get-tuple-element.329), channel_id=1, source_target_pairs={{0,16},{16,32},{32,48},{48,64},{64,80},{80,96},{96,112},{1,17},{17... | collective-permute-start | bytes 196616 | tf_op jit(solution)/shard_map/ppermute | solution.py:17
  15.6 6.5 %collective-permute-start.1 = (bf16[1,1,16,2,8,128]{5,4,3,2,1,0:T(8,128)(2,1)S(1)}, bf16[1,1,16,2,8,128]{5,4,3,2,1,0:T(8,128)(2,1)S(1)}, u32[]{:S(2)}, u32[]{:S(2)}) collective-permute-start(bf16[1,1,16,2,8,128]{5,4,3,2,1,0:T(8,128)(2,1)S(1)} %get-tuple-element.330), channel_id=1, source_target_pairs={{16,0},{32,16},{48,32},{64,48},{80,64},{96,80},{112,96},{17,1},{33... | collective-permute-start | bytes 196616 | tf_op jit(solution)/shard_map/ppermute | solution.py:19
  22.2 5.3 %collective-permute-start.2 = (bf16[1,18,1,2,8,128]{5,4,3,2,1,0:T(8,128)(2,1)S(1)}, bf16[1,18,1,2,8,128]{5,4,3,2,1,0:T(8,128)(2,1)S(1)}, u32[]{:S(2)}, u32[]{:S(2)}) collective-permute-start(bf16[1,18,1,2,8,128]{5,4,3,2,1,0:T(8,128)(2,1)S(1)} %get-tuple-element.323), channel_id=1, source_target_pairs={{0,1},{1,2},{2,3},{3,4},{4,5},{5,6},{6,7},{7,8},{8,9},{9,10},{10,1... | collective-permute-start | bytes 221192 | tf_op jit(solution)/shard_map/ppermute | solution.py:17
  25.4 5.1 %collective-permute-start.3 = (bf16[1,18,1,2,8,128]{5,4,3,2,1,0:T(8,128)(2,1)S(1)}, bf16[1,18,1,2,8,128]{5,4,3,2,1,0:T(8,128)(2,1)S(1)}, u32[]{:S(2)}, u32[]{:S(2)}) collective-permute-start(bf16[1,18,1,2,8,128]{5,4,3,2,1,0:T(8,128)(2,1)S(1)} %get-tuple-element.324), channel_id=1, source_target_pairs={{1,0},{2,1},{3,2},{4,3},{5,4},{6,5},{7,6},{8,7},{9,8},{10,9},{11,1... | collective-permute-start | bytes 221192 | tf_op jit(solution)/shard_map/ppermute | solution.py:19
  50.3 15.3 %copy-start.4 = (bf16[8,8,2,8,128]{4,3,2,1,0:T(8,128)(2,1)S(1)}, bf16[8,8,2,8,128]{4,3,2,1,0:T(8,128)(2,1)}, u32[]{:S(2)}) copy-start(bf16[8,8,2,8,128]{4,3,2,1,0:T(8,128)(2,1)} %get-tuple-element.659) | copy-start | bytes 786436 | tf_op jit(solution)/shard_map/while
  65.6 3.0 copy-start.18
  68.6 3.6 copy-start.6
  72.2 0.7 copy-start.7
  88.5 15.3 %copy-start.3 = (bf16[8,8,2,8,128]{4,3,2,1,0:T(8,128)(2,1)S(1)}, bf16[8,8,2,8,128]{4,3,2,1,0:T(8,128)(2,1)}, u32[]{:S(2)}) copy-start(bf16[8,8,2,8,128]{4,3,2,1,0:T(8,128)(2,1)} %get-tuple-element.695) | copy-start | bytes 786436 | tf_op jit(solution)/shard_map/while
  103.8 3.0 copy-start.17
  106.8 3.6 copy-start.9
  110.4 0.7 copy-start.10
  112.5 37.7 %copy-start = (bf16[10,10,3,8,128]{4,3,2,1,0:T(8,128)(2,1)S(1)}, bf16[10,10,3,8,128]{4,3,2,1,0:T(8,128)(2,1)}, u32[]{:S(2)}) copy-start(bf16[10,10,3,8,128]{4,3,2,1,0:T(8,128)(2,1)} %get-tuple-element.740) | copy-start | bytes 1843204
  112.5 37.8 %copy-start.20 = (s32[2,27]{1,0:T(2,128)S(1)}, s32[2,27]{1,0:T(2,128)}, u32[]{:S(2)}) copy-start(s32[2,27]{1,0:T(2,128)} %get-tuple-element.739) | copy-start | bytes 652
  126.9 15.3 %copy-start.2 = (bf16[8,8,2,8,128]{4,3,2,1,0:T(8,128)(2,1)S(1)}, bf16[8,8,2,8,128]{4,3,2,1,0:T(8,128)(2,1)}, u32[]{:S(2)}) copy-start(bf16[8,8,2,8,128]{4,3,2,1,0:T(8,128)(2,1)} %get-tuple-element.731) | copy-start | bytes 786436 | tf_op jit(solution)/shard_map/while
  142.2 3.0 copy-start.16
  145.2 3.6 copy-start.12
  148.8 0.7 copy-start.13
  164.6 15.3 %copy-start.1 = (bf16[8,8,2,8,128]{4,3,2,1,0:T(8,128)(2,1)S(1)}, bf16[8,8,2,8,128]{4,3,2,1,0:T(8,128)(2,1)}, u32[]{:S(2)}) copy-start(bf16[8,8,2,8,128]{4,3,2,1,0:T(8,128)(2,1)} %get-tuple-element.767) | copy-start | bytes 786436 | tf_op jit(solution)/shard_map/while
  179.9 3.0 copy-start.15
  187.1 1.4 copy-start.8
  187.1 1.4 copy-start.11
  187.1 1.4 copy-start.14
Sparse Core Ops, SparseCore 0:
  188.6 299.7 all-reduce.2
where the time goes:
time: 502 us
  waiting for transfers between devices  302 us (60%)
  local copies, waits for them, and re-layouts  81.4 us (16%)
  other arithmetic  62.7 us (12%)
  matrix products  25.1 us (5%)
  between operations  14.2 us (3%)
  starting transfers between devices  10.2 us (2%)
  loops' own time  6.67 us (1%)
    psum x1, waiting for transfers between devices, reduce_kernel(): summed = lax.psum(flat_terms, ('dcn', 'gx', 'gy'))  299 us
    while x68, other arithmetic  51.2 us
    while x64, local copies, waits for them, and re-layouts  26.7 us
    gather x12, local copies, waits for them, and re-layouts, leaf_columns(): planes.append(padded[rows_x, rows_y, chosen_slot])  20 us
    gather x24, local copies, waits for them, and re-layouts, leaf_columns(): chosen_slot = jnp.take(adjacent_row, base_index + layer)  15.7 us
    dot_general x4, matrix products, grad_update(): jnp.dot(columns, wrows, preferred_element_type=jnp.float32)  13.3 us
    dot_general x4, matrix products, kernel_update(): jnp.dot(own.T, columns, preferred_element_type=jnp.float32)  11.9 us
  transfers between devices with their start and end apart: 5, of which 2 were waited for; matrix products, arithmetic and copies ran while one was open for 1% of the time, Pallas kernels for 0%

commit v1 on v0

v1 whole, which is shorter than its diff:
```python
import math

import jax
import jax.numpy as jnp
from jax import lax
from jax.experimental import pallas as pl
from jax.experimental.pallas import tpu as pltpu
from jax.sharding import PartitionSpec as P

EDGE = 8
WIDTH = 128
VIEW = EDGE + 2
ROWS = 2 * EDGE
UNIT = EDGE * EDGE * ROWS


def conv_kernel(nbr, lz, grad, feat, keep, top, bottom, left, right, wrows, out, kgrad, field, view, own, acc):
    nx, ny = grad.shape[0], grad.shape[1]
    zero_y = jnp.zeros((ny + 2, EDGE, WIDTH), jnp.float32)

    def fill(x, carry):
        field[x + 1, 1 : ny + 1, 0:2] = grad[x].astype(jnp.float32) * keep[x].astype(jnp.float32)
        return carry

    lax.fori_loop(0, nx, fill, 0)
    field[0, 1 : ny + 1, 0:2] = top[0].astype(jnp.float32)
    field[nx + 1, 1 : ny + 1, 0:2] = bottom[0].astype(jnp.float32)

    def sides(x, carry):
        field[x, 0, 0:2] = left[x, 0].astype(jnp.float32)
        field[x, ny + 1, 0:2] = right[x, 0].astype(jnp.float32)
        field[x, :, 2] = zero_y
        return carry

    lax.fori_loop(0, nx + 2, sides, 0)
    kgrad[...] = jnp.zeros_like(kgrad)

    def view_rows(i, slot, xl, p):
        spot_x = EDGE * i + xl
        for q, (start, count) in enumerate(((0, 1), (1, EDGE), (EDGE + 1, 1))):
            parts = ([], [], [])
            row = lax.broadcasted_iota(jnp.int32, (count, EDGE, WIDTH), 1)
            for j in range(2):
                base = ((i * 2 + j) * 2 + slot) * 27 + 9 * p + 3 * q
                span = pl.ds(EDGE * j + start, count)
                below = field[spot_x, span, nbr[base]]
                here = field[spot_x, span, nbr[base + 1]]
                above = field[spot_x, span, nbr[base + 2]]
                parts[0].append(pltpu.roll(jnp.where(row == 0, above, here), EDGE - 1, 1))
                parts[1].append(here)
                parts[2].append(pltpu.roll(jnp.where(row == EDGE - 1, below, here), 1, 1))
            for c in range(3):
                view[c, xl, start : start + count] = jnp.concatenate(parts[c], axis=1).astype(jnp.bfloat16)

    def unit(step, carry):
        i = step // 2
        slot = step % 2
        live = jnp.logical_or(lz[i * 4 + slot] >= 0, lz[i * 4 + 2 + slot] >= 0)

        @pl.when(live)
        def _():
            view_rows(i, slot, 0, 0)

            def middle(xl, c2):
                view_rows(i, slot, xl, 1)
                return c2

            lax.fori_loop(1, EDGE + 1, middle, 0)
            view_rows(i, slot, EDGE + 1, 2)

            def own_rows(xl, c2):
                x = EDGE * i + xl
                pair = [
                    feat[x, EDGE * j : EDGE * j + EDGE, slot].astype(jnp.float32)
                    * keep[x, EDGE * j : EDGE * j + EDGE, slot].astype(jnp.float32)
                    for j in range(2)
                ]
                own[xl] = jnp.concatenate(pair, axis=1).astype(jnp.bfloat16).reshape(EDGE * ROWS, WIDTH)
                return c2

            lax.fori_loop(0, EDGE, own_rows, 0)
            own_t = own[...].reshape(UNIT, WIDTH).T
            acc[...] = jnp.zeros_like(acc)

            def offset(t, c2):
                a = t // 3
                b = t % 3
                pieces = [
                    view[c, pl.ds(2 - a, EDGE), pl.ds(2 - b, EDGE)].reshape(UNIT, WIDTH) for c in range(3)
                ]
                columns = jnp.concatenate(pieces, axis=1)
                weights = wrows[pl.ds(pl.multiple_of(t * 3 * WIDTH, 3 * WIDTH), 3 * WIDTH), :]
                acc[...] += jnp.dot(columns, weights, preferred_element_type=jnp.float32)
                terms = jnp.dot(own_t, columns, preferred_element_type=jnp.float32)
                for c in range(3):
                    kgrad[3 * t + c] += terms[:, c * WIDTH : (c + 1) * WIDTH]
                return c2

            lax.fori_loop(0, 9, offset, 0)

            def emit(xl, c2):
                x = EDGE * i + xl
                block = acc[pl.ds(pl.multiple_of(xl * EDGE * ROWS, EDGE * ROWS), EDGE * ROWS), :]
                block = block.reshape(EDGE, 2, EDGE, WIDTH)
                for j in range(2):
                    k = keep[x, EDGE * j : EDGE * j + EDGE, slot].astype(jnp.float32)
                    out[x, EDGE * j : EDGE * j + EDGE, slot] = (block[:, j] * k).astype(jnp.bfloat16)
                return c2

            lax.fori_loop(0, EDGE, emit, 0)

        @pl.when(jnp.logical_not(live))
        def _():
            def blank(xl, c2):
                out[EDGE * i + xl, :, slot] = jnp.zeros((ny, EDGE, WIDTH), jnp.bfloat16)
                return c2

            lax.fori_loop(0, EDGE, blank, 0)

        return carry

    lax.fori_loop(0, 4, unit, 0)


def exchange(blocks, axis):
    return lax.all_to_all(blocks, axis, 0, 0)


def spread(block, axis):
    count = lax.axis_size(axis)
    return exchange(jnp.broadcast_to(block[None], (count,) + block.shape), axis)


def reduce_terms(terms, scale):
    cores = lax.axis_size("dcn")
    wide = lax.axis_size("gy")
    rows = terms.shape[0]
    half = jnp.sum(exchange(terms.reshape(cores, rows // cores, WIDTH), "dcn"), axis=0)
    piece = jnp.sum(exchange(half.reshape(wide, rows // cores // wide, WIDTH), "gy"), axis=0)
    total = jnp.sum(spread(piece, "gx"), axis=0) * scale
    half = spread(total, "gy").reshape(rows // cores, WIDTH)
    return spread(half, "dcn").reshape(rows, WIDTH)


def local(features, grad_out, occupancy, leaf_z, neighbours, kernel):
    nx, ny = grad_out.shape[1], grad_out.shape[2]
    cols_x, cols_y = leaf_z.shape[1], leaf_z.shape[2]
    grad = grad_out[0]
    feat = features[0]
    active = (leaf_z[0] >= 0).astype(jnp.int32)
    active_vox = jnp.repeat(jnp.repeat(active, EDGE, axis=0), EDGE, axis=1)
    keep = (occupancy[0] * active_vox[..., None]).astype(jnp.bfloat16)
    keep = jnp.broadcast_to(keep[..., None], grad.shape)

    def shift(block, axis, step):
        count = lax.axis_size(axis)
        pairs = [(i, i + step) for i in range(count) if 0 <= i + step < count]
        return lax.ppermute(block, axis, pairs)

    top = shift(grad[nx - 1 :] * keep[nx - 1 :], "gx", 1)
    bottom = shift(grad[:1] * keep[:1], "gx", -1)

    def side(y):
        return jnp.concatenate(
            [top[:, y : y + 1], grad[:, y : y + 1] * keep[:, y : y + 1], bottom[:, y : y + 1]], axis=0
        )

    left = shift(side(ny - 1), "gy", 1)
    right = shift(side(0), "gy", -1)
    wrows = jnp.transpose(kernel, (0, 2, 1)).reshape(27 * WIDTH, WIDTH)
    scale = 1.0 / math.sqrt(
        lax.axis_size("dcn") * lax.axis_size("gx") * lax.axis_size("gy") * nx * ny * 2 * EDGE
    )
    smem = pl.BlockSpec(memory_space=pltpu.SMEM)
    vmem = pl.BlockSpec(memory_space=pltpu.VMEM)
    out, terms = pl.pallas_call(
        conv_kernel,
        out_shape=(
            jax.ShapeDtypeStruct(grad.shape, jnp.bfloat16),
            jax.ShapeDtypeStruct((27, WIDTH, WIDTH), jnp.float32),
        ),
        in_specs=[smem, smem] + [vmem] * 8,
        out_specs=(vmem, vmem),
        scratch_shapes=[
            pltpu.VMEM((nx + 2, ny + 2, 3, EDGE, WIDTH), jnp.float32),
            pltpu.VMEM((3, VIEW, VIEW, ROWS, WIDTH), jnp.bfloat16),
            pltpu.VMEM((EDGE, EDGE * ROWS, WIDTH), jnp.bfloat16),
            pltpu.VMEM((UNIT, WIDTH), jnp.float32),
        ],
        compiler_params=pltpu.CompilerParams(vmem_limit_bytes=40 << 20),
        name="conv_backward",
    )(
        neighbours.reshape(-1),
        leaf_z.reshape(-1),
        grad,
        feat,
        keep,
        top,
        bottom,
        left,
        right,
        wrows,
    )
    kernel_grad = reduce_terms(terms.reshape(27 * WIDTH, WIDTH), scale)
    return out[None], kernel_grad.reshape(27, WIDTH, WIDTH)


def solution(mesh):
    return jax.shard_map(
        local,
        mesh=mesh,
        in_specs=(
            P("dcn", "gx", "gy", None, None, None),
            P("dcn", "gx", "gy", None, None, None),
            P("dcn", "gx", "gy", None, None),
            P("dcn", "gx", "gy", None),
            P("dcn", "gx", "gy", None, None),
            P(),
        ),
        out_specs=(P("dcn", "gx", "gy", None, None, None), P()),
        check_vma=False,
    )
```

time: 502 us -> 114 us (0.23)
  waiting for transfers between devices: 302 us -> 1.47 us
  blocking collectives: 0 us -> 77.2 us
  local copies, waits for them, and re-layouts: 81.4 us -> 6.2 us
  other arithmetic: 62.7 us -> 3.99 us
  matrix products: 25.1 us -> 0 us
  between operations: 14.2 us -> 0.91 us
  Pallas kernels: 0 us -> 12.7 us
  loops' own time: 6.67 us -> 0 us
    psum x1 -> x0, waiting for transfers between devices: 299 us -> none  [reduce_kernel(): summed = lax.psum(flat_terms, ('dcn', 'gx', 'gy'))]
    all_to_all x0 -> x5, blocking collectives: none -> 77.2 us  [exchange(): return lax.all_to_all(blocks, axis, 0, 0)]
    while x68 -> x0, other arithmetic: 51.2 us -> none
    gather x36 -> x0, local copies, waits for them, and re-layouts: 35.7 us -> none  [the longest x12 20 us: leaf_columns(): planes.append(padded[rows_x, rows_y, chosen_slot])]
    while x64 -> x0, local copies, waits for them, and re-layouts: 26.7 us -> none
    dot_general x8 -> x0, matrix products: 25.1 us -> none  [the longest x4 13.3 us: grad_update(): jnp.dot(columns, wrows, preferred_element_type=jnp.float32)]
    pallas_call x0 -> x1, Pallas kernels: none -> 12.7 us  [local(): pl.pallas_call(conv_kernel, out_shape=(jax.ShapeDtypeStruct(grad.shape, j...]
    another operation x4 -> x0, loops' own time: 6.67 us -> none  [local(): lax.fori_loop(0, leaf_total, joint_step, (grad_start, kernel_acc))]
  transfers between devices with their start and end apart: 5 -> 4, of which waited for: 2 -> 1; matrix products, arithmetic and copies ran while one was open for 1% -> 4% of each run, Pallas kernels for 0% -> 0%
where the time goes in v1:
time: 114 us; the launch traced here: 113 us
  blocking collectives  77.2 us (68%)
  Pallas kernels  12.7 us (11%)
  starting transfers between devices  10.9 us (10%)
  local copies, waits for them, and re-layouts  6.2 us (5%)
  other arithmetic  3.99 us (4%)
  waiting for transfers between devices  1.47 us (1%)
    all_to_all x5, blocking collectives, exchange(): return lax.all_to_all(blocks, axis, 0, 0)  77.2 us
    pallas_call x1, Pallas kernels, local(): pl.pallas_call(conv_kernel, out_shape=(jax.ShapeDtypeStruct(grad.shape, j...  12.7 us
    ppermute x4, starting transfers between devices, shift(): return lax.ppermute(block, axis, pairs)  10.9 us
  transfers between devices with their start and end apart: 4, of which 1 were waited for; matrix products, arithmetic and copies ran while one was open for 4% of the time, Pallas kernels for 0%

profile of v1, /device:TPU:1, one launch (start us, length us, event | category | flops | bytes accessed | tf_op | source)
XLA Modules:
  0.0 113.4 jit_solution(1098423949597209443)
XLA Ops:
  0.6 0.0 copy-start.2
  0.6 0.0 copy-start.3
  0.6 0.7 fusion.2
  1.4 0.1 copy.37
  1.5 0.1 broadcast_in_dim.46
  1.6 0.1 reshape.79
  1.7 0.1 copy.41
  1.7 0.9 fusion
  2.7 0.1 copy.43
  2.8 0.1 copy.42
  2.9 1.0 bitcast_multiply_fusion.2
  3.9 1.3 %collective-permute-start.1 = (bf16[1,16,2,8,128]{4,3,2,1,0:T(8,128)(2,1)S(1)}, bf16[1,16,2,8,128]{4,3,2,1,0:T(8,128)(2,1)S(1)}, u32[]{:S(2)}, u32[]{:S(2)}) collective-permute-start(bf16[1,16,2,8,128]{4,3,2,1,0:T(8,128)(2,1)S(1)} %get-tuple-element.8), channel_id=1, source_target_pairs={{16,0},{32,16},{48,32},{64,48},{80,64},{96,80},{112,96},{17,1},{33... | collective-permute-start | bytes 196616 | tf_op jit(solution)/shard_map/ppermute | solution.py:158
  5.2 5.0 %collective-permute-start = (bf16[1,16,2,8,128]{4,3,2,1,0:T(8,128)(2,1)S(1)}, bf16[1,16,2,8,128]{4,3,2,1,0:T(8,128)(2,1)S(1)}, u32[]{:S(2)}, u32[]{:S(2)}) collective-permute-start(bf16[1,16,2,8,128]{4,3,2,1,0:T(8,128)(2,1)S(1)} %get-tuple-element.9), channel_id=1, source_target_pairs={{0,16},{16,32},{32,48},{48,64},{64,80},{80,96},{96,112},{1,17},{17... | collective-permute-start | bytes 196616 | tf_op jit(solution)/shard_map/ppermute | solution.py:158
  10.2 1.0 copy.36
  11.3 0.1 copy.45
  11.3 0.1 copy.44
  11.4 1.0 slice_multiply_fusion
  12.4 0.0 copy-start
  12.5 0.0 copy-start.1
  12.5 0.0 collective-permute-done.1.bottom
  12.5 0.0 collective-permute-done.top
  12.5 3.3 %collective-permute-start.2 = (bf16[18,1,2,8,128]{4,3,2,1,0:T(8,128)(2,1)S(1)}, bf16[18,1,2,8,128]{4,3,2,1,0:T(8,128)(2,1)S(1)}, u32[]{:S(2)}, u32[]{:S(2)}) collective-permute-start(bf16[18,1,2,8,128]{4,3,2,1,0:T(8,128)(2,1)S(1)} %pad_maximum_fusion), channel_id=1, source_target_pairs={{0,1},{1,2},{2,3},{3,4},{4,5},{5,6},{6,7},{7,8},{8,9},{9,10},{10,1... | collective-permute-start | bytes 221192 | tf_op jit(solution)/shard_map/ppermute | solution.py:158
  15.9 1.3 %collective-permute-start.3 = (bf16[18,1,2,8,128]{4,3,2,1,0:T(8,128)(2,1)S(1)}, bf16[18,1,2,8,128]{4,3,2,1,0:T(8,128)(2,1)S(1)}, u32[]{:S(2)}, u32[]{:S(2)}) collective-permute-start(bf16[18,1,2,8,128]{4,3,2,1,0:T(8,128)(2,1)S(1)} %pad_maximum_fusion.1), channel_id=1, source_target_pairs={{1,0},{2,1},{3,2},{4,3},{5,4},{6,5},{7,6},{8,7},{9,8},{10,9},{11,1... | collective-permute-start | bytes 221192 | tf_op jit(solution)/shard_map/ppermute | solution.py:158
  17.2 0.0 copy-done.2
  17.2 0.1 reshape.78.lz
  17.3 0.2 copy.40
  17.5 0.0 copy-done.3
  17.5 0.1 reshape.77.nbr
  17.6 1.9 %copy.46 = bf16[27,128,128]{2,1,0:T(8,128)(2,1)S(1)} copy(bf16[27,128,128]{1,2,0:T(8,128)(2,1)} %bitcast.39) | data formatting | bytes 1769472 | tf_op jit(solution)/shard_map/transpose | solution.py:170
  19.5 0.0 collective-permute-done.2.left
  19.5 1.5 %collective-permute-done.3.right = bf16[18,1,2,8,128]{4,3,2,1,0:T(8,128)(2,1)S(1)} collective-permute-done((bf16[18,1,2,8,128]{4,3,2,1,0:T(8,128)(2,1)S(1)}, bf16[18,1,2,8,128]{4,3,2,1,0:T(8,128)(2,1)S(1)}, u32[]{:S(2)}, u32[]{:S(2)}) %collective-permute-start.3) | collective-permute-done | bytes 73760 | tf_op jit(solution)/shard_map/ppermute | solution.py:158
  21.0 0.6 broadcast_in_dim.48.keep
  21.6 0.0 copy-done
  21.6 0.0 copy-done.1
  21.6 12.7 %conv_backward.1 = (bf16[16,16,2,8,128]{4,3,2,1,0:T(8,128)(2,1)}, f32[27,128,128]{2,1,0:T(8,128)S(1)}) custom-call(s32[216]{0:T(256)S(1)} %reshape.77.nbr, s32[8]{0:T(128)S(1)} %reshape.78.lz, bf16[16,16,2,8,128]{4,3,2,1,0:T(8,128)(2,1)S(1)} %bitcast.36, bf16[16,16,2,8,128]{4,3,2,1,0:T(8,128)(2,1)S(1)} %bitcast.37, ...), custom_call_target="tpu_custom_call" | custom-call | tf_op jit(solution)/shard_map/conv_backward/pallas_call | solution.py:176
  34.4 7.3 %all_to_all.25 = f32[2,1728,128]{2,1,0:T(8,128)S(1)} all-to-all(f32[2,1728,128]{2,1,0:T(8,128)S(1)} %bitcast.34), channel_id=1, replica_groups=mesh['dcn'=2,'gx'=8,'gy'=16] {'dcn'}, dimensions={0} | all-to-all | bytes 3538944 | tf_op jit(solution)/shard_map/all_to_all | solution.py:126
  41.6 0.2 reduce_sum.27
  41.8 0.1 reshape.81
  41.9 21.8 %all_to_all.26 = f32[16,108,128]{2,1,0:T(8,128)S(1)} all-to-all(f32[16,108,128]{2,1,0:T(8,128)S(1)} %reshape.81), channel_id=1, replica_groups=mesh['dcn'=2,'gx'=8,'gy'=16] {'gy'}, dimensions={0} | all-to-all | bytes 1769472 | tf_op jit(solution)/shard_map/all_to_all | solution.py:126
  63.7 0.1 reduce_sum.28
  63.8 21.7 %all_to_all.27 = f32[8,108,128]{2,1,0:T(8,128)S(1)} all-to-all(f32[8,108,128]{2,1,0:T(8,128)S(1)} %broadcast_in_dim.56), channel_id=1, replica_groups=mesh['dcn'=2,'gx'=8,'gy'=16] {'gx'}, dimensions={0} | all-to-all | bytes 884736 | tf_op jit(solution)/shard_map/all_to_all | solution.py:126
  85.6 0.1 broadcast_in_dim.57
  85.7 17.3 %all_to_all.28 = f32[16,108,128]{2,1,0:T(8,128)S(1)} all-to-all(f32[16,108,128]{2,1,0:T(8,128)S(1)} %broadcast_in_dim.57), channel_id=1, replica_groups=mesh['dcn'=2,'gx'=8,'gy'=16] {'gy'}, dimensions={0} | all-to-all | bytes 1769472 | tf_op jit(solution)/shard_map/all_to_all | solution.py:126
  103.0 0.1 broadcast_in_dim.58
  103.0 0.1 broadcast_in_dim.59
  103.2 9.1 %all_to_all.29 = f32[2,1728,128]{2,1,0:T(8,128)S(1)} all-to-all(f32[2,1728,128]{2,1,0:T(8,128)S(1)} %broadcast_in_dim.59), channel_id=1, replica_groups=mesh['dcn'=2,'gx'=8,'gy'=16] {'dcn'}, dimensions={0} | all-to-all | bytes 3538944 | tf_op jit(solution)/shard_map/all_to_all | solution.py:126
  112.2 1.2 %copy.50 = f32[27,128,128]{2,1,0:T(8,128)} copy(f32[27,128,128]{2,1,0:T(8,128)S(1)} %bitcast.38) | data formatting | bytes 3538944
  (13 shorter events, 0.1 us)
Async XLA Ops:
  0.6 16.6 %copy-start.2 = (s32[1,2,2,2]{3,2,1,0:T(2,128)S(1)}, s32[1,2,2,2]{3,2,1,0:T(2,128)}, u32[]{:S(2)}) copy-start(s32[1,2,2,2]{3,2,1,0:T(2,128)} %param.9) | copy-start | bytes 100
  0.6 16.9 %copy-start.3 = (s32[1,2,2,2,27]{4,3,2,1,0:T(2,128)S(1)}, s32[1,2,2,2,27]{4,3,2,1,0:T(2,128)}, u32[]{:S(2)}) copy-start(s32[1,2,2,2,27]{4,3,2,1,0:T(2,128)} %param.10) | copy-start | bytes 2596
  3.9 8.6 %collective-permute-start.1 = (bf16[1,16,2,8,128]{4,3,2,1,0:T(8,128)(2,1)S(1)}, bf16[1,16,2,8,128]{4,3,2,1,0:T(8,128)(2,1)S(1)}, u32[]{:S(2)}, u32[]{:S(2)}) collective-permute-start(bf16[1,16,2,8,128]{4,3,2,1,0:T(8,128)(2,1)S(1)} %get-tuple-element.8), channel_id=1, source_target_pairs={{16,0},{32,16},{48,32},{64,48},{80,64},{96,80},{112,96},{17,1},{33... | collective-permute-start | bytes 196616 | tf_op jit(solution)/shard_map/ppermute | solution.py:158
  5.2 7.3 %collective-permute-start = (bf16[1,16,2,8,128]{4,3,2,1,0:T(8,128)(2,1)S(1)}, bf16[1,16,2,8,128]{4,3,2,1,0:T(8,128)(2,1)S(1)}, u32[]{:S(2)}, u32[]{:S(2)}) collective-permute-start(bf16[1,16,2,8,128]{4,3,2,1,0:T(8,128)(2,1)S(1)} %get-tuple-element.9), channel_id=1, source_target_pairs={{0,16},{16,32},{32,48},{48,64},{64,80},{80,96},{96,112},{1,17},{17... | collective-permute-start | bytes 196616 | tf_op jit(solution)/shard_map/ppermute | solution.py:158
  12.4 9.2 %copy-start = (bf16[1,16,16,2,8,128]{5,4,3,2,1,0:T(8,128)(2,1)S(1)}, bf16[1,16,16,2,8,128]{5,4,3,2,1,0:T(8,128)(2,1)}, u32[]{:S(2)}) copy-start(bf16[1,16,16,2,8,128]{5,4,3,2,1,0:T(8,128)(2,1)} %param.7) | copy-start | bytes 3145732
  12.5 9.2 %copy-start.1 = (bf16[1,16,16,2,8,128]{5,4,3,2,1,0:T(8,128)(2,1)S(1)}, bf16[1,16,16,2,8,128]{5,4,3,2,1,0:T(8,128)(2,1)}, u32[]{:S(2)}) copy-start(bf16[1,16,16,2,8,128]{5,4,3,2,1,0:T(8,128)(2,1)} %param.6) | copy-start | bytes 3145732
  12.5 7.0 %collective-permute-start.2 = (bf16[18,1,2,8,128]{4,3,2,1,0:T(8,128)(2,1)S(1)}, bf16[18,1,2,8,128]{4,3,2,1,0:T(8,128)(2,1)S(1)}, u32[]{:S(2)}, u32[]{:S(2)}) collective-permute-start(bf16[18,1,2,8,128]{4,3,2,1,0:T(8,128)(2,1)S(1)} %pad_maximum_fusion), channel_id=1, source_target_pairs={{0,1},{1,2},{2,3},{3,4},{4,5},{5,6},{6,7},{7,8},{8,9},{9,10},{10,1... | collective-permute-start | bytes 221192 | tf_op jit(solution)/shard_map/ppermute | solution.py:158
  15.9 5.1 %collective-permute-start.3 = (bf16[18,1,2,8,128]{4,3,2,1,0:T(8,128)(2,1)S(1)}, bf16[18,1,2,8,128]{4,3,2,1,0:T(8,128)(2,1)S(1)}, u32[]{:S(2)}, u32[]{:S(2)}) collective-permute-start(bf16[18,1,2,8,128]{4,3,2,1,0:T(8,128)(2,1)S(1)} %pad_maximum_fusion.1), channel_id=1, source_target_pairs={{1,0},{2,1},{3,2},{4,3},{5,4},{6,5},{7,6},{8,7},{9,8},{10,9},{11,1... | collective-permute-start | bytes 221192 | tf_op jit(solution)/shard_map/ppermute | solution.py:158

commit v2 on v1

--- a/solution.py
+++ b/solution.py
@@ -12,9 +12,11 @@
 VIEW = EDGE + 2
 ROWS = 2 * EDGE
 UNIT = EDGE * EDGE * ROWS
-
-
-def conv_kernel(nbr, lz, grad, feat, keep, top, bottom, left, right, wrows, out, kgrad, field, view, own, acc):
+HALF = 27 * WIDTH // 2
+PADDED = 1792
+
+
+def fill_field(grad, keep, top, bottom, left, right, field):
     nx, ny = grad.shape[0], grad.shape[1]
     zero_y = jnp.zeros((ny + 2, EDGE, WIDTH), jnp.float32)
 
@@ -33,9 +35,10 @@
         return carry
 
     lax.fori_loop(0, nx + 2, sides, 0)
-    kgrad[...] = jnp.zeros_like(kgrad)
-
-    def view_rows(i, slot, xl, p):
+
+
+def fill_view(nbr, field, view, i, slot):
+    def view_rows(xl, p):
         spot_x = EDGE * i + xl
         for q, (start, count) in enumerate(((0, 1), (1, EDGE), (EDGE + 1, 1))):
             parts = ([], [], [])
@@ -52,21 +55,38 @@
             for c in range(3):
                 view[c, xl, start : start + count] = jnp.concatenate(parts[c], axis=1).astype(jnp.bfloat16)
 
+    view_rows(0, 0)
+
+    def middle(xl, carry):
+        view_rows(xl, 1)
+        return carry
+
+    lax.fori_loop(1, EDGE + 1, middle, 0)
+    view_rows(EDGE + 1, 2)
+
+
+def columns_at(view, t):
+    a = t // 3
+    b = t % 3
+    pieces = [view[c, pl.ds(2 - a, EDGE), pl.ds(2 - b, EDGE)].reshape(UNIT, WIDTH) for c in range(3)]
+    return jnp.concatenate(pieces, axis=1)
+
+
+def pair_live(lz, i, slot):
+    return jnp.logical_or(lz[i * 4 + slot] >= 0, lz[i * 4 + 2 + slot] >= 0)
+
+
+def terms_kernel(nbr, lz, grad, feat, keep, top, bottom, left, right, terms, field, view, own):
+    fill_field(grad, keep, top, bottom, left, right, field)
+    terms[...] = jnp.zeros_like(terms)
+
     def unit(step, carry):
         i = step // 2
         slot = step % 2
-        live = jnp.logical_or(lz[i * 4 + slot] >= 0, lz[i * 4 + 2 + slot] >= 0)
-
-        @pl.when(live)
+
+        @pl.when(pair_live(lz, i, slot))
         def _():
-            view_rows(i, slot, 0, 0)
-
-            def middle(xl, c2):
-                view_rows(i, slot, xl, 1)
-                return c2
-
-            lax.fori_loop(1, EDGE + 1, middle, 0)
-            view_rows(i, slot, EDGE + 1, 2)
+            fill_view(nbr, field, view, i, slot)
 
             def own_rows(xl, c2):
                 x = EDGE * i + xl
@@ -80,20 +100,41 @@
 
             lax.fori_loop(0, EDGE, own_rows, 0)
             own_t = own[...].reshape(UNIT, WIDTH).T
+
+            def offset(t, c2):
+                part = jnp.dot(own_t, columns_at(view, t), preferred_element_type=jnp.float32)
+                for c in range(3):
+                    for s in range(2):
+                        half = 2 * (3 * t + c) + s
+                        core = (half >= 27).astype(jnp.int32)
+                        spot = pl.ds(pl.multiple_of(half * 64 - core * HALF, 64), 64)
+                        terms[core, spot] += part[s * 64 : s * 64 + 64, c * WIDTH : (c + 1) * WIDTH]
+                return c2
+
+            lax.fori_loop(0, 9, offset, 0)
+
+        return carry
+
+    lax.fori_loop(0, 4, unit, 0)
+
+
+def feature_kernel(nbr, lz, grad, keep, top, bottom, left, right, wrows, out, field, view, acc):
+    ny = grad.shape[1]
+    fill_field(grad, keep, top, bottom, left, right, field)
+
+    def unit(step, carry):
+        i = step // 2
+        slot = step % 2
+        live = pair_live(lz, i, slot)
+
+        @pl.when(live)
+        def _():
+            fill_view(nbr, field, view, i, slot)
             acc[...] = jnp.zeros_like(acc)
 
             def offset(t, c2):
-                a = t // 3
-                b = t % 3
-                pieces = [
-                    view[c, pl.ds(2 - a, EDGE), pl.ds(2 - b, EDGE)].reshape(UNIT, WIDTH) for c in range(3)
-                ]
-                columns = jnp.concatenate(pieces, axis=1)
                 weights = wrows[pl.ds(pl.multiple_of(t * 3 * WIDTH, 3 * WIDTH), 3 * WIDTH), :]
-                acc[...] += jnp.dot(columns, weights, preferred_element_type=jnp.float32)
-                terms = jnp.dot(own_t, columns, preferred_element_type=jnp.float32)
-                for c in range(3):
-                    kgrad[3 * t + c] += terms[:, c * WIDTH : (c + 1) * WIDTH]
+                acc[...] += jnp.dot(columns_at(view, t), weights, preferred_element_type=jnp.float32)
                 return c2
 
             lax.fori_loop(0, 9, offset, 0)
@@ -122,29 +163,72 @@
     lax.fori_loop(0, 4, unit, 0)
 
 
+def encode(value, coded, places):
+    rows = value.shape[0]
+    peak = jnp.max(jnp.abs(value), axis=0, keepdims=True)
+    power = jnp.floor(jnp.log2(jnp.maximum(peak, 1e-30)) + 1.001)
+    code = jnp.clip(jnp.round(value * jnp.exp2(15.0 - power)), -32767.0, 32767.0)
+    code = code.astype(jnp.int32).astype(jnp.int16)
+    power = jnp.broadcast_to(power, (EDGE, WIDTH)).astype(jnp.int32).astype(jnp.int16)
+    for place in places:
+        coded[place, 0:rows] = code
+        coded[place, rows : rows + EDGE] = power
+
+
+def decode(coded):
+    rows = coded.shape[0] - EDGE
+    power = coded[rows:].astype(jnp.int32).astype(jnp.float32)[0:1]
+    return coded[:rows].astype(jnp.int32).astype(jnp.float32) * jnp.exp2(power - 15.0)
+
+
+def encode_half_kernel(pair, coded):
+    chunk = coded.shape[1] - EDGE
+    for n in range(coded.shape[0]):
+        spot = slice(n * chunk, n * chunk + chunk)
+        encode(pair[0, spot] + pair[1, spot], coded, (n,))
+
+
+def sum_kernel(scale, coded, again):
+    total = decode(coded[0])
+    for n in range(1, coded.shape[0]):
+        total = total + decode(coded[n])
+    encode(total * scale, again, range(again.shape[0]))
+
+
+def decode_kernel(coded, out):
+    chunk = coded.shape[2] - EDGE
+    for core in range(2):
+        for n in range(coded.shape[1]):
+            rows = min(chunk, HALF - n * chunk)
+            start = core * HALF + n * chunk
+            out[start : start + rows] = decode(coded[core, n])[0:rows]
+
+
+def call(kernel, name, out_shape, scratch=(), scalars=0, flops=0, nbytes=4 << 20):
+    smem = pl.BlockSpec(memory_space=pltpu.SMEM)
+    vmem = pl.BlockSpec(memory_space=pltpu.VMEM)
+
+    def run(*args):
+        return pl.pallas_call(
+            kernel,
+            out_shape=out_shape,
+            in_specs=[smem] * scalars + [vmem] * (len(args) - scalars),
+            out_specs=vmem,
+            scratch_shapes=list(scratch),
+            compiler_params=pltpu.CompilerParams(vmem_limit_bytes=40 << 20),
+            cost_estimate=pl.CostEstimate(flops=flops, bytes_accessed=nbytes, transcendentals=0),
+            name=name,
+        )(*args)
+
+    return run
+
+
 def exchange(blocks, axis):
     return lax.all_to_all(blocks, axis, 0, 0)
 
 
-def spread(block, axis):
-    count = lax.axis_size(axis)
-    return exchange(jnp.broadcast_to(block[None], (count,) + block.shape), axis)
-
-
-def reduce_terms(terms, scale):
-    cores = lax.axis_size("dcn")
-    wide = lax.axis_size("gy")
-    rows = terms.shape[0]
-    half = jnp.sum(exchange(terms.reshape(cores, rows // cores, WIDTH), "dcn"), axis=0)
-    piece = jnp.sum(exchange(half.reshape(wide, rows // cores // wide, WIDTH), "gy"), axis=0)
-    total = jnp.sum(spread(piece, "gx"), axis=0) * scale
-    half = spread(total, "gy").reshape(rows // cores, WIDTH)
-    return spread(half, "dcn").reshape(rows, WIDTH)
-
-
 def local(features, grad_out, occupancy, leaf_z, neighbours, kernel):
     nx, ny = grad_out.shape[1], grad_out.shape[2]
-    cols_x, cols_y = leaf_z.shape[1], leaf_z.shape[2]
     grad = grad_out[0]
     feat = features[0]
     active = (leaf_z[0] >= 0).astype(jnp.int32)
@@ -171,37 +255,49 @@
     scale = 1.0 / math.sqrt(
         lax.axis_size("dcn") * lax.axis_size("gx") * lax.axis_size("gy") * nx * ny * 2 * EDGE
     )
-    smem = pl.BlockSpec(memory_space=pltpu.SMEM)
-    vmem = pl.BlockSpec(memory_space=pltpu.VMEM)
-    out, terms = pl.pallas_call(
-        conv_kernel,
-        out_shape=(
-            jax.ShapeDtypeStruct(grad.shape, jnp.bfloat16),
-            jax.ShapeDtypeStruct((27, WIDTH, WIDTH), jnp.float32),
-        ),
-        in_specs=[smem, smem] + [vmem] * 8,
-        out_specs=(vmem, vmem),
-        scratch_shapes=[
-            pltpu.VMEM((nx + 2, ny + 2, 3, EDGE, WIDTH), jnp.float32),
-            pltpu.VMEM((3, VIEW, VIEW, ROWS, WIDTH), jnp.bfloat16),
-            pltpu.VMEM((EDGE, EDGE * ROWS, WIDTH), jnp.bfloat16),
-            pltpu.VMEM((UNIT, WIDTH), jnp.float32),
-        ],
-        compiler_params=pltpu.CompilerParams(vmem_limit_bytes=40 << 20),
-        name="conv_backward",
-    )(
-        neighbours.reshape(-1),
-        leaf_z.reshape(-1),
-        grad,
-        feat,
-        keep,
-        top,
-        bottom,
-        left,
-        right,
-        wrows,
-    )
-    kernel_grad = reduce_terms(terms.reshape(27 * WIDTH, WIDTH), scale)
+    nbr = neighbours.reshape(-1)
+    lz = leaf_z.reshape(-1)
+    edges = (top, bottom, left, right)
+    field = pltpu.VMEM((nx + 2, ny + 2, 3, EDGE, WIDTH), jnp.float32)
+    view = pltpu.VMEM((3, VIEW, VIEW, ROWS, WIDTH), jnp.bfloat16)
+    own = pltpu.VMEM((EDGE, EDGE * ROWS, WIDTH), jnp.bfloat16)
+    acc = pltpu.VMEM((UNIT, WIDTH), jnp.float32)
+    product = 2 * 4 * 512 * 27 * WIDTH * WIDTH
+
+    terms = call(
+        terms_kernel,
+        "conv_terms",
+        jax.ShapeDtypeStruct((2, PADDED, WIDTH), jnp.float32),
+        (field, view, own),
+        scalars=2,
+        flops=product,
+    )(nbr, lz, grad, feat, keep, *edges)
+    pair = exchange(terms, "dcn")
+    grad_late, pair = lax.optimization_barrier((grad, pair))
+    out = call(
+        feature_kernel,
+        "conv_features",
+        jax.ShapeDtypeStruct(grad.shape, jnp.bfloat16),
+        (field, view, acc),
+        scalars=2,
+        flops=product,
+    )(nbr, lz, grad_late, keep, *edges, wrows)
+
+    gx, gy = lax.axis_size("gx"), lax.axis_size("gy")
+
+    def coded(count):
+        return jax.ShapeDtypeStruct((count, PADDED // gy + EDGE, WIDTH), jnp.int16)
+
+    half = call(encode_half_kernel, "encode_half", coded(gy), nbytes=2 << 20)(pair)
+    half = exchange(half, "gy")
+    piece = call(lambda c, o: sum_kernel(1.0, c, o), "sum_piece", coded(gx), nbytes=1 << 20)(half)
+    piece = exchange(piece, "gx")
+    total = call(lambda c, o: sum_kernel(scale, c, o), "sum_total", coded(gy), nbytes=1 << 20)(piece)
+    total = exchange(total, "gy")
+    total = exchange(jnp.broadcast_to(total[None], (2,) + total.shape), "dcn")
+    kernel_grad = call(
+        decode_kernel, "decode_total", jax.ShapeDtypeStruct((27 * WIDTH, WIDTH), jnp.float32), nbytes=3 << 20
+    )(total)
     return out[None], kernel_grad.reshape(27, WIDTH, WIDTH)
 
 

time: 114 us -> 104 us (0.912); the launches traced: 113 us -> 102 us
  blocking collectives: 77.2 us -> 50.6 us
  Pallas kernels: 12.7 us -> 20.6 us
  starting transfers between devices: 10.9 us -> 14.4 us
  waiting for transfers between devices: 1.47 us -> 4.97 us
    all_to_all x5 -> x4, blocking collectives: 77.2 us -> 50.6 us  [exchange(): return lax.all_to_all(blocks, axis, 0, 0)]
    pallas_call x1 -> x6, Pallas kernels: 12.7 us -> 20.6 us  [run(): pl.pallas_call(kernel, out_shape=out_shape, in_specs=[smem] * scalars + [...]
    all_to_all x0 -> x1, starting transfers between devices: none -> 4.22 us  [exchange(): return lax.all_to_all(blocks, axis, 0, 0)]
    ppermute x4, waiting for transfers between devices: 1.47 us -> 4.97 us  [shift(): return lax.ppermute(block, axis, pairs)]
  transfers between devices with their start and end apart: 4 -> 5, of which waited for: 1 -> 2; matrix products, arithmetic and copies ran while one was open for 4% -> 4% of each run, Pallas kernels for 0% -> 9%
where the time goes in v2:
time: 104 us; the launch traced here: 102 us
  blocking collectives  50.6 us (49%)
  Pallas kernels  20.6 us (20%)
  starting transfers between devices  14.4 us (14%)
  local copies, waits for them, and re-layouts  7.03 us (7%)
  waiting for transfers between devices  4.97 us (5%)
  other arithmetic  3.75 us (4%)
    all_to_all x4, blocking collectives, exchange(): return lax.all_to_all(blocks, axis, 0, 0)  50.6 us
    pallas_call x6, Pallas kernels, run(): pl.pallas_call(kernel, out_shape=out_shape, in_specs=[smem] * scalars + [...  20.6 us
    ppermute x4, starting transfers between devices, shift(): return lax.ppermute(block, axis, pairs)  10.2 us
    ppermute x4, waiting for transfers between devices, shift(): return lax.ppermute(block, axis, pairs)  4.97 us
    all_to_all x1, starting transfers between devices, exchange(): return lax.all_to_all(blocks, axis, 0, 0)  4.22 us
    unnamed x9, local copies, waits for them, and re-layouts  2.26 us
  transfers between devices with their start and end apart: 5, of which 2 were waited for; matrix products, arithmetic and copies ran while one was open for 4% of the time, Pallas kernels for 9%

profile of v2, /device:TPU:1, one launch (start us, length us, event | category | flops | bytes accessed | tf_op | source)
XLA Modules:
  0.0 102.2 jit_solution(3992762168432259800)
XLA Ops:
  0.6 0.0 copy-start.2
  0.6 0.0 copy-start
  0.7 0.0 copy-start.3
  0.7 0.8 fusion.2
  1.4 0.1 copy.15
  1.5 0.1 broadcast_in_dim.33
  1.6 0.1 reshape.75
  1.7 0.1 copy.19
  1.8 0.9 fusion
  2.7 0.1 copy.20
  2.8 0.1 copy.21
  2.9 1.0 bitcast_multiply_fusion.2
  3.9 4.4 %collective-permute-start = (bf16[1,16,2,8,128]{4,3,2,1,0:T(8,128)(2,1)S(1)}, bf16[1,16,2,8,128]{4,3,2,1,0:T(8,128)(2,1)S(1)}, u32[]{:S(2)}, u32[]{:S(2)}) collective-permute-start(bf16[1,16,2,8,128]{4,3,2,1,0:T(8,128)(2,1)S(1)} %get-tuple-element.9), channel_id=1, source_target_pairs={{0,16},{16,32},{32,48},{48,64},{64,80},{80,96},{96,112},{1,17},{17... | collective-permute-start | bytes 196616 | tf_op jit(solution)/shard_map/ppermute | solution.py:242
  8.3 1.3 %collective-permute-start.1 = (bf16[1,16,2,8,128]{4,3,2,1,0:T(8,128)(2,1)S(1)}, bf16[1,16,2,8,128]{4,3,2,1,0:T(8,128)(2,1)S(1)}, u32[]{:S(2)}, u32[]{:S(2)}) collective-permute-start(bf16[1,16,2,8,128]{4,3,2,1,0:T(8,128)(2,1)S(1)} %get-tuple-element.8), channel_id=1, source_target_pairs={{16,0},{32,16},{48,32},{64,48},{80,64},{96,80},{112,96},{17,1},{33... | collective-permute-start | bytes 196616 | tf_op jit(solution)/shard_map/ppermute | solution.py:242
  9.6 1.0 %copy.14 = s32[1,16,16,2,8]{1,4,3,2,0:T(8,128)S(1)} copy(s32[1,16,16,2,8]{2,4,3,1,0:T(8,128)} %param.8) | data formatting | bytes 32768 | tf_op args[2]
  10.7 0.1 copy.22
  10.8 0.1 copy.23
  10.9 1.0 slice_multiply_fusion
  11.9 0.0 collective-permute-done.top
  11.9 1.6 %collective-permute-done.1.bottom = bf16[1,16,2,8,128]{4,3,2,1,0:T(8,128)(2,1)S(1)} collective-permute-done((bf16[1,16,2,8,128]{4,3,2,1,0:T(8,128)(2,1)S(1)}, bf16[1,16,2,8,128]{4,3,2,1,0:T(8,128)(2,1)S(1)}, u32[]{:S(2)}, u32[]{:S(2)}) %collective-permute-start.1) | collective-permute-done | bytes 65568 | tf_op jit(solution)/shard_map/ppermute | solution.py:242
  13.5 3.2 %collective-permute-start.2 = (bf16[18,1,2,8,128]{4,3,2,1,0:T(8,128)(2,1)S(1)}, bf16[18,1,2,8,128]{4,3,2,1,0:T(8,128)(2,1)S(1)}, u32[]{:S(2)}, u32[]{:S(2)}) collective-permute-start(bf16[18,1,2,8,128]{4,3,2,1,0:T(8,128)(2,1)S(1)} %pad_maximum_fusion), channel_id=1, source_target_pairs={{0,1},{1,2},{2,3},{3,4},{4,5},{5,6},{6,7},{7,8},{8,9},{9,10},{10,1... | collective-permute-start | bytes 221192 | tf_op jit(solution)/shard_map/ppermute | solution.py:242
  16.7 1.3 %collective-permute-start.3 = (bf16[18,1,2,8,128]{4,3,2,1,0:T(8,128)(2,1)S(1)}, bf16[18,1,2,8,128]{4,3,2,1,0:T(8,128)(2,1)S(1)}, u32[]{:S(2)}, u32[]{:S(2)}) collective-permute-start(bf16[18,1,2,8,128]{4,3,2,1,0:T(8,128)(2,1)S(1)} %pad_maximum_fusion.1), channel_id=1, source_target_pairs={{1,0},{2,1},{3,2},{4,3},{5,4},{6,5},{7,6},{8,7},{9,8},{10,9},{11,1... | collective-permute-start | bytes 221192 | tf_op jit(solution)/shard_map/ppermute | solution.py:242
  18.0 0.2 copy.18
  18.3 0.0 copy-done.2
  18.3 0.1 reshape.74.lz
  18.4 0.0 copy-done.3
  18.4 0.1 reshape.73.nbr
  18.5 0.0 collective-permute-done.2.left
  18.5 3.4 %collective-permute-done.3.right = bf16[18,1,2,8,128]{4,3,2,1,0:T(8,128)(2,1)S(1)} collective-permute-done((bf16[18,1,2,8,128]{4,3,2,1,0:T(8,128)(2,1)S(1)}, bf16[18,1,2,8,128]{4,3,2,1,0:T(8,128)(2,1)S(1)}, u32[]{:S(2)}, u32[]{:S(2)}) %collective-permute-start.3) | collective-permute-done | bytes 73760 | tf_op jit(solution)/shard_map/ppermute | solution.py:242
  21.8 0.6 broadcast_in_dim.35.keep
  22.4 0.0 copy-done
  22.5 0.0 copy-start.1
  22.5 1.2 %copy-done.1 = bf16[1,16,16,2,8,128]{5,4,3,2,1,0:T(8,128)(2,1)S(1)} copy-done((bf16[1,16,16,2,8,128]{5,4,3,2,1,0:T(8,128)(2,1)S(1)}, bf16[1,16,16,2,8,128]{5,4,3,2,1,0:T(8,128)(2,1)}, u32[]{:S(2)}) %copy-start.1) | copy-done | bytes 1048600
  23.7 8.1 %conv_terms.1 = f32[2,1792,128]{2,1,0:T(8,128)S(1)} custom-call(s32[216]{0:T(256)S(1)} %reshape.73.nbr, s32[8]{0:T(128)S(1)} %reshape.74.lz, bf16[16,16,2,8,128]{4,3,2,1,0:T(8,128)(2,1)S(1)} %bitcast.34, bf16[16,16,2,8,128]{4,3,2,1,0:T(8,128)(2,1)S(1)} %bitcast.36, bf16[16,16,2,8,128]{4,3,2,1,0:T(8,128)(2,1)S(1)} %broadcast_in_dim.35.keep, ...), custom_call_target="tpu_custom_call" | custom-call | flops 1811939328 | bytes 4194304 | tf_op jit(solution)/shard_map/conv_terms/pallas_call | solution.py:212
  31.8 8.2 %all_to_all.25.pair = f32[2,1792,128]{2,1,0:T(8,128)S(1)} all-to-all(f32[2,1792,128]{2,1,0:T(8,128)S(1)} %conv_terms.1), channel_id=1, replica_groups=mesh['dcn'=2,'gx'=8,'gy'=16] {'dcn'}, dimensions={0} | all-to-all | bytes 3670016 | tf_op jit(solution)/shard_map/all_to_all | solution.py:227
  40.0 0.2 encode_half.1
  40.2 17.9 %all_to_all.26.c = s16[16,120,128]{2,1,0:T(8,128)(2,1)S(1)} all-to-all(s16[16,120,128]{2,1,0:T(8,128)(2,1)S(1)} %encode_half.1), channel_id=1, replica_groups=mesh['dcn'=2,'gx'=8,'gy'=16] {'gy'}, dimensions={0} | all-to-all | bytes 983040 | tf_op jit(solution)/shard_map/all_to_all | solution.py:227
  58.1 0.2 sum_piece.1
  58.3 17.1 %all_to_all.27.c = s16[8,120,128]{2,1,0:T(8,128)(2,1)S(1)} all-to-all(s16[8,120,128]{2,1,0:T(8,128)(2,1)S(1)} %sum_piece.1), channel_id=1, replica_groups=mesh['dcn'=2,'gx'=8,'gy'=16] {'gx'}, dimensions={0} | all-to-all | bytes 491520 | tf_op jit(solution)/shard_map/all_to_all | solution.py:227
  75.4 0.9 sum_total.1
  76.3 4.2 %all-to-all-start.3 = ((s16[16,120,128]{2,1,0:T(8,128)(2,1)}), s16[16,120,128]{2,1,0:T(8,128)(2,1)}, u32[]{:S(2)}, u32[]{:S(2)}) async-start(s16[16,120,128]{2,1,0:T(8,128)(2,1)} %sum_total.1), calls=%async_computation.3 | async-start | bytes 983040 | tf_op jit(solution)/shard_map/all_to_all | solution.py:227
  80.6 1.9 %copy.24 = bf16[27,128,128]{2,1,0:T(8,128)(2,1)S(1)} copy(bf16[27,128,128]{1,2,0:T(8,128)(2,1)} %bitcast.38) | data formatting | bytes 1769472 | tf_op jit(solution)/shard_map/transpose | solution.py:254
  82.5 9.7 %conv_features.1 = bf16[16,16,2,8,128]{4,3,2,1,0:T(8,128)(2,1)} custom-call(s32[216]{0:T(256)S(1)} %reshape.73.nbr, s32[8]{0:T(128)S(1)} %reshape.74.lz, bf16[16,16,2,8,128]{4,3,2,1,0:T(8,128)(2,1)S(1)} %bitcast.35, bf16[16,16,2,8,128]{4,3,2,1,0:T(8,128)(2,1)S(1)} %broadcast_in_dim.35.keep, bf16[1,16,2,8,128]{4,3,2,1,0:T(8,128)(2,1)S(1)} %collective-permute-done.top, ...), custom_call_target="tpu_custom_call" | custom-call | flops 1811939328 | bytes 4194304 | tf_op jit(solution)/shard_map/conv_features/pallas_call | solution.py:212
  92.2 0.0 all-to-all-done.3
  92.2 1.2 %broadcast_in_dim.43 = s16[2,16,120,128]{3,2,1,0:T(8,128)(2,1)S(1)} broadcast(s16[16,120,128]{2,1,0:T(8,128)(2,1)} %all-to-all-done.3), dimensions={1,2,3} | broadcast | bytes 1474560 | tf_op jit(solution)/shard_map/broadcast_in_dim | solution.py:297
  93.3 7.5 %all_to_all.28.coded = s16[2,16,120,128]{3,2,1,0:T(8,128)(2,1)S(1)} all-to-all(s16[2,16,120,128]{3,2,1,0:T(8,128)(2,1)S(1)} %broadcast_in_dim.43), channel_id=1, replica_groups=mesh['dcn'=2,'gx'=8,'gy'=16] {'dcn'}, dimensions={0} | all-to-all | bytes 1966080 | tf_op jit(solution)/shard_map/all_to_all | solution.py:227
  100.8 1.4 %decode_total.1 = f32[3456,128]{1,0:T(8,128)} custom-call(s16[2,16,120,128]{3,2,1,0:T(8,128)(2,1)S(1)} %all_to_all.28.coded), custom_call_target="tpu_custom_call" | custom-call | bytes 3145728 | tf_op jit(solution)/shard_map/decode_total/pallas_call | solution.py:212
  (10 shorter events, 0.1 us)
Async XLA Ops:
  0.6 17.7 %copy-start.2 = (s32[1,2,2,2]{3,2,1,0:T(2,128)S(1)}, s32[1,2,2,2]{3,2,1,0:T(2,128)}, u32[]{:S(2)}) copy-start(s32[1,2,2,2]{3,2,1,0:T(2,128)} %param.9) | copy-start | bytes 100
  0.6 21.8 %copy-start = (bf16[1,16,16,2,8,128]{5,4,3,2,1,0:T(8,128)(2,1)S(1)}, bf16[1,16,16,2,8,128]{5,4,3,2,1,0:T(8,128)(2,1)}, u32[]{:S(2)}) copy-start(bf16[1,16,16,2,8,128]{5,4,3,2,1,0:T(8,128)(2,1)} %param.7) | copy-start | bytes 3145732
  0.7 17.7 %copy-start.3 = (s32[1,2,2,2,27]{4,3,2,1,0:T(2,128)S(1)}, s32[1,2,2,2,27]{4,3,2,1,0:T(2,128)}, u32[]{:S(2)}) copy-start(s32[1,2,2,2,27]{4,3,2,1,0:T(2,128)} %param.10) | copy-start | bytes 2596
  3.9 8.0 %collective-permute-start = (bf16[1,16,2,8,128]{4,3,2,1,0:T(8,128)(2,1)S(1)}, bf16[1,16,2,8,128]{4,3,2,1,0:T(8,128)(2,1)S(1)}, u32[]{:S(2)}, u32[]{:S(2)}) collective-permute-start(bf16[1,16,2,8,128]{4,3,2,1,0:T(8,128)(2,1)S(1)} %get-tuple-element.9), channel_id=1, source_target_pairs={{0,16},{16,32},{32,48},{48,64},{64,80},{80,96},{96,112},{1,17},{17... | collective-permute-start | bytes 196616 | tf_op jit(solution)/shard_map/ppermute | solution.py:242
  8.3 5.2 %collective-permute-start.1 = (bf16[1,16,2,8,128]{4,3,2,1,0:T(8,128)(2,1)S(1)}, bf16[1,16,2,8,128]{4,3,2,1,0:T(8,128)(2,1)S(1)}, u32[]{:S(2)}, u32[]{:S(2)}) collective-permute-start(bf16[1,16,2,8,128]{4,3,2,1,0:T(8,128)(2,1)S(1)} %get-tuple-element.8), channel_id=1, source_target_pairs={{16,0},{32,16},{48,32},{64,48},{80,64},{96,80},{112,96},{17,1},{33... | collective-permute-start | bytes 196616 | tf_op jit(solution)/shard_map/ppermute | solution.py:242
  13.5 5.0 %collective-permute-start.2 = (bf16[18,1,2,8,128]{4,3,2,1,0:T(8,128)(2,1)S(1)}, bf16[18,1,2,8,128]{4,3,2,1,0:T(8,128)(2,1)S(1)}, u32[]{:S(2)}, u32[]{:S(2)}) collective-permute-start(bf16[18,1,2,8,128]{4,3,2,1,0:T(8,128)(2,1)S(1)} %pad_maximum_fusion), channel_id=1, source_target_pairs={{0,1},{1,2},{2,3},{3,4},{4,5},{5,6},{6,7},{7,8},{8,9},{9,10},{10,1... | collective-permute-start | bytes 221192 | tf_op jit(solution)/shard_map/ppermute | solution.py:242
  16.7 5.1 %collective-permute-start.3 = (bf16[18,1,2,8,128]{4,3,2,1,0:T(8,128)(2,1)S(1)}, bf16[18,1,2,8,128]{4,3,2,1,0:T(8,128)(2,1)S(1)}, u32[]{:S(2)}, u32[]{:S(2)}) collective-permute-start(bf16[18,1,2,8,128]{4,3,2,1,0:T(8,128)(2,1)S(1)} %pad_maximum_fusion.1), channel_id=1, source_target_pairs={{1,0},{2,1},{3,2},{4,3},{5,4},{6,5},{7,6},{8,7},{9,8},{10,9},{11,1... | collective-permute-start | bytes 221192 | tf_op jit(solution)/shard_map/ppermute | solution.py:242
  22.5 1.2 %copy-start.1 = (bf16[1,16,16,2,8,128]{5,4,3,2,1,0:T(8,128)(2,1)S(1)}, bf16[1,16,16,2,8,128]{5,4,3,2,1,0:T(8,128)(2,1)}, u32[]{:S(2)}) copy-start(bf16[1,16,16,2,8,128]{5,4,3,2,1,0:T(8,128)(2,1)} %param.6) | copy-start | bytes 3145732
  76.3 15.8 %all-to-all-start.3 = ((s16[16,120,128]{2,1,0:T(8,128)(2,1)}), s16[16,120,128]{2,1,0:T(8,128)(2,1)}, u32[]{:S(2)}, u32[]{:S(2)}) async-start(s16[16,120,128]{2,1,0:T(8,128)(2,1)} %sum_total.1), calls=%async_computation.3 | async-start | bytes 983040 | tf_op jit(solution)/shard_map/all_to_all | solution.py:227

commit v3 on v2

v3 whole, which is shorter than its diff:
```python
import math

import jax
import jax.numpy as jnp
from jax import lax
from jax.experimental import pallas as pl
from jax.experimental.pallas import tpu as pltpu
from jax.sharding import PartitionSpec as P

EDGE = 8
WIDTH = 128
VIEW = EDGE + 2
ROWS = 2 * EDGE
UNIT = EDGE * EDGE * ROWS
HALF = 27 * WIDTH // 2
PADDED = 1792


def shifted(below, here, above):
    row = lax.broadcasted_iota(jnp.int32, here.shape, 1)
    return (
        pltpu.roll(jnp.where(row == 0, above, here), EDGE - 1, 1),
        here,
        pltpu.roll(jnp.where(row == EDGE - 1, below, here), 1, 1),
    )


REGIONS = ((0, 1), (1, EDGE), (EDGE + 1, 1))


def table_base(i, j, slot):
    return ((i * 2 + j) * 2 + slot) * 27


def pair_live(lz, i, slot):
    return jnp.logical_or(lz[i * 4 + slot] >= 0, lz[i * 4 + 2 + slot] >= 0)


def fill_field(i, grad, keep, edges, field):
    ny = grad.shape[1]
    low, high = (1, VIEW) if i == 0 else (0, VIEW - 1)

    def fill(r, carry):
        x = EDGE * i - 1 + r
        field[r, 1 : ny + 1, 0:2] = grad[x].astype(jnp.float32) * keep[x].astype(jnp.float32)
        return carry

    lax.fori_loop(low, high, fill, 0)
    outer = 0 if i == 0 else VIEW - 1
    field[:, :, 2] = jnp.zeros((VIEW, ny + 2, EDGE, WIDTH), jnp.float32)
    if edges is None:
        field[outer, :, 0:2] = jnp.zeros((ny + 2, 2, EDGE, WIDTH), jnp.float32)
        field[:, 0, 0:2] = jnp.zeros((VIEW, 2, EDGE, WIDTH), jnp.float32)
        field[:, ny + 1, 0:2] = jnp.zeros((VIEW, 2, EDGE, WIDTH), jnp.float32)
    else:
        top, bottom, left, right = edges
        field[outer, 1 : ny + 1, 0:2] = (top, bottom)[i][0].astype(jnp.float32)
        field[:, 0, 0:2] = left[EDGE * i : EDGE * i + VIEW, 0].astype(jnp.float32)
        field[:, ny + 1, 0:2] = right[EDGE * i : EDGE * i + VIEW, 0].astype(jnp.float32)


def fill_view(nbr, field, view, i, slot):
    def view_rows(xl, p):
        for q, (start, count) in enumerate(REGIONS):
            halves = []
            for j in range(2):
                base = table_base(i, j, slot) + 9 * p + 3 * q
                span = pl.ds(EDGE * j + start, count)
                halves.append(shifted(*(field[xl, span, nbr[base + r]] for r in range(3))))
            for c in range(3):
                both = jnp.concatenate([halves[0][c], halves[1][c]], axis=1)
                view[c, xl, start : start + count] = both.astype(jnp.bfloat16)

    view_rows(0, 0)

    def middle(xl, carry):
        view_rows(xl, 1)
        return carry

    lax.fori_loop(1, EDGE + 1, middle, 0)
    view_rows(EDGE + 1, 2)


def columns_at(view, t):
    a = t // 3
    b = t % 3
    pieces = [view[c, pl.ds(2 - a, EDGE), pl.ds(2 - b, EDGE)].reshape(UNIT, WIDTH) for c in range(3)]
    return jnp.concatenate(pieces, axis=1)


def pair_row(feat, keep, x, slot):
    pair = [
        feat[x, EDGE * j : EDGE * j + EDGE, slot].astype(jnp.float32)
        * keep[x, EDGE * j : EDGE * j + EDGE, slot].astype(jnp.float32)
        for j in range(2)
    ]
    return jnp.concatenate(pair, axis=1).reshape(EDGE * ROWS, WIDTH)


def add_terms(total, first, part):
    for c in range(3):
        for s in range(2):
            half = 2 * (first + c) + s
            if isinstance(half, int):
                core, start = half // 27, half * 64 - half // 27 * HALF
            else:
                core = (half >= 27).astype(jnp.int32)
                start = pl.multiple_of(half * 64 - core * HALF, 64)
            total[core, pl.ds(start, 64)] += part[s * 64 : s * 64 + 64, c * WIDTH : (c + 1) * WIDTH]


def terms_kernel(i, nbr, lz, grad, feat, keep, *refs):
    *before, terms, field, view, own = refs
    fill_field(i, grad, keep, None, field)
    terms[...] = before[0][...] if before else jnp.zeros_like(terms)

    def unit(slot, carry):
        @pl.when(pair_live(lz, i, slot))
        def _():
            fill_view(nbr, field, view, i, slot)

            def own_rows(xl, c2):
                own[xl] = pair_row(feat, keep, EDGE * i + xl, slot).astype(jnp.bfloat16)
                return c2

            lax.fori_loop(0, EDGE, own_rows, 0)
            own_t = own[...].reshape(UNIT, WIDTH).T

            def offset(t, c2):
                part = jnp.dot(own_t, columns_at(view, t), preferred_element_type=jnp.float32)
                add_terms(terms, 3 * t, part)
                return c2

            lax.fori_loop(0, 9, offset, 0)

        return carry

    lax.fori_loop(0, 2, unit, 0)


def edge_kernel(nbr, lz, core, feat, keep, top, bottom, left, right, before, mine, theirs, total, strip, side, row_view, side_view):
    nx, ny = feat.shape[0], feat.shape[1]
    total[...] = before[...]
    for i in range(2):
        spot = (0, nx + 1)[i]
        strip[i, 1 : ny + 1, 0:2] = (top, bottom)[i][0].astype(jnp.float32)
        strip[i, 0, 0:2] = left[spot, 0].astype(jnp.float32)
        strip[i, ny + 1, 0:2] = right[spot, 0].astype(jnp.float32)
        side[i, 1 : nx + 1, 0:2] = (left, right)[i][1 : nx + 1, 0].astype(jnp.float32)
        for end in (0, nx + 1):
            side[i, end, 0:2] = jnp.zeros((2, EDGE, WIDTH), jnp.float32)
    strip[:, :, 2] = jnp.zeros((2, ny + 2, EDGE, WIDTH), jnp.float32)
    side[:, :, 2] = jnp.zeros((2, nx + 2, EDGE, WIDTH), jnp.float32)

    def product(own_t, pieces, first):
        columns = jnp.concatenate(pieces, axis=1).astype(jnp.bfloat16)
        add_terms(total, first, jnp.dot(own_t, columns, preferred_element_type=jnp.float32))

    def unit(i, slot):
        for q, (start, count) in enumerate(REGIONS):
            halves = []
            for j in range(2):
                base = table_base(i, j, slot) + 18 * i + 3 * q
                span = pl.ds(EDGE * j + start, count)
                halves.append(shifted(*(strip[i, span, nbr[base + r]] for r in range(3))))
            for c in range(3):
                both = jnp.concatenate([halves[0][c], halves[1][c]], axis=1)
                row_view[c, start : start + count] = both.astype(jnp.bfloat16)
        own_t = pair_row(feat, keep, (0, nx - 1)[i], slot).T.astype(jnp.bfloat16)
        for b in range(3):
            pieces = [row_view[c, 2 - b : 2 - b + EDGE].reshape(EDGE * ROWS, WIDTH) for c in range(3)]
            product(own_t, pieces, 18 - 18 * i + 3 * b)
        for j in range(2):
            for p, (start, count) in enumerate(REGIONS):
                base = table_base(i, j, slot) + 9 * p + 6 * j
                span = pl.ds(EDGE * i + start, count)
                moved = shifted(*(side[j, span, nbr[base + r]] for r in range(3)))
                for c in range(3):
                    side_view[c, start : start + count] = moved[c]
            spot = (slice(EDGE * i, EDGE * i + EDGE), (0, ny - 1)[j], slot)
            own_t = (feat[spot].astype(jnp.float32) * keep[spot].astype(jnp.float32)).reshape(EDGE * EDGE, WIDTH)
            own_t = own_t.T.astype(jnp.bfloat16)
            for a in range(3):
                pieces = [side_view[c, 2 - a : 2 - a + EDGE].reshape(EDGE * EDGE, WIDTH) for c in range(3)]
                product(own_t, pieces, 9 * a + 6 - 6 * j)

    for i in range(2):

        def slots(slot, carry, i=i):
            @pl.when(pair_live(lz, i, slot))
            def _():
                unit(i, slot)

            return carry

        lax.fori_loop(0, 2, slots, 0)
    here = core[0]
    chunk = theirs.shape[1] - EDGE
    mine[...] = total[here]
    for n in range(theirs.shape[0]):
        encode(total[1 - here, n * chunk : n * chunk + chunk], theirs, (n,))


def feature_kernel(i, nbr, lz, grad, keep, top, bottom, left, right, wrows, *refs):
    out, field, view, acc = refs[-4:]
    ny = grad.shape[1]
    fill_field(i, grad, keep, (top, bottom, left, right), field)

    def unit(slot, carry):
        live = pair_live(lz, i, slot)

        @pl.when(live)
        def _():
            fill_view(nbr, field, view, i, slot)
            acc[...] = jnp.zeros_like(acc)

            def offset(t, c2):
                weights = wrows[pl.ds(pl.multiple_of(t * 3 * WIDTH, 3 * WIDTH), 3 * WIDTH), :]
                acc[...] += jnp.dot(columns_at(view, t), weights, preferred_element_type=jnp.float32)
                return c2

            lax.fori_loop(0, 9, offset, 0)

            def emit(xl, c2):
                x = EDGE * i + xl
                block = acc[pl.ds(pl.multiple_of(xl * EDGE * ROWS, EDGE * ROWS), EDGE * ROWS), :]
                block = block.reshape(EDGE, 2, EDGE, WIDTH)
                for j in range(2):
                    k = keep[x, EDGE * j : EDGE * j + EDGE, slot].astype(jnp.float32)
                    out[xl, EDGE * j : EDGE * j + EDGE, slot] = (block[:, j] * k).astype(jnp.bfloat16)
                return c2

            lax.fori_loop(0, EDGE, emit, 0)

        @pl.when(jnp.logical_not(live))
        def _():
            def blank(xl, c2):
                out[xl, :, slot] = jnp.zeros((ny, EDGE, WIDTH), jnp.bfloat16)
                return c2

            lax.fori_loop(0, EDGE, blank, 0)

        return carry

    lax.fori_loop(0, 2, unit, 0)


def encode(value, coded, places):
    rows = value.shape[0]
    peak = jnp.max(jnp.abs(value), axis=0, keepdims=True)
    power = jnp.floor(jnp.log2(jnp.maximum(peak, 1e-30)) + 1.001)
    code = jnp.clip(jnp.round(value * jnp.exp2(15.0 - power)), -32767.0, 32767.0)
    code = code.astype(jnp.int32).astype(jnp.int16)
    power = jnp.broadcast_to(power, (EDGE, WIDTH)).astype(jnp.int32).astype(jnp.int16)
    for place in places:
        coded[place, 0:rows] = code
        coded[place, rows : rows + EDGE] = power


def decode(coded):
    rows = coded.shape[0] - EDGE
    power = coded[rows:].astype(jnp.int32).astype(jnp.float32)[0:1]
    return coded[:rows].astype(jnp.int32).astype(jnp.float32) * jnp.exp2(power - 15.0)


def encode_half_kernel(mine, theirs, coded):
    chunk = coded.shape[1] - EDGE
    for n in range(coded.shape[0]):
        encode(mine[n * chunk : n * chunk + chunk] + decode(theirs[n]), coded, (n,))


def sum_kernel(scale, coded, again):
    total = decode(coded[0])
    for n in range(1, coded.shape[0]):
        total = total + decode(coded[n])
    encode(total * scale, again, range(again.shape[0]))


def decode_kernel(core, mine, theirs, out):
    chunk = mine.shape[1] - EDGE
    here = core[0]
    for base, coded in ((here * HALF, mine), ((1 - here) * HALF, theirs)):
        for n in range(coded.shape[0]):
            rows = min(chunk, HALF - n * chunk)
            out[pl.ds(pl.multiple_of(base + n * chunk, EDGE), rows)] = decode(coded[n])[0:rows]


SMEM = pl.BlockSpec(memory_space=pltpu.SMEM)
VMEM = pl.BlockSpec(memory_space=pltpu.VMEM)


def call(kernel, name, out_shape, scratch=(), scalars=0, flops=0, nbytes=4 << 20):
    def run(*args):
        return pl.pallas_call(
            kernel,
            out_shape=out_shape,
            in_specs=[SMEM] * scalars + [VMEM] * (len(args) - scalars),
            out_specs=jax.tree.map(lambda _: VMEM, out_shape),
            scratch_shapes=list(scratch),
            compiler_params=pltpu.CompilerParams(vmem_limit_bytes=40 << 20),
            cost_estimate=pl.CostEstimate(flops=flops, bytes_accessed=nbytes, transcendentals=0),
            name=name,
        )(*args)

    return run


def features_call(i, args, scratch, flops, before=None):
    grad = args[2]
    block = (EDGE,) + grad.shape[1:]
    specs = [SMEM, SMEM] + [VMEM] * (len(args) - 2)
    if before is not None:
        args = args + (before,)
        specs.append(pl.BlockSpec(memory_space=pl.ANY))
    return pl.pallas_call(
        lambda *refs: feature_kernel(i, *refs),
        grid=(1,),
        out_shape=jax.ShapeDtypeStruct(grad.shape, jnp.bfloat16),
        in_specs=specs,
        out_specs=pl.BlockSpec(block, lambda g: (i, 0, 0, 0, 0)),
        scratch_shapes=list(scratch),
        input_output_aliases={} if before is None else {len(args) - 1: 0},
        compiler_params=pltpu.CompilerParams(vmem_limit_bytes=40 << 20),
        cost_estimate=pl.CostEstimate(flops=flops, bytes_accessed=4 << 20, transcendentals=0),
        name="conv_features",
    )(*args)


def exchange(blocks, axis):
    return lax.all_to_all(blocks, axis, 0, 0)


def local(features, grad_out, occupancy, leaf_z, neighbours, kernel):
    nx, ny = grad_out.shape[1], grad_out.shape[2]
    grad = grad_out[0]
    feat = features[0]
    active = (leaf_z[0] >= 0).astype(jnp.int32)
    active_vox = jnp.repeat(jnp.repeat(active, EDGE, axis=0), EDGE, axis=1)
    keep = (occupancy[0] * active_vox[..., None]).astype(jnp.bfloat16)
    keep = jnp.broadcast_to(keep[..., None], grad.shape)
    nbr = neighbours.reshape(-1)
    lz = leaf_z.reshape(-1)
    gx, gy = lax.axis_size("gx"), lax.axis_size("gy")
    core = lax.axis_index("dcn").astype(jnp.int32).reshape(1)
    scale = 1.0 / math.sqrt(lax.axis_size("dcn") * gx * gy * nx * ny * 2 * EDGE)
    field = pltpu.VMEM((VIEW, ny + 2, 3, EDGE, WIDTH), jnp.float32)
    view = pltpu.VMEM((3, VIEW, VIEW, ROWS, WIDTH), jnp.bfloat16)
    own = pltpu.VMEM((EDGE, EDGE * ROWS, WIDTH), jnp.bfloat16)
    acc = pltpu.VMEM((UNIT, WIDTH), jnp.float32)
    terms_shape = jax.ShapeDtypeStruct((2, PADDED, WIDTH), jnp.float32)
    product = 2 * 2 * 512 * 27 * WIDTH * WIDTH

    def shift(block, axis, step):
        count = lax.axis_size(axis)
        pairs = [(i, i + step) for i in range(count) if 0 <= i + step < count]
        return lax.ppermute(block, axis, pairs)

    def terms_of(i, *before):
        return call(
            lambda *refs: terms_kernel(i, *refs),
            "conv_terms",
            terms_shape,
            (field, view, own),
            scalars=2,
            flops=product,
        )(nbr, lz, grad, feat, keep, *before)

    def coded(count):
        return jax.ShapeDtypeStruct((count, PADDED // gy + EDGE, WIDTH), jnp.int16)

    top = shift(grad[nx - 1 :] * keep[nx - 1 :], "gx", 1)
    bottom = shift(grad[:1] * keep[:1], "gx", -1)
    terms = terms_of(0)
    top, bottom, terms = lax.optimization_barrier((top, bottom, terms))

    def side(y):
        return jnp.concatenate(
            [top[:, y : y + 1], grad[:, y : y + 1] * keep[:, y : y + 1], bottom[:, y : y + 1]], axis=0
        )

    left = shift(side(ny - 1), "gy", 1)
    right = shift(side(0), "gy", -1)
    terms = terms_of(1, terms)
    wrows = jnp.transpose(kernel, (0, 2, 1)).reshape(27 * WIDTH, WIDTH)
    edges = (top, bottom, left, right)
    mine, theirs = call(
        edge_kernel,
        "edge_terms",
        (jax.ShapeDtypeStruct((PADDED, WIDTH), jnp.float32), coded(gy)),
        (
            pltpu.VMEM((2, PADDED, WIDTH), jnp.float32),
            pltpu.VMEM((2, ny + 2, 3, EDGE, WIDTH), jnp.float32),
            pltpu.VMEM((2, nx + 2, 3, EDGE, WIDTH), jnp.float32),
            pltpu.VMEM((3, VIEW, ROWS, WIDTH), jnp.bfloat16),
            pltpu.VMEM((3, VIEW, EDGE, WIDTH), jnp.float32),
        ),
        scalars=3,
        flops=product // 4,
    )(nbr, lz, core, feat, keep, *edges, terms)
    theirs = lax.ppermute(theirs, "dcn", [(0, 1), (1, 0)])
    half = call(encode_half_kernel, "encode_half", coded(gy), nbytes=2 << 20)(mine, theirs)

    grad_late, half = lax.optimization_barrier((grad, half))
    out = features_call(0, (nbr, lz, grad_late, keep) + edges + (wrows,), (field, view, acc), product)
    half = exchange(half, "gy")
    piece = call(lambda c, o: sum_kernel(1.0, c, o), "sum_piece", coded(gx), nbytes=1 << 20)(half)
    piece, out = lax.optimization_barrier((piece, out))
    piece = exchange(piece, "gx")
    total = call(lambda c, o: sum_kernel(scale, c, o), "sum_total", coded(gy), nbytes=1 << 20)(piece)
    grad_last, total = lax.optimization_barrier((grad_late, total))
    out = features_call(1, (nbr, lz, grad_last, keep) + edges + (wrows,), (field, view, acc), product, out)
    total, out = lax.optimization_barrier((exchange(total, "gy"), out))
    other = lax.ppermute(total, "dcn", [(0, 1), (1, 0)])
    kernel_grad = call(
        decode_kernel,
        "decode_total",
        jax.ShapeDtypeStruct((27 * WIDTH, WIDTH), jnp.float32),
        scalars=1,
        nbytes=3 << 20,
    )(core, total, other)
    return out[None], kernel_grad.reshape(27, WIDTH, WIDTH)


def solution(mesh):
    return jax.shard_map(
        local,
        mesh=mesh,
        in_specs=(
            P("dcn", "gx", "gy", None, None, None),
            P("dcn", "gx", "gy", None, None, None),
            P("dcn", "gx", "gy", None, None),
            P("dcn", "gx", "gy", None),
            P("dcn", "gx", "gy", None, None),
            P(),
        ),
        out_specs=(P("dcn", "gx", "gy", None, None, None), P()),
        check_vma=False,
    )
```

time: 104 us -> 98.1 us (0.943)
  blocking collectives: 50.6 us -> 19.2 us
  starting transfers between devices: 14.4 us -> 32.3 us
  local copies, waits for them, and re-layouts: 7.03 us -> 11.9 us
  Pallas kernels: 20.6 us -> 24.3 us
    all_to_all x4 -> x1, blocking collectives: 50.6 us -> 19.2 us  [exchange(): return lax.all_to_all(blocks, axis, 0, 0)]
    all_to_all x1 -> x2, starting transfers between devices: 4.22 us -> 15.5 us  [exchange(): return lax.all_to_all(blocks, axis, 0, 0)]
    ppermute x0 -> x2, starting transfers between devices: none -> 5.82 us  [the longest x1 4.22 us: local(): other = lax.ppermute(total, 'dcn', [(0, 1), (1, 0)])]
    ppermute x4, waiting for transfers between devices: 4.97 us -> 0.01 us  [shift(): return lax.ppermute(block, axis, pairs)]
    unnamed x9 -> x25, local copies, waits for them, and re-layouts: 2.26 us -> 6.93 us
    pallas_call x6 -> x9, Pallas kernels: 20.6 us -> 24.3 us  [the longest x7 13.6 us: run(): pl.pallas_call(kernel, out_shape=out_shape, in_specs=[SMEM] * scalars + [...]
    ppermute x0 -> x2, waiting for transfers between devices: none -> 2.98 us  [the longest x1 1.49 us: local(): theirs = lax.ppermute(theirs, 'dcn', [(0, 1), (1, 0)])]
    broadcast_in_dim x1 -> x0, local copies, waits for them, and re-layouts: 1.16 us -> none  [local(): total = exchange(jnp.broadcast_to(total[None], (2,) + total.shape), 'dcn')]
  transfers between devices with their start and end apart: 5 -> 8, of which waited for: 2 -> 4; matrix products, arithmetic and copies ran while one was open for 4% -> 7% of each run, Pallas kernels for 9% -> 20%
where the time goes in v3:
time: 98.1 us; the launch traced here: 97.2 us
  starting transfers between devices  32.3 us (33%)
  Pallas kernels  24.3 us (25%)
  blocking collectives  19.2 us (20%)
  local copies, waits for them, and re-layouts  11.9 us (12%)
  other arithmetic  4.47 us (5%)
  waiting for transfers between devices  4.05 us (4%)
    all_to_all x1, blocking collectives, exchange(): return lax.all_to_all(blocks, axis, 0, 0)  19.2 us
    all_to_all x2, starting transfers between devices, exchange(): return lax.all_to_all(blocks, axis, 0, 0)  15.5 us
    pallas_call x7, Pallas kernels, run(): pl.pallas_call(kernel, out_shape=out_shape, in_specs=[SMEM] * scalars + [...  13.6 us
    ppermute x4, starting transfers between devices, shift(): return lax.ppermute(block, axis, pairs)  10.9 us
    pallas_call x2, Pallas kernels, features_call(): pl.pallas_call(lambda *refs: feature_kernel(i, *refs), grid=(1,), out_sha...  10.8 us
    unnamed x25, local copies, waits for them, and re-layouts  6.93 us
    ppermute x1, starting transfers between devices, local(): other = lax.ppermute(total, 'dcn', [(0, 1), (1, 0)])  4.22 us
  transfers between devices with their start and end apart: 8, of which 4 were waited for; matrix products, arithmetic and copies ran while one was open for 7% of the time, Pallas kernels for 20%

profile of v3, /device:TPU:1, one launch (start us, length us, event | category | flops | bytes accessed | tf_op | source)
XLA Modules:
  0.0 97.2 jit_solution(5296973420104641821)
XLA Ops:
  0.6 0.0 copy-start
  0.6 0.0 copy-start.1
  0.7 0.8 fusion.2
  1.5 0.1 copy.16
  1.6 0.1 broadcast_in_dim.27
  1.7 0.1 reshape.78
  1.8 0.1 copy.20
  1.8 0.9 fusion
  2.8 0.1 copy.21
  2.9 0.1 copy.22
  2.9 1.7 %bitcast_multiply_fusion.2 = (bf16[1,16,2,8,128]{4,3,2,1,0:T(8,128)(2,1)}, bf16[1,16,2,8,128]{4,3,2,1,0:T(8,128)(2,1)}) fusion(bf16[1,16,16,2,8,128]{5,4,3,2,1,0:T(8,128)(2,1)} %param.7, bf16[16,2,8]{2,1,0:T(2,128)(2,1)S(1)} %copy.22, bf16[16,2,8]{2,1,0:T(2,128)(2,1)S(1)} %copy.21), kind=kLoop, calls=%fused_computation.8 | loop fusion | flops 65536 | bytes 263168 | tf_op jit(solution)/shard_map/mul | solution.py:372
  4.6 4.4 %collective-permute-start = (bf16[1,16,2,8,128]{4,3,2,1,0:T(8,128)(2,1)}, bf16[1,16,2,8,128]{4,3,2,1,0:T(8,128)(2,1)S(1)}, u32[]{:S(2)}, u32[]{:S(2)}) collective-permute-start(bf16[1,16,2,8,128]{4,3,2,1,0:T(8,128)(2,1)} %get-tuple-element.31), channel_id=1, source_target_pairs={{0,16},{16,32},{32,48},{48,64},{64,80},{80,96},{96,112},{1,17},{17... | collective-permute-start | bytes 196616 | tf_op jit(solution)/shard_map/ppermute | solution.py:356
  9.0 1.3 %collective-permute-start.1 = (bf16[1,16,2,8,128]{4,3,2,1,0:T(8,128)(2,1)}, bf16[1,16,2,8,128]{4,3,2,1,0:T(8,128)(2,1)S(1)}, u32[]{:S(2)}, u32[]{:S(2)}) collective-permute-start(bf16[1,16,2,8,128]{4,3,2,1,0:T(8,128)(2,1)} %get-tuple-element.30), channel_id=1, source_target_pairs={{16,0},{32,16},{48,32},{64,48},{80,64},{96,80},{112,96},{17,1},{33... | collective-permute-start | bytes 196616 | tf_op jit(solution)/shard_map/ppermute | solution.py:356
  10.3 1.0 %copy.15 = s32[1,16,16,2,8]{1,4,3,2,0:T(8,128)S(1)} copy(s32[1,16,16,2,8]{2,4,3,1,0:T(8,128)} %param.8) | data formatting | bytes 32768 | tf_op args[2]
  11.3 0.8 reshape.76.refs_1_.lz
  12.1 0.2 copy.19
  12.4 0.8 reshape.75.refs_0_.nbr
  13.1 0.1 copy.23
  13.2 0.1 copy.24
  13.3 1.0 %slice_multiply_fusion = (bf16[16,1,2,8,128]{4,3,2,1,0:T(8,128)(2,1)S(1)}, bf16[16,1,2,8,128]{4,3,2,1,0:T(8,128)(2,1)S(1)}) fusion(bf16[16,16,2,8,128]{4,3,2,1,0:T(8,128)(2,1)} %bitcast.33, bf16[16,2,8]{2,1,0:T(2,128)(2,1)S(1)} %copy.24, bf16[16,2,8]{2,1,0:T(2,128)(2,1)S(1)} %copy.23), kind=kLoop, calls=%fused_computation.6 | loop fusion | flops 65536 | bytes 263168 | tf_op jit(solution)/shard_map/mul | solution.py:378
  14.3 0.6 broadcast_in_dim.29.refs_4_.keep.refs_3_
  15.0 0.0 copy-done
  15.0 0.0 copy-done.1
  15.0 4.4 %conv_terms.2.refs_5_ = f32[2,1792,128]{2,1,0:T(8,128)S(1)} custom-call(s32[216]{0:T(256)S(1)} %reshape.75.refs_0_.nbr, s32[8]{0:T(128)S(1)} %reshape.76.refs_1_.lz, bf16[16,16,2,8,128]{4,3,2,1,0:T(8,128)(2,1)S(1)} %bitcast.34, bf16[16,16,2,8,128]{4,3,2,1,0:T(8,128)(2,1)S(1)} %bitcast.38, bf16[16,16,2,8,128]{4,3,2,1,0:T(8,128)(2,1)S(1)} %broadcast_in_dim.29.refs_4_.keep.refs_3_), custom_call_target="tpu_custom_call" | custom-call | flops 905969664 | bytes 4194304 | tf_op jit(solution)/shard_map/conv_terms/pallas_call | solution.py:294
  19.4 0.0 collective-permute-done.top.refs_4_
  19.4 0.0 copy-start.6
  19.4 0.0 collective-permute-done.1.bottom.refs_5_
  19.4 0.0 copy-start.9
  19.4 1.3 %collective-permute-start.3 = (bf16[18,1,2,8,128]{4,3,2,1,0:T(8,128)(2,1)S(1)}, bf16[18,1,2,8,128]{4,3,2,1,0:T(8,128)(2,1)S(1)}, u32[]{:S(2)}, u32[]{:S(2)}) collective-permute-start(bf16[18,1,2,8,128]{4,3,2,1,0:T(8,128)(2,1)S(1)} %pad_maximum_fusion.1), channel_id=1, source_target_pairs={{1,0},{2,1},{3,2},{4,3},{5,4},{6,5},{7,6},{8,7},{9,8},{10,9},{11,1... | collective-permute-start | bytes 221192 | tf_op jit(solution)/shard_map/ppermute | solution.py:356
  20.7 4.0 %collective-permute-start.2 = (bf16[18,1,2,8,128]{4,3,2,1,0:T(8,128)(2,1)S(1)}, bf16[18,1,2,8,128]{4,3,2,1,0:T(8,128)(2,1)S(1)}, u32[]{:S(2)}, u32[]{:S(2)}) collective-permute-start(bf16[18,1,2,8,128]{4,3,2,1,0:T(8,128)(2,1)S(1)} %pad_maximum_fusion), channel_id=1, source_target_pairs={{0,1},{1,2},{2,3},{3,4},{4,5},{5,6},{6,7},{7,8},{8,9},{9,10},{10,1... | collective-permute-start | bytes 221192 | tf_op jit(solution)/shard_map/ppermute | solution.py:356
  24.7 4.4 %conv_terms.3.before = f32[2,1792,128]{2,1,0:T(8,128)S(1)} custom-call(s32[216]{0:T(256)S(1)} %reshape.75.refs_0_.nbr, s32[8]{0:T(128)S(1)} %reshape.76.refs_1_.lz, bf16[16,16,2,8,128]{4,3,2,1,0:T(8,128)(2,1)S(1)} %bitcast.35, bf16[16,16,2,8,128]{4,3,2,1,0:T(8,128)(2,1)S(1)} %bitcast.39, ...), custom_call_target="tpu_custom_call" | custom-call | flops 905969664 | bytes 4194304 | tf_op jit(solution)/shard_map/conv_terms/pallas_call | solution.py:294
  29.1 0.0 collective-permute-done.3.right.refs_7_
  29.1 0.0 collective-permute-done.2.left.refs_6_
  29.1 0.0 copy-start.3
  29.2 0.0 copy-done.6
  29.2 0.0 copy-done.9
  29.2 2.0 %edge_terms.1 = (f32[1792,128]{1,0:T(8,128)S(1)}, s16[16,120,128]{2,1,0:T(8,128)(2,1)S(1)}) custom-call(s32[216]{0:T(256)S(1)} %reshape.75.refs_0_.nbr, s32[8]{0:T(128)S(1)} %reshape.76.refs_1_.lz, s32[1]{0:T(128)} %bitcast.1.core, bf16[16,16,2,8,128]{4,3,2,1,0:T(8,128)(2,1)S(1)} %bitcast.40, ...), custom_call_target="tpu_custom_call" | custom-call | flops 226492416 | bytes 4194304 | tf_op jit(solution)/shard_map/edge_terms/pallas_call | solution.py:294
  31.1 0.0 copy-done.3
  31.1 1.6 %collective-permute-start.4 = (s16[16,120,128]{2,1,0:T(8,128)(2,1)S(1)}, s16[16,120,128]{2,1,0:T(8,128)(2,1)S(1)}, u32[]{:S(2)}, u32[]{:S(2)}) collective-permute-start(s16[16,120,128]{2,1,0:T(8,128)(2,1)S(1)} %get-tuple-element.19), channel_id=1, source_target_pairs={{0,128},{128,0},{1,129},{129,1},{2,130},{130,2},{3,131},{131,3},{4... | collective-permute-start | bytes 1474568 | tf_op jit(solution)/shard_map/ppermute | solution.py:400
  32.8 1.5 %collective-permute-done.4.theirs = s16[16,120,128]{2,1,0:T(8,128)(2,1)S(1)} collective-permute-done((s16[16,120,128]{2,1,0:T(8,128)(2,1)S(1)}, s16[16,120,128]{2,1,0:T(8,128)(2,1)S(1)}, u32[]{:S(2)}, u32[]{:S(2)}) %collective-permute-start.4) | collective-permute-done | bytes 491552 | tf_op jit(solution)/shard_map/ppermute | solution.py:400
  34.2 1.1 %encode_half.1 = s16[16,120,128]{2,1,0:T(8,128)(2,1)} custom-call(f32[1792,128]{1,0:T(8,128)S(1)} %get-tuple-element.18.mine, s16[16,120,128]{2,1,0:T(8,128)(2,1)S(1)} %collective-permute-done.4.theirs), custom_call_target="tpu_custom_call" | custom-call | bytes 2097152 | tf_op jit(solution)/shard_map/encode_half/pallas_call | solution.py:294
  35.3 8.7 %all-to-all-start = ((s16[16,120,128]{2,1,0:T(8,128)(2,1)}), s16[16,120,128]{2,1,0:T(8,128)(2,1)S(1)}, u32[]{:S(2)}, u32[]{:S(2)}) async-start(s16[16,120,128]{2,1,0:T(8,128)(2,1)} %encode_half.1), calls=%async_computation | async-start | bytes 983040 | tf_op jit(solution)/shard_map/all_to_all | solution.py:330
  44.0 1.9 %copy.25 = bf16[27,128,128]{2,1,0:T(8,128)(2,1)S(1)} copy(bf16[27,128,128]{1,2,0:T(8,128)(2,1)} %bitcast.45) | data formatting | bytes 1769472 | tf_op jit(solution)/shard_map/transpose | solution.py:384
  45.9 0.0 copy-start.4
  46.0 0.9 copy-done.4
  46.8 0.8 copy-done.7
  47.7 0.8 copy-done.10
  48.5 5.4 %conv_features.2.refs_9_ = bf16[16,16,2,8,128]{4,3,2,1,0:T(8,128)(2,1)} custom-call(s32[216]{0:T(256)S(1)} %reshape.75.refs_0_.nbr, s32[8]{0:T(128)S(1)} %reshape.76.refs_1_.lz, bf16[16,16,2,8,128]{4,3,2,1,0:T(8,128)(2,1)S(1)} %bitcast.36, bf16[16,16,2,8,128]{4,3,2,1,0:T(8,128)(2,1)S(1)} %broadcast_in_dim.29.refs_4_.keep.refs_3_, ...), custom_call_target="tpu_custom_call" | custom-call | flops 905969664 | bytes 4194304 | tf_op jit(solution)/shard_map/conv_features/pallas_call | solution.py:315
  53.9 0.2 all-to-all-done.c
  54.1 0.2 sum_piece.1
  54.3 19.2 %all_to_all.15.c = s16[8,120,128]{2,1,0:T(8,128)(2,1)S(1)} all-to-all(s16[8,120,128]{2,1,0:T(8,128)(2,1)S(1)} %sum_piece.1), channel_id=1, replica_groups=mesh['dcn'=2,'gx'=8,'gy'=16] {'gx'}, dimensions={0} | all-to-all | bytes 491520 | tf_op jit(solution)/shard_map/all_to_all | solution.py:330
  73.5 0.2 sum_total.1
  73.7 0.0 copy-start.2
  73.7 0.8 copy-done.2
  74.5 6.8 %all-to-all-start.2 = ((s16[16,120,128]{2,1,0:T(8,128)(2,1)}), s16[16,120,128]{2,1,0:T(8,128)(2,1)S(1)}, u32[]{:S(2)}, u32[]{:S(2)}) async-start(s16[16,120,128]{2,1,0:T(8,128)(2,1)} %copy-done.2), calls=%async_computation.2 | async-start | bytes 983040 | tf_op jit(solution)/shard_map/all_to_all | solution.py:330
  81.3 0.0 copy-start.5
  81.3 0.9 copy-done.5
  82.2 0.8 copy-done.8
  83.0 0.8 copy-done.11
  83.9 5.4 %conv_features.3 = bf16[16,16,2,8,128]{4,3,2,1,0:T(8,128)(2,1)} custom-call(s32[216]{0:T(256)S(1)} %reshape.75.refs_0_.nbr, s32[8]{0:T(128)S(1)} %reshape.76.refs_1_.lz, bf16[16,16,2,8,128]{4,3,2,1,0:T(8,128)(2,1)S(1)} %bitcast.37, bf16[16,16,2,8,128]{4,3,2,1,0:T(8,128)(2,1)S(1)} %broadcast_in_dim.29.refs_4_.keep.refs_3_, ...), custom_call_target="tpu_custom_call", output_to_operand_aliasing={{}: (9, {})} | custom-call | flops 905969664 | bytes 4194304 | tf_op jit(solution)/shard_map/conv_features/pallas_call | solution.py:315
  89.3 0.8 all-to-all-done.2.mine
  90.1 4.2 %collective-permute-start.5 = (s16[16,120,128]{2,1,0:T(8,128)(2,1)S(1)}, s16[16,120,128]{2,1,0:T(8,128)(2,1)S(1)}, u32[]{:S(2)}, u32[]{:S(2)}) collective-permute-start(s16[16,120,128]{2,1,0:T(8,128)(2,1)S(1)} %all-to-all-done.2.mine), channel_id=1, source_target_pairs={{0,128},{128,0},{1,129},{129,1},{2,130},{130,2},{3,131},{131,3},{4... | collective-permute-start | bytes 1474568 | tf_op jit(solution)/shard_map/ppermute | solution.py:413
  94.3 1.5 %collective-permute-done.5.theirs = s16[16,120,128]{2,1,0:T(8,128)(2,1)S(1)} collective-permute-done((s16[16,120,128]{2,1,0:T(8,128)(2,1)S(1)}, s16[16,120,128]{2,1,0:T(8,128)(2,1)S(1)}, u32[]{:S(2)}, u32[]{:S(2)}) %collective-permute-start.5) | collective-permute-done | bytes 491552 | tf_op jit(solution)/shard_map/ppermute | solution.py:413
  95.8 1.4 %decode_total.1 = f32[3456,128]{1,0:T(8,128)} custom-call(s32[1]{0:T(128)} %bitcast.1.core, s16[16,120,128]{2,1,0:T(8,128)(2,1)S(1)} %all-to-all-done.2.mine, s16[16,120,128]{2,1,0:T(8,128)(2,1)S(1)} %collective-permute-done.5.theirs), custom_call_target="tpu_custom_call" | custom-call | bytes 3145728 | tf_op jit(solution)/shard_map/decode_total/pallas_call | solution.py:294
  (13 shorter events, 0.1 us)
Async XLA Ops:
  0.6 14.3 %copy-start = (bf16[1,16,16,2,8,128]{5,4,3,2,1,0:T(8,128)(2,1)S(1)}, bf16[1,16,16,2,8,128]{5,4,3,2,1,0:T(8,128)(2,1)}, u32[]{:S(2)}) copy-start(bf16[1,16,16,2,8,128]{5,4,3,2,1,0:T(8,128)(2,1)} %param.7) | copy-start | bytes 3145732
  0.6 14.3 %copy-start.1 = (bf16[1,16,16,2,8,128]{5,4,3,2,1,0:T(8,128)(2,1)S(1)}, bf16[1,16,16,2,8,128]{5,4,3,2,1,0:T(8,128)(2,1)}, u32[]{:S(2)}) copy-start(bf16[1,16,16,2,8,128]{5,4,3,2,1,0:T(8,128)(2,1)} %param.6) | copy-start | bytes 3145732
  4.6 14.7 %collective-permute-start = (bf16[1,16,2,8,128]{4,3,2,1,0:T(8,128)(2,1)}, bf16[1,16,2,8,128]{4,3,2,1,0:T(8,128)(2,1)S(1)}, u32[]{:S(2)}, u32[]{:S(2)}) collective-permute-start(bf16[1,16,2,8,128]{4,3,2,1,0:T(8,128)(2,1)} %get-tuple-element.31), channel_id=1, source_target_pairs={{0,16},{16,32},{32,48},{48,64},{64,80},{80,96},{96,112},{1,17},{17... | collective-permute-start | bytes 196616 | tf_op jit(solution)/shard_map/ppermute | solution.py:356
  9.0 10.4 %collective-permute-start.1 = (bf16[1,16,2,8,128]{4,3,2,1,0:T(8,128)(2,1)}, bf16[1,16,2,8,128]{4,3,2,1,0:T(8,128)(2,1)S(1)}, u32[]{:S(2)}, u32[]{:S(2)}) collective-permute-start(bf16[1,16,2,8,128]{4,3,2,1,0:T(8,128)(2,1)} %get-tuple-element.30), channel_id=1, source_target_pairs={{16,0},{32,16},{48,32},{64,48},{80,64},{96,80},{112,96},{17,1},{33... | collective-permute-start | bytes 196616 | tf_op jit(solution)/shard_map/ppermute | solution.py:356
  19.4 9.8 %copy-start.6 = (bf16[1,16,2,8,128]{4,3,2,1,0:T(8,128)(2,1)}, bf16[1,16,2,8,128]{4,3,2,1,0:T(8,128)(2,1)S(1)}, u32[]{:S(2)}) copy-start(bf16[1,16,2,8,128]{4,3,2,1,0:T(8,128)(2,1)S(1)} %collective-permute-done.top.refs_4_) | copy-start | bytes 196612
  19.4 9.8 %copy-start.9 = (bf16[1,16,2,8,128]{4,3,2,1,0:T(8,128)(2,1)}, bf16[1,16,2,8,128]{4,3,2,1,0:T(8,128)(2,1)S(1)}, u32[]{:S(2)}) copy-start(bf16[1,16,2,8,128]{4,3,2,1,0:T(8,128)(2,1)S(1)} %collective-permute-done.1.bottom.refs_5_) | copy-start | bytes 196612
  19.4 9.7 %collective-permute-start.3 = (bf16[18,1,2,8,128]{4,3,2,1,0:T(8,128)(2,1)S(1)}, bf16[18,1,2,8,128]{4,3,2,1,0:T(8,128)(2,1)S(1)}, u32[]{:S(2)}, u32[]{:S(2)}) collective-permute-start(bf16[18,1,2,8,128]{4,3,2,1,0:T(8,128)(2,1)S(1)} %pad_maximum_fusion.1), channel_id=1, source_target_pairs={{1,0},{2,1},{3,2},{4,3},{5,4},{6,5},{7,6},{8,7},{9,8},{10,9},{11,1... | collective-permute-start | bytes 221192 | tf_op jit(solution)/shard_map/ppermute | solution.py:356
  20.7 8.4 %collective-permute-start.2 = (bf16[18,1,2,8,128]{4,3,2,1,0:T(8,128)(2,1)S(1)}, bf16[18,1,2,8,128]{4,3,2,1,0:T(8,128)(2,1)S(1)}, u32[]{:S(2)}, u32[]{:S(2)}) collective-permute-start(bf16[18,1,2,8,128]{4,3,2,1,0:T(8,128)(2,1)S(1)} %pad_maximum_fusion), channel_id=1, source_target_pairs={{0,1},{1,2},{2,3},{3,4},{4,5},{5,6},{6,7},{7,8},{8,9},{9,10},{10,1... | collective-permute-start | bytes 221192 | tf_op jit(solution)/shard_map/ppermute | solution.py:356
  29.1 2.0 %copy-start.3 = (bf16[18,1,2,8,128]{4,3,2,1,0:T(8,128)(2,1)}, bf16[18,1,2,8,128]{4,3,2,1,0:T(8,128)(2,1)S(1)}, u32[]{:S(2)}) copy-start(bf16[18,1,2,8,128]{4,3,2,1,0:T(8,128)(2,1)S(1)} %collective-permute-done.2.left.refs_6_) | copy-start | bytes 221188
  31.1 3.1 %collective-permute-start.4 = (s16[16,120,128]{2,1,0:T(8,128)(2,1)S(1)}, s16[16,120,128]{2,1,0:T(8,128)(2,1)S(1)}, u32[]{:S(2)}, u32[]{:S(2)}) collective-permute-start(s16[16,120,128]{2,1,0:T(8,128)(2,1)S(1)} %get-tuple-element.19), channel_id=1, source_target_pairs={{0,128},{128,0},{1,129},{129,1},{2,130},{130,2},{3,131},{131,3},{4... | collective-permute-start | bytes 1474568 | tf_op jit(solution)/shard_map/ppermute | solution.py:400
  35.3 18.8 %all-to-all-start = ((s16[16,120,128]{2,1,0:T(8,128)(2,1)}), s16[16,120,128]{2,1,0:T(8,128)(2,1)S(1)}, u32[]{:S(2)}, u32[]{:S(2)}) async-start(s16[16,120,128]{2,1,0:T(8,128)(2,1)} %encode_half.1), calls=%async_computation | async-start | bytes 983040 | tf_op jit(solution)/shard_map/all_to_all | solution.py:330
  45.9 0.9 copy-start.4
  46.8 0.8 copy-start.7
  47.7 0.8 copy-start.10
  73.7 0.8 copy-start.2
  74.5 15.6 %all-to-all-start.2 = ((s16[16,120,128]{2,1,0:T(8,128)(2,1)}), s16[16,120,128]{2,1,0:T(8,128)(2,1)S(1)}, u32[]{:S(2)}, u32[]{:S(2)}) async-start(s16[16,120,128]{2,1,0:T(8,128)(2,1)} %copy-done.2), calls=%async_computation.2 | async-start | bytes 983040 | tf_op jit(solution)/shard_map/all_to_all | solution.py:330
  81.3 0.9 copy-start.5
  82.2 0.8 copy-start.8
  83.0 0.8 copy-start.11
  90.1 5.7 %collective-permute-start.5 = (s16[16,120,128]{2,1,0:T(8,128)(2,1)S(1)}, s16[16,120,128]{2,1,0:T(8,128)(2,1)S(1)}, u32[]{:S(2)}, u32[]{:S(2)}) collective-permute-start(s16[16,120,128]{2,1,0:T(8,128)(2,1)S(1)} %all-to-all-done.2.mine), channel_id=1, source_target_pairs={{0,128},{128,0},{1,129},{129,1},{2,130},{130,2},{3,131},{131,3},{4... | collective-permute-start | bytes 1474568 | tf_op jit(solution)/shard_map/ppermute | solution.py:413

commit v4 on v3

--- a/solution.py
+++ b/solution.py
@@ -28,16 +28,24 @@
 REGIONS = ((0, 1), (1, EDGE), (EDGE + 1, 1))
 
 
-def table_base(i, j, slot):
-    return ((i * 2 + j) * 2 + slot) * 27
+def slots_of(nbr, i, j, slot, first):
+    return [nbr[0, i, j, slot, first + r] for r in range(3)]
+
+
+def live_at(lz, i, j, slot):
+    return lz[0, i, j, slot] >= 0
 
 
 def pair_live(lz, i, slot):
-    return jnp.logical_or(lz[i * 4 + slot] >= 0, lz[i * 4 + 2 + slot] >= 0)
-
-
-def fill_field(i, grad, keep, edges, field):
-    ny = grad.shape[1]
+    return jnp.logical_or(live_at(lz, i, 0, slot), live_at(lz, i, 1, slot))
+
+
+def kept(value, keep, live):
+    return value.astype(jnp.float32) * (keep.astype(jnp.float32) * live.astype(jnp.float32))
+
+
+def fill_field(i, grad, keep, halo, field):
+    nx, ny = grad.shape[0], grad.shape[1]
     low, high = (1, VIEW) if i == 0 else (0, VIEW - 1)
 
     def fill(r, carry):
@@ -48,15 +56,16 @@
     lax.fori_loop(low, high, fill, 0)
     outer = 0 if i == 0 else VIEW - 1
     field[:, :, 2] = jnp.zeros((VIEW, ny + 2, EDGE, WIDTH), jnp.float32)
-    if edges is None:
+    if halo is None:
         field[outer, :, 0:2] = jnp.zeros((ny + 2, 2, EDGE, WIDTH), jnp.float32)
         field[:, 0, 0:2] = jnp.zeros((VIEW, 2, EDGE, WIDTH), jnp.float32)
         field[:, ny + 1, 0:2] = jnp.zeros((VIEW, 2, EDGE, WIDTH), jnp.float32)
     else:
-        top, bottom, left, right = edges
-        field[outer, 1 : ny + 1, 0:2] = (top, bottom)[i][0].astype(jnp.float32)
-        field[:, 0, 0:2] = left[EDGE * i : EDGE * i + VIEW, 0].astype(jnp.float32)
-        field[:, ny + 1, 0:2] = right[EDGE * i : EDGE * i + VIEW, 0].astype(jnp.float32)
+        left = 2 * ny + EDGE * i
+        right = left + nx + 2
+        field[outer, 1 : ny + 1, 0:2] = halo[ny * i : ny * i + ny].astype(jnp.float32)
+        field[:, 0, 0:2] = halo[left : left + VIEW].astype(jnp.float32)
+        field[:, ny + 1, 0:2] = halo[right : right + VIEW].astype(jnp.float32)
 
 
 def fill_view(nbr, field, view, i, slot):
@@ -64,9 +73,8 @@
         for q, (start, count) in enumerate(REGIONS):
             halves = []
             for j in range(2):
-                base = table_base(i, j, slot) + 9 * p + 3 * q
                 span = pl.ds(EDGE * j + start, count)
-                halves.append(shifted(*(field[xl, span, nbr[base + r]] for r in range(3))))
+                halves.append(shifted(*(field[xl, span, s] for s in slots_of(nbr, i, j, slot, 9 * p + 3 * q))))
             for c in range(3):
                 both = jnp.concatenate([halves[0][c], halves[1][c]], axis=1)
                 view[c, xl, start : start + count] = both.astype(jnp.bfloat16)
@@ -88,12 +96,11 @@
     return jnp.concatenate(pieces, axis=1)
 
 
-def pair_row(feat, keep, x, slot):
-    pair = [
-        feat[x, EDGE * j : EDGE * j + EDGE, slot].astype(jnp.float32)
-        * keep[x, EDGE * j : EDGE * j + EDGE, slot].astype(jnp.float32)
-        for j in range(2)
-    ]
+def pair_row(lz, feat, keep, i, x, slot):
+    pair = []
+    for j in range(2):
+        spot = (x, slice(EDGE * j, EDGE * j + EDGE), slot)
+        pair.append(kept(feat[spot], keep[spot], live_at(lz, i, j, slot)))
     return jnp.concatenate(pair, axis=1).reshape(EDGE * ROWS, WIDTH)
 
 
@@ -109,38 +116,42 @@
             total[core, pl.ds(start, 64)] += part[s * 64 : s * 64 + 64, c * WIDTH : (c + 1) * WIDTH]
 
 
-def terms_kernel(i, nbr, lz, grad, feat, keep, *refs):
-    *before, terms, field, view, own = refs
-    fill_field(i, grad, keep, None, field)
-    terms[...] = before[0][...] if before else jnp.zeros_like(terms)
-
-    def unit(slot, carry):
-        @pl.when(pair_live(lz, i, slot))
-        def _():
-            fill_view(nbr, field, view, i, slot)
-
-            def own_rows(xl, c2):
-                own[xl] = pair_row(feat, keep, EDGE * i + xl, slot).astype(jnp.bfloat16)
-                return c2
-
-            lax.fori_loop(0, EDGE, own_rows, 0)
-            own_t = own[...].reshape(UNIT, WIDTH).T
-
-            def offset(t, c2):
-                part = jnp.dot(own_t, columns_at(view, t), preferred_element_type=jnp.float32)
-                add_terms(terms, 3 * t, part)
-                return c2
-
-            lax.fori_loop(0, 9, offset, 0)
-
-        return carry
-
-    lax.fori_loop(0, 2, unit, 0)
-
-
-def edge_kernel(nbr, lz, core, feat, keep, top, bottom, left, right, before, mine, theirs, total, strip, side, row_view, side_view):
+def terms_kernel(nbr, lz, grad, feat, keep, terms, field, view, own):
+    terms[...] = jnp.zeros_like(terms)
+    for i in range(2):
+        fill_field(i, grad, keep, None, field)
+
+        def unit(slot, carry, i=i):
+            @pl.when(pair_live(lz, i, slot))
+            def _():
+                fill_view(nbr, field, view, i, slot)
+
+                def own_rows(xl, c2):
+                    own[xl] = pair_row(lz, feat, keep, i, EDGE * i + xl, slot).astype(jnp.bfloat16)
+                    return c2
+
+                lax.fori_loop(0, EDGE, own_rows, 0)
+                own_t = own[...].reshape(UNIT, WIDTH).T
+
+                def offset(t, c2):
+                    part = jnp.dot(own_t, columns_at(view, t), preferred_element_type=jnp.float32)
+                    add_terms(terms, 3 * t, part)
+                    return c2
+
+                lax.fori_loop(0, 9, offset, 0)
+
+            return carry
+
+        lax.fori_loop(0, 2, unit, 0)
+
+
+def edge_kernel(nbr, lz, core, feat, keep, top, bottom, left, right, before, mine, theirs, halo, total, strip, side, row_view, side_view):
     nx, ny = feat.shape[0], feat.shape[1]
     total[...] = before[...]
+    halo[0:ny] = top[0]
+    halo[ny : 2 * ny] = bottom[0]
+    halo[2 * ny : 2 * ny + nx + 2] = left[:, 0]
+    halo[2 * ny + nx + 2 :] = right[:, 0]
     for i in range(2):
         spot = (0, nx + 1)[i]
         strip[i, 1 : ny + 1, 0:2] = (top, bottom)[i][0].astype(jnp.float32)
@@ -160,25 +171,23 @@
         for q, (start, count) in enumerate(REGIONS):
             halves = []
             for j in range(2):
-                base = table_base(i, j, slot) + 18 * i + 3 * q
                 span = pl.ds(EDGE * j + start, count)
-                halves.append(shifted(*(strip[i, span, nbr[base + r]] for r in range(3))))
+                halves.append(shifted(*(strip[i, span, s] for s in slots_of(nbr, i, j, slot, 18 * i + 3 * q))))
             for c in range(3):
                 both = jnp.concatenate([halves[0][c], halves[1][c]], axis=1)
                 row_view[c, start : start + count] = both.astype(jnp.bfloat16)
-        own_t = pair_row(feat, keep, (0, nx - 1)[i], slot).T.astype(jnp.bfloat16)
+        own_t = pair_row(lz, feat, keep, i, (0, nx - 1)[i], slot).T.astype(jnp.bfloat16)
         for b in range(3):
             pieces = [row_view[c, 2 - b : 2 - b + EDGE].reshape(EDGE * ROWS, WIDTH) for c in range(3)]
             product(own_t, pieces, 18 - 18 * i + 3 * b)
         for j in range(2):
             for p, (start, count) in enumerate(REGIONS):
-                base = table_base(i, j, slot) + 9 * p + 6 * j
                 span = pl.ds(EDGE * i + start, count)
-                moved = shifted(*(side[j, span, nbr[base + r]] for r in range(3)))
+                moved = shifted(*(side[j, span, s] for s in slots_of(nbr, i, j, slot, 9 * p + 6 * j)))
                 for c in range(3):
                     side_view[c, start : start + count] = moved[c]
             spot = (slice(EDGE * i, EDGE * i + EDGE), (0, ny - 1)[j], slot)
-            own_t = (feat[spot].astype(jnp.float32) * keep[spot].astype(jnp.float32)).reshape(EDGE * EDGE, WIDTH)
+            own_t = kept(feat[spot], keep[spot], live_at(lz, i, j, slot)).reshape(EDGE * EDGE, WIDTH)
             own_t = own_t.T.astype(jnp.bfloat16)
             for a in range(3):
                 pieces = [side_view[c, 2 - a : 2 - a + EDGE].reshape(EDGE * EDGE, WIDTH) for c in range(3)]
@@ -201,10 +210,10 @@
         encode(total[1 - here, n * chunk : n * chunk + chunk], theirs, (n,))
 
 
-def feature_kernel(i, nbr, lz, grad, keep, top, bottom, left, right, wrows, *refs):
+def feature_kernel(i, nbr, lz, grad, keep, halo, wrows, *refs):
     out, field, view, acc = refs[-4:]
     ny = grad.shape[1]
-    fill_field(i, grad, keep, (top, bottom, left, right), field)
+    fill_field(i, grad, keep, halo, field)
 
     def unit(slot, carry):
         live = pair_live(lz, i, slot)
@@ -226,8 +235,9 @@
                 block = acc[pl.ds(pl.multiple_of(xl * EDGE * ROWS, EDGE * ROWS), EDGE * ROWS), :]
                 block = block.reshape(EDGE, 2, EDGE, WIDTH)
                 for j in range(2):
-                    k = keep[x, EDGE * j : EDGE * j + EDGE, slot].astype(jnp.float32)
-                    out[xl, EDGE * j : EDGE * j + EDGE, slot] = (block[:, j] * k).astype(jnp.bfloat16)
+                    span = slice(EDGE * j, EDGE * j + EDGE)
+                    value = kept(block[:, j], keep[x, span, slot], live_at(lz, i, j, slot))
+                    out[xl, span, slot] = value.astype(jnp.bfloat16)
                 return c2
 
             lax.fori_loop(0, EDGE, emit, 0)
@@ -297,7 +307,7 @@
             in_specs=[SMEM] * scalars + [VMEM] * (len(args) - scalars),
             out_specs=jax.tree.map(lambda _: VMEM, out_shape),
             scratch_shapes=list(scratch),
-            compiler_params=pltpu.CompilerParams(vmem_limit_bytes=40 << 20),
+            compiler_params=pltpu.CompilerParams(vmem_limit_bytes=20 << 20),
             cost_estimate=pl.CostEstimate(flops=flops, bytes_accessed=nbytes, transcendentals=0),
             name=name,
         )(*args)
@@ -320,7 +330,7 @@
         out_specs=pl.BlockSpec(block, lambda g: (i, 0, 0, 0, 0)),
         scratch_shapes=list(scratch),
         input_output_aliases={} if before is None else {len(args) - 1: 0},
-        compiler_params=pltpu.CompilerParams(vmem_limit_bytes=40 << 20),
+        compiler_params=pltpu.CompilerParams(vmem_limit_bytes=20 << 20),
         cost_estimate=pl.CostEstimate(flops=flops, bytes_accessed=4 << 20, transcendentals=0),
         name="conv_features",
     )(*args)
@@ -334,12 +344,7 @@
     nx, ny = grad_out.shape[1], grad_out.shape[2]
     grad = grad_out[0]
     feat = features[0]
-    active = (leaf_z[0] >= 0).astype(jnp.int32)
-    active_vox = jnp.repeat(jnp.repeat(active, EDGE, axis=0), EDGE, axis=1)
-    keep = (occupancy[0] * active_vox[..., None]).astype(jnp.bfloat16)
-    keep = jnp.broadcast_to(keep[..., None], grad.shape)
-    nbr = neighbours.reshape(-1)
-    lz = leaf_z.reshape(-1)
+    keep = jnp.broadcast_to(occupancy[0].astype(jnp.bfloat16)[..., None], grad.shape)
     gx, gy = lax.axis_size("gx"), lax.axis_size("gy")
     core = lax.axis_index("dcn").astype(jnp.int32).reshape(1)
     scale = 1.0 / math.sqrt(lax.axis_size("dcn") * gx * gy * nx * ny * 2 * EDGE)
@@ -347,7 +352,6 @@
     view = pltpu.VMEM((3, VIEW, VIEW, ROWS, WIDTH), jnp.bfloat16)
     own = pltpu.VMEM((EDGE, EDGE * ROWS, WIDTH), jnp.bfloat16)
     acc = pltpu.VMEM((UNIT, WIDTH), jnp.float32)
-    terms_shape = jax.ShapeDtypeStruct((2, PADDED, WIDTH), jnp.float32)
     product = 2 * 2 * 512 * 27 * WIDTH * WIDTH
 
     def shift(block, axis, step):
@@ -355,23 +359,12 @@
         pairs = [(i, i + step) for i in range(count) if 0 <= i + step < count]
         return lax.ppermute(block, axis, pairs)
 
-    def terms_of(i, *before):
-        return call(
-            lambda *refs: terms_kernel(i, *refs),
-            "conv_terms",
-            terms_shape,
-            (field, view, own),
-            scalars=2,
-            flops=product,
-        )(nbr, lz, grad, feat, keep, *before)
-
     def coded(count):
         return jax.ShapeDtypeStruct((count, PADDED // gy + EDGE, WIDTH), jnp.int16)
 
-    top = shift(grad[nx - 1 :] * keep[nx - 1 :], "gx", 1)
+    core, last = lax.optimization_barrier((core, grad[nx - 1 :] * keep[nx - 1 :]))
+    top = shift(last, "gx", 1)
     bottom = shift(grad[:1] * keep[:1], "gx", -1)
-    terms = terms_of(0)
-    top, bottom, terms = lax.optimization_barrier((top, bottom, terms))
 
     def side(y):
         return jnp.concatenate(
@@ -380,13 +373,24 @@
 
     left = shift(side(ny - 1), "gy", 1)
     right = shift(side(0), "gy", -1)
-    terms = terms_of(1, terms)
+    terms = call(
+        terms_kernel,
+        "conv_terms",
+        jax.ShapeDtypeStruct((2, PADDED, WIDTH), jnp.float32),
+        (field, view, own),
+        scalars=2,
+        flops=2 * product,
+    )(neighbours, leaf_z, grad, feat, keep)
     wrows = jnp.transpose(kernel, (0, 2, 1)).reshape(27 * WIDTH, WIDTH)
     edges = (top, bottom, left, right)
-    mine, theirs = call(
+    mine, theirs, halo = call(
         edge_kernel,
         "edge_terms",
-        (jax.ShapeDtypeStruct((PADDED, WIDTH), jnp.float32), coded(gy)),
+        (
+            jax.ShapeDtypeStruct((PADDED, WIDTH), jnp.float32),
+            coded(gy),
+            jax.ShapeDtypeStruct((2 * (nx + ny + 2), 2, EDGE, WIDTH), jnp.bfloat16),
+        ),
         (
             pltpu.VMEM((2, PADDED, WIDTH), jnp.float32),
             pltpu.VMEM((2, ny + 2, 3, EDGE, WIDTH), jnp.float32),
@@ -396,19 +400,21 @@
         ),
         scalars=3,
         flops=product // 4,
-    )(nbr, lz, core, feat, keep, *edges, terms)
+    )(neighbours, leaf_z, core, feat, keep, *edges, terms)
     theirs = lax.ppermute(theirs, "dcn", [(0, 1), (1, 0)])
     half = call(encode_half_kernel, "encode_half", coded(gy), nbytes=2 << 20)(mine, theirs)
 
-    grad_late, half = lax.optimization_barrier((grad, half))
-    out = features_call(0, (nbr, lz, grad_late, keep) + edges + (wrows,), (field, view, acc), product)
+    def features_part(i, value, *before):
+        late, value = lax.optimization_barrier((grad, value))
+        args = (neighbours, leaf_z, late, keep, halo, wrows)
+        return features_call(i, args, (field, view, acc), product, *before), value
+
     half = exchange(half, "gy")
     piece = call(lambda c, o: sum_kernel(1.0, c, o), "sum_piece", coded(gx), nbytes=1 << 20)(half)
-    piece, out = lax.optimization_barrier((piece, out))
-    piece = exchange(piece, "gx")
+    out, piece = features_part(0, piece)
+    piece, out = lax.optimization_barrier((exchange(piece, "gx"), out))
     total = call(lambda c, o: sum_kernel(scale, c, o), "sum_total", coded(gy), nbytes=1 << 20)(piece)
-    grad_last, total = lax.optimization_barrier((grad_late, total))
-    out = features_call(1, (nbr, lz, grad_last, keep) + edges + (wrows,), (field, view, acc), product, out)
+    out, total = features_part(1, total, out)
     total, out = lax.optimization_barrier((exchange(total, "gy"), out))
     other = lax.ppermute(total, "dcn", [(0, 1), (1, 0)])
     kernel_grad = call(

time: 98.1 us -> 92 us (0.938)
  local copies, waits for them, and re-layouts: 11.9 us -> 6.77 us
  waiting for transfers between devices: 4.05 us -> 7.72 us
  starting transfers between devices: 32.3 us -> 29.3 us
  blocking collectives: 19.2 us -> 17.7 us
    unnamed x25 -> x16, local copies, waits for them, and re-layouts: 6.93 us -> 1.75 us
    all_to_all x2, starting transfers between devices: 15.5 us -> 12.2 us  [exchange(): return lax.all_to_all(blocks, axis, 0, 0)]
    all_to_all x2, waiting for transfers between devices: 1.06 us -> 4.22 us  [exchange(): return lax.all_to_all(blocks, axis, 0, 0)]
    reshape x4 -> x0, local copies, waits for them, and re-layouts: 1.62 us -> none  [the longest x1 0.77 us: local(): nbr = neighbours.reshape(-1)]
    all_to_all x1, blocking collectives: 19.2 us -> 17.7 us  [exchange(): return lax.all_to_all(blocks, axis, 0, 0)]
    pallas_call x7 -> x6, Pallas kernels: 13.6 us -> 13 us  [run(): pl.pallas_call(kernel, out_shape=out_shape, in_specs=[SMEM] * scalars + [...]
    convert_element_type x3 -> x2, other arithmetic: 1.78 us -> 1.98 us  [local(): occupancy[0].astype(jnp.bfloat16)[..., None]]
  transfers between devices with their start and end apart: 8 -> 8, of which waited for: 4 -> 5; matrix products, arithmetic and copies ran while one was open for 7% -> 7% of each run, Pallas kernels for 20% -> 21%
where the time goes in v4:
time: 92 us; the launch traced here: 90.5 us
  starting transfers between devices  29.3 us (32%)
  Pallas kernels  24.1 us (26%)
  blocking collectives  17.7 us (19%)
  waiting for transfers between devices  7.72 us (8%)
  local copies, waits for them, and re-layouts  6.77 us (7%)
  other arithmetic  4.01 us (4%)
    all_to_all x1, blocking collectives, exchange(): return lax.all_to_all(blocks, axis, 0, 0)  17.7 us
    pallas_call x6, Pallas kernels, run(): pl.pallas_call(kernel, out_shape=out_shape, in_specs=[SMEM] * scalars + [...  13 us
    all_to_all x2, starting transfers between devices, exchange(): return lax.all_to_all(blocks, axis, 0, 0)  12.2 us
    pallas_call x2, Pallas kernels, features_call(): pl.pallas_call(lambda *refs: feature_kernel(i, *refs), grid=(1,), out_sha...  11 us
    ppermute x4, starting transfers between devices, shift(): return lax.ppermute(block, axis, pairs)  10.2 us
    ppermute x1, starting transfers between devices, local(): other = lax.ppermute(total, 'dcn', [(0, 1), (1, 0)])  4.65 us
    all_to_all x2, waiting for transfers between devices, exchange(): return lax.all_to_all(blocks, axis, 0, 0)  4.22 us
    ppermute x1, starting transfers between devices, local(): theirs = lax.ppermute(theirs, 'dcn', [(0, 1), (1, 0)])  2.29 us
  transfers between devices with their start and end apart: 8, of which 5 were waited for; matrix products, arithmetic and copies ran while one was open for 7% of the time, Pallas kernels for 21%

profile of v4, /device:TPU:1, one launch (start us, length us, event | category | flops | bytes accessed | tf_op | source)
XLA Modules:
  0.0 90.5 jit_solution(121602940571266966)
XLA Ops:
  0.6 0.0 copy-start
  0.6 0.0 copy-start.4
  0.7 0.0 copy-start.6
  0.7 0.0 copy-start.7
  0.7 1.1 %convert_element_type.15 = bf16[1,16,16,2,8]{2,4,3,1,0:T(8,128)(2,1)S(1)} convert(s32[1,16,16,2,8]{2,4,3,1,0:T(8,128)} %param.8) | non-fusion elementwise | flops 4096 | bytes 24576 | tf_op jit(solution)/shard_map/convert_element_type | solution.py:347
  1.8 0.1 copy.18
  1.8 0.1 copy.20
  1.9 1.0 %bitcast_multiply_fusion = (bf16[1,16,2,8,128]{4,3,2,1,0:T(8,128)(2,1)S(1)}, bf16[1,16,2,8,128]{4,3,2,1,0:T(8,128)(2,1)S(1)}) fusion(bf16[1,16,16,2,8,128]{5,4,3,2,1,0:T(8,128)(2,1)} %param.7, bf16[16,2,8]{2,1,0:T(2,128)(2,1)S(1)} %copy.20, bf16[16,2,8]{2,1,0:T(2,128)(2,1)S(1)} %copy.18), kind=kLoop, calls=%fused_computation.4 | loop fusion | flops 65536 | bytes 263168 | tf_op jit(solution)/shard_map/mul | solution.py:367
  2.9 4.4 %collective-permute-start = (bf16[1,16,2,8,128]{4,3,2,1,0:T(8,128)(2,1)S(1)}, bf16[1,16,2,8,128]{4,3,2,1,0:T(8,128)(2,1)S(1)}, u32[]{:S(2)}, u32[]{:S(2)}) collective-permute-start(bf16[1,16,2,8,128]{4,3,2,1,0:T(8,128)(2,1)S(1)} %get-tuple-element.16), channel_id=1, source_target_pairs={{0,16},{16,32},{32,48},{48,64},{64,80},{80,96},{96,112},{1,17},{17... | collective-permute-start | bytes 196616 | tf_op jit(solution)/shard_map/ppermute | solution.py:360
  7.3 1.3 %collective-permute-start.1 = (bf16[1,16,2,8,128]{4,3,2,1,0:T(8,128)(2,1)S(1)}, bf16[1,16,2,8,128]{4,3,2,1,0:T(8,128)(2,1)S(1)}, u32[]{:S(2)}, u32[]{:S(2)}) collective-permute-start(bf16[1,16,2,8,128]{4,3,2,1,0:T(8,128)(2,1)S(1)} %get-tuple-element.30), channel_id=1, source_target_pairs={{16,0},{32,16},{48,32},{64,48},{80,64},{96,80},{112,96},{17,1},{33... | collective-permute-start | bytes 196616 | tf_op jit(solution)/shard_map/ppermute | solution.py:360
  8.6 0.9 %convert_bitcast_fusion = bf16[16,16,2,8]{1,3,2,0:T(8,128)(2,1)S(1)} fusion(s32[1,16,16,2,8]{2,4,3,1,0:T(8,128)} %param.8), kind=kLoop, calls=%fused_computation.11 | loop fusion | flops 4096 | bytes 24576 | tf_op jit(solution)/shard_map/convert_element_type | solution.py:347
  9.5 0.1 fusion.1
  9.6 0.2 copy.21
  9.8 0.1 copy.22
  9.9 0.2 copy.23
  10.1 0.1 copy.24
  10.2 1.0 %slice_multiply_fusion = (bf16[16,1,2,8,128]{4,3,2,1,0:T(8,128)(2,1)S(1)}, bf16[16,1,2,8,128]{4,3,2,1,0:T(8,128)(2,1)S(1)}) fusion(bf16[16,16,2,8,128]{4,3,2,1,0:T(8,128)(2,1)} %bitcast.21, bf16[16,2,8]{2,1,0:T(2,128)(2,1)S(1)} %copy.24, bf16[16,2,8]{2,1,0:T(2,128)(2,1)S(1)} %copy.22), kind=kLoop, calls=%fused_computation.2 | loop fusion | flops 65536 | bytes 263168 | tf_op jit(solution)/shard_map/mul | solution.py:371
  11.2 0.8 copy.19
  12.0 0.0 collective-permute-done.top
  12.0 0.5 collective-permute-done.1.bottom
  12.5 3.2 %collective-permute-start.2 = (bf16[18,1,2,8,128]{4,3,2,1,0:T(8,128)(2,1)S(1)}, bf16[18,1,2,8,128]{4,3,2,1,0:T(8,128)(2,1)S(1)}, u32[]{:S(2)}, u32[]{:S(2)}) collective-permute-start(bf16[18,1,2,8,128]{4,3,2,1,0:T(8,128)(2,1)S(1)} %pad_maximum_fusion), channel_id=1, source_target_pairs={{0,1},{1,2},{2,3},{3,4},{4,5},{5,6},{6,7},{7,8},{8,9},{9,10},{10,1... | collective-permute-start | bytes 221192 | tf_op jit(solution)/shard_map/ppermute | solution.py:360
  15.8 1.3 %collective-permute-start.3 = (bf16[18,1,2,8,128]{4,3,2,1,0:T(8,128)(2,1)S(1)}, bf16[18,1,2,8,128]{4,3,2,1,0:T(8,128)(2,1)S(1)}, u32[]{:S(2)}, u32[]{:S(2)}) collective-permute-start(bf16[18,1,2,8,128]{4,3,2,1,0:T(8,128)(2,1)S(1)} %pad_maximum_fusion.1), channel_id=1, source_target_pairs={{1,0},{2,1},{3,2},{4,3},{5,4},{6,5},{7,6},{8,7},{9,8},{10,9},{11,1... | collective-permute-start | bytes 221192 | tf_op jit(solution)/shard_map/ppermute | solution.py:360
  17.1 1.5 %broadcast_in_dim.23.keep.refs_3_ = bf16[16,16,2,8,128]{4,3,2,1,0:T(8,128)(2,1)S(1)} broadcast(bf16[16,16,2,8]{3,2,1,0:T(2,128)(2,1)} %copy.19), dimensions={0,1,2,3} | broadcast | bytes 1056768 | tf_op jit(solution)/shard_map/broadcast_in_dim | solution.py:347
  18.6 0.0 copy-done
  18.6 0.0 copy-done.4
  18.6 0.0 copy-done.6
  18.6 0.0 copy-done.7
  18.6 0.0 copy-start.5
  18.6 8.2 %conv_terms.1.before = f32[2,1792,128]{2,1,0:T(8,128)S(1)} custom-call(s32[1,2,2,2,27]{4,3,2,1,0:T(2,128)S(1)} %copy-done.6, s32[1,2,2,2]{3,2,1,0:T(2,128)S(1)} %copy-done.7, bf16[16,16,2,8,128]{4,3,2,1,0:T(8,128)(2,1)S(1)} %bitcast.22, bf16[16,16,2,8,128]{4,3,2,1,0:T(8,128)(2,1)S(1)} %bitcast.25, bf16[16,16,2,8,128]{4,3,2,1,0:T(8,128)(2,1)S(1)} %broadcast_in_dim.23.keep.refs_3_), custom_call_target="tpu_custom_call" | custom-call | flops 1811939328 | bytes 4194304 | tf_op jit(solution)/shard_map/conv_terms/pallas_call | solution.py:304
  26.8 0.0 collective-permute-done.2.left
  26.9 0.0 collective-permute-done.3.right
  26.9 0.0 copy-done.5
  26.9 2.1 %edge_terms.1 = (f32[1792,128]{1,0:T(8,128)S(1)}, s16[16,120,128]{2,1,0:T(8,128)(2,1)S(1)}, bf16[68,2,8,128]{3,2,1,0:T(8,128)(2,1)S(1)}) custom-call(s32[1,2,2,2,27]{4,3,2,1,0:T(2,128)S(1)} %copy-done.6, s32[1,2,2,2]{3,2,1,0:T(2,128)S(1)} %copy-done.7, s32[1]{0:T(128)} %bitcast.1.core, bf16[16,16,2,8,128]{4,3,2,1,0:T(8,128)(2,1)S(1)} %bitcast.26, ...), custom_call_target="tpu_custom_call" | custom-call | flops 226492416 | bytes 4194304 | tf_op jit(solution)/shard_map/edge_terms/pallas_call | solution.py:304
  28.9 0.0 copy-start.2
  29.0 2.3 %collective-permute-start.4 = (s16[16,120,128]{2,1,0:T(8,128)(2,1)S(1)}, s16[16,120,128]{2,1,0:T(8,128)(2,1)S(1)}, u32[]{:S(2)}, u32[]{:S(2)}) collective-permute-start(s16[16,120,128]{2,1,0:T(8,128)(2,1)S(1)} %get-tuple-element.18), channel_id=1, source_target_pairs={{0,128},{128,0},{1,129},{129,1},{2,130},{130,2},{3,131},{131,3},{4... | collective-permute-start | bytes 1474568 | tf_op jit(solution)/shard_map/ppermute | solution.py:404
  31.2 1.5 %collective-permute-done.4.theirs = s16[16,120,128]{2,1,0:T(8,128)(2,1)S(1)} collective-permute-done((s16[16,120,128]{2,1,0:T(8,128)(2,1)S(1)}, s16[16,120,128]{2,1,0:T(8,128)(2,1)S(1)}, u32[]{:S(2)}, u32[]{:S(2)}) %collective-permute-start.4) | collective-permute-done | bytes 491552 | tf_op jit(solution)/shard_map/ppermute | solution.py:404
  32.7 0.3 encode_half.1
  33.1 17.7 %all_to_all.15.c = s16[16,120,128]{2,1,0:T(8,128)(2,1)S(1)} all-to-all(s16[16,120,128]{2,1,0:T(8,128)(2,1)S(1)} %encode_half.1), channel_id=1, replica_groups=mesh['dcn'=2,'gx'=8,'gy'=16] {'gy'}, dimensions={0} | all-to-all | bytes 983040 | tf_op jit(solution)/shard_map/all_to_all | solution.py:340
  50.8 0.9 sum_piece.1
  51.7 8.7 %all-to-all-start.1 = ((s16[8,120,128]{2,1,0:T(8,128)(2,1)}), s16[8,120,128]{2,1,0:T(8,128)(2,1)S(1)}, u32[]{:S(2)}, u32[]{:S(2)}) async-start(s16[8,120,128]{2,1,0:T(8,128)(2,1)} %sum_piece.1), calls=%async_computation.1 | async-start | bytes 491520 | tf_op jit(solution)/shard_map/all_to_all | solution.py:340
  60.3 1.9 %copy.25 = bf16[27,128,128]{2,1,0:T(8,128)(2,1)S(1)} copy(bf16[27,128,128]{1,2,0:T(8,128)(2,1)} %bitcast.29) | data formatting | bytes 1769472 | tf_op jit(solution)/shard_map/transpose | solution.py:384
  62.2 0.0 copy-done.2
  62.2 5.5 %conv_features.2.refs_6_ = bf16[16,16,2,8,128]{4,3,2,1,0:T(8,128)(2,1)} custom-call(s32[1,2,2,2,27]{4,3,2,1,0:T(2,128)S(1)} %copy-done.6, s32[1,2,2,2]{3,2,1,0:T(2,128)S(1)} %copy-done.7, bf16[16,16,2,8,128]{4,3,2,1,0:T(8,128)(2,1)S(1)} %bitcast.23, bf16[16,16,2,8,128]{4,3,2,1,0:T(8,128)(2,1)S(1)} %broadcast_in_dim.23.keep.refs_3_, ...), custom_call_target="tpu_custom_call" | custom-call | flops 905969664 | bytes 4194304 | tf_op jit(solution)/shard_map/conv_features/pallas_call | solution.py:325
  67.7 1.8 %all-to-all-done.1.c = s16[8,120,128]{2,1,0:T(8,128)(2,1)S(1)} async-done(((s16[8,120,128]{2,1,0:T(8,128)(2,1)}), s16[8,120,128]{2,1,0:T(8,128)(2,1)S(1)}, u32[]{:S(2)}, u32[]{:S(2)}) %all-to-all-start.1) | async-done | bytes 245792 | tf_op jit(solution)/shard_map/all_to_all | solution.py:340
  69.6 0.2 sum_total.1
  69.8 0.0 copy-start.1
  69.8 0.8 copy-done.1
  70.5 3.6 %all-to-all-start.2 = ((s16[16,120,128]{2,1,0:T(8,128)(2,1)}), s16[16,120,128]{2,1,0:T(8,128)(2,1)S(1)}, u32[]{:S(2)}, u32[]{:S(2)}) async-start(s16[16,120,128]{2,1,0:T(8,128)(2,1)} %copy-done.1), calls=%async_computation.2 | async-start | bytes 983040 | tf_op jit(solution)/shard_map/all_to_all | solution.py:340
  74.1 0.0 copy-start.3
  74.1 0.9 %copy-done.3 = bf16[68,2,8,128]{3,2,1,0:T(8,128)(2,1)S(1)} copy-done((bf16[68,2,8,128]{3,2,1,0:T(8,128)(2,1)S(1)}, bf16[68,2,8,128]{3,2,1,0:T(8,128)(2,1)}, u32[]{:S(2)}) %copy-start.3) | copy-done | bytes 278552
  75.1 5.5 %conv_features.3 = bf16[16,16,2,8,128]{4,3,2,1,0:T(8,128)(2,1)} custom-call(s32[1,2,2,2,27]{4,3,2,1,0:T(2,128)S(1)} %copy-done.6, s32[1,2,2,2]{3,2,1,0:T(2,128)S(1)} %copy-done.7, bf16[16,16,2,8,128]{4,3,2,1,0:T(8,128)(2,1)S(1)} %bitcast.24, bf16[16,16,2,8,128]{4,3,2,1,0:T(8,128)(2,1)S(1)} %broadcast_in_dim.23.keep.refs_3_, ...), custom_call_target="tpu_custom_call", output_to_operand_aliasing={{}: (6, {})} | custom-call | flops 905969664 | bytes 4194304 | tf_op jit(solution)/shard_map/conv_features/pallas_call | solution.py:325
  80.6 2.4 %all-to-all-done.2.mine = s16[16,120,128]{2,1,0:T(8,128)(2,1)S(1)} async-done(((s16[16,120,128]{2,1,0:T(8,128)(2,1)}), s16[16,120,128]{2,1,0:T(8,128)(2,1)S(1)}, u32[]{:S(2)}, u32[]{:S(2)}) %all-to-all-start.2) | async-done | bytes 491552 | tf_op jit(solution)/shard_map/all_to_all | solution.py:340
  83.0 4.6 %collective-permute-start.5 = (s16[16,120,128]{2,1,0:T(8,128)(2,1)S(1)}, s16[16,120,128]{2,1,0:T(8,128)(2,1)S(1)}, u32[]{:S(2)}, u32[]{:S(2)}) collective-permute-start(s16[16,120,128]{2,1,0:T(8,128)(2,1)S(1)} %all-to-all-done.2.mine), channel_id=1, source_target_pairs={{0,128},{128,0},{1,129},{129,1},{2,130},{130,2},{3,131},{131,3},{4... | collective-permute-start | bytes 1474568 | tf_op jit(solution)/shard_map/ppermute | solution.py:419
  87.6 1.5 %collective-permute-done.5.theirs = s16[16,120,128]{2,1,0:T(8,128)(2,1)S(1)} collective-permute-done((s16[16,120,128]{2,1,0:T(8,128)(2,1)S(1)}, s16[16,120,128]{2,1,0:T(8,128)(2,1)S(1)}, u32[]{:S(2)}, u32[]{:S(2)}) %collective-permute-start.5) | collective-permute-done | bytes 491552 | tf_op jit(solution)/shard_map/ppermute | solution.py:419
  89.1 1.4 %decode_total.1 = f32[3456,128]{1,0:T(8,128)} custom-call(s32[1]{0:T(128)} %bitcast.1.core, s16[16,120,128]{2,1,0:T(8,128)(2,1)S(1)} %all-to-all-done.2.mine, s16[16,120,128]{2,1,0:T(8,128)(2,1)S(1)} %collective-permute-done.5.theirs), custom_call_target="tpu_custom_call" | custom-call | bytes 3145728 | tf_op jit(solution)/shard_map/decode_total/pallas_call | solution.py:304
  (5 shorter events, 0.0 us)
Async XLA Ops:
  0.6 18.0 %copy-start = (bf16[1,16,16,2,8,128]{5,4,3,2,1,0:T(8,128)(2,1)S(1)}, bf16[1,16,16,2,8,128]{5,4,3,2,1,0:T(8,128)(2,1)}, u32[]{:S(2)}) copy-start(bf16[1,16,16,2,8,128]{5,4,3,2,1,0:T(8,128)(2,1)} %param.7) | copy-start | bytes 3145732
  0.6 17.9 %copy-start.4 = (bf16[1,16,16,2,8,128]{5,4,3,2,1,0:T(8,128)(2,1)S(1)}, bf16[1,16,16,2,8,128]{5,4,3,2,1,0:T(8,128)(2,1)}, u32[]{:S(2)}) copy-start(bf16[1,16,16,2,8,128]{5,4,3,2,1,0:T(8,128)(2,1)} %param.6) | copy-start | bytes 3145732
  0.7 17.9 %copy-start.6 = (s32[1,2,2,2,27]{4,3,2,1,0:T(2,128)S(1)}, s32[1,2,2,2,27]{4,3,2,1,0:T(2,128)}, u32[]{:S(2)}) copy-start(s32[1,2,2,2,27]{4,3,2,1,0:T(2,128)} %refs_0_.3) | copy-start | bytes 2596
  0.7 17.9 %copy-start.7 = (s32[1,2,2,2]{3,2,1,0:T(2,128)S(1)}, s32[1,2,2,2]{3,2,1,0:T(2,128)}, u32[]{:S(2)}) copy-start(s32[1,2,2,2]{3,2,1,0:T(2,128)} %refs_1_.3) | copy-start | bytes 100
  2.9 9.1 %collective-permute-start = (bf16[1,16,2,8,128]{4,3,2,1,0:T(8,128)(2,1)S(1)}, bf16[1,16,2,8,128]{4,3,2,1,0:T(8,128)(2,1)S(1)}, u32[]{:S(2)}, u32[]{:S(2)}) collective-permute-start(bf16[1,16,2,8,128]{4,3,2,1,0:T(8,128)(2,1)S(1)} %get-tuple-element.16), channel_id=1, source_target_pairs={{0,16},{16,32},{32,48},{48,64},{64,80},{80,96},{96,112},{1,17},{17... | collective-permute-start | bytes 196616 | tf_op jit(solution)/shard_map/ppermute | solution.py:360
  7.3 5.2 %collective-permute-start.1 = (bf16[1,16,2,8,128]{4,3,2,1,0:T(8,128)(2,1)S(1)}, bf16[1,16,2,8,128]{4,3,2,1,0:T(8,128)(2,1)S(1)}, u32[]{:S(2)}, u32[]{:S(2)}) collective-permute-start(bf16[1,16,2,8,128]{4,3,2,1,0:T(8,128)(2,1)S(1)} %get-tuple-element.30), channel_id=1, source_target_pairs={{16,0},{32,16},{48,32},{64,48},{80,64},{96,80},{112,96},{17,1},{33... | collective-permute-start | bytes 196616 | tf_op jit(solution)/shard_map/ppermute | solution.py:360
  12.5 14.3 %collective-permute-start.2 = (bf16[18,1,2,8,128]{4,3,2,1,0:T(8,128)(2,1)S(1)}, bf16[18,1,2,8,128]{4,3,2,1,0:T(8,128)(2,1)S(1)}, u32[]{:S(2)}, u32[]{:S(2)}) collective-permute-start(bf16[18,1,2,8,128]{4,3,2,1,0:T(8,128)(2,1)S(1)} %pad_maximum_fusion), channel_id=1, source_target_pairs={{0,1},{1,2},{2,3},{3,4},{4,5},{5,6},{6,7},{7,8},{8,9},{9,10},{10,1... | collective-permute-start | bytes 221192 | tf_op jit(solution)/shard_map/ppermute | solution.py:360
  15.8 11.1 %collective-permute-start.3 = (bf16[18,1,2,8,128]{4,3,2,1,0:T(8,128)(2,1)S(1)}, bf16[18,1,2,8,128]{4,3,2,1,0:T(8,128)(2,1)S(1)}, u32[]{:S(2)}, u32[]{:S(2)}) collective-permute-start(bf16[18,1,2,8,128]{4,3,2,1,0:T(8,128)(2,1)S(1)} %pad_maximum_fusion.1), channel_id=1, source_target_pairs={{1,0},{2,1},{3,2},{4,3},{5,4},{6,5},{7,6},{8,7},{9,8},{10,9},{11,1... | collective-permute-start | bytes 221192 | tf_op jit(solution)/shard_map/ppermute | solution.py:360
  18.6 8.2 %copy-start.5 = (bf16[1,16,16,2,8,128]{5,4,3,2,1,0:T(8,128)(2,1)S(1)}, bf16[1,16,16,2,8,128]{5,4,3,2,1,0:T(8,128)(2,1)}, u32[]{:S(2)}) copy-start(bf16[1,16,16,2,8,128]{5,4,3,2,1,0:T(8,128)(2,1)} %param.6) | copy-start | bytes 3145732
  28.9 33.3 %copy-start.2 = (bf16[68,2,8,128]{3,2,1,0:T(8,128)(2,1)}, bf16[68,2,8,128]{3,2,1,0:T(8,128)(2,1)S(1)}, u32[]{:S(2)}) copy-start(bf16[68,2,8,128]{3,2,1,0:T(8,128)(2,1)S(1)} %get-tuple-element.21.refs_4_) | copy-start | bytes 835588
  29.0 3.8 %collective-permute-start.4 = (s16[16,120,128]{2,1,0:T(8,128)(2,1)S(1)}, s16[16,120,128]{2,1,0:T(8,128)(2,1)S(1)}, u32[]{:S(2)}, u32[]{:S(2)}) collective-permute-start(s16[16,120,128]{2,1,0:T(8,128)(2,1)S(1)} %get-tuple-element.18), channel_id=1, source_target_pairs={{0,128},{128,0},{1,129},{129,1},{2,130},{130,2},{3,131},{131,3},{4... | collective-permute-start | bytes 1474568 | tf_op jit(solution)/shard_map/ppermute | solution.py:404
  51.7 17.9 %all-to-all-start.1 = ((s16[8,120,128]{2,1,0:T(8,128)(2,1)}), s16[8,120,128]{2,1,0:T(8,128)(2,1)S(1)}, u32[]{:S(2)}, u32[]{:S(2)}) async-start(s16[8,120,128]{2,1,0:T(8,128)(2,1)} %sum_piece.1), calls=%async_computation.1 | async-start | bytes 491520 | tf_op jit(solution)/shard_map/all_to_all | solution.py:340
  69.8 0.8 copy-start.1
  70.5 12.4 %all-to-all-start.2 = ((s16[16,120,128]{2,1,0:T(8,128)(2,1)}), s16[16,120,128]{2,1,0:T(8,128)(2,1)S(1)}, u32[]{:S(2)}, u32[]{:S(2)}) async-start(s16[16,120,128]{2,1,0:T(8,128)(2,1)} %copy-done.1), calls=%async_computation.2 | async-start | bytes 983040 | tf_op jit(solution)/shard_map/all_to_all | solution.py:340
  74.1 1.0 %copy-start.3 = (bf16[68,2,8,128]{3,2,1,0:T(8,128)(2,1)S(1)}, bf16[68,2,8,128]{3,2,1,0:T(8,128)(2,1)}, u32[]{:S(2)}) copy-start(bf16[68,2,8,128]{3,2,1,0:T(8,128)(2,1)} %copy-done.2) | copy-start | bytes 835588
  83.0 6.1 %collective-permute-start.5 = (s16[16,120,128]{2,1,0:T(8,128)(2,1)S(1)}, s16[16,120,128]{2,1,0:T(8,128)(2,1)S(1)}, u32[]{:S(2)}, u32[]{:S(2)}) collective-permute-start(s16[16,120,128]{2,1,0:T(8,128)(2,1)S(1)} %all-to-all-done.2.mine), channel_id=1, source_target_pairs={{0,128},{128,0},{1,129},{129,1},{2,130},{130,2},{3,131},{131,3},{4... | collective-permute-start | bytes 1474568 | tf_op jit(solution)/shard_map/ppermute | solution.py:419

commit v5 on v4

--- a/solution.py
+++ b/solution.py
@@ -89,10 +89,13 @@
     view_rows(EDGE + 1, 2)
 
 
-def columns_at(view, t):
-    a = t // 3
-    b = t % 3
-    pieces = [view[c, pl.ds(2 - a, EDGE), pl.ds(2 - b, EDGE)].reshape(UNIT, WIDTH) for c in range(3)]
+def columns_of(view):
+    pieces = [
+        view[c, 2 - a : 2 - a + EDGE, 2 - b : 2 - b + EDGE].reshape(UNIT, WIDTH)
+        for a in range(3)
+        for b in range(3)
+        for c in range(3)
+    ]
     return jnp.concatenate(pieces, axis=1)
 
 
@@ -108,12 +111,8 @@
     for c in range(3):
         for s in range(2):
             half = 2 * (first + c) + s
-            if isinstance(half, int):
-                core, start = half // 27, half * 64 - half // 27 * HALF
-            else:
-                core = (half >= 27).astype(jnp.int32)
-                start = pl.multiple_of(half * 64 - core * HALF, 64)
-            total[core, pl.ds(start, 64)] += part[s * 64 : s * 64 + 64, c * WIDTH : (c + 1) * WIDTH]
+            core, start = half // 27, half * 64 - half // 27 * HALF
+            total[core, start : start + 64] += part[s * 64 : s * 64 + 64, c * WIDTH : (c + 1) * WIDTH]
 
 
 def terms_kernel(nbr, lz, grad, feat, keep, terms, field, view, own):
@@ -133,12 +132,9 @@
                 lax.fori_loop(0, EDGE, own_rows, 0)
                 own_t = own[...].reshape(UNIT, WIDTH).T
 
-                def offset(t, c2):
-                    part = jnp.dot(own_t, columns_at(view, t), preferred_element_type=jnp.float32)
-                    add_terms(terms, 3 * t, part)
-                    return c2
-
-                lax.fori_loop(0, 9, offset, 0)
+                part = jnp.dot(own_t, columns_of(view), preferred_element_type=jnp.float32)
+                for k in range(0, 27, 3):
+                    add_terms(terms, k, part[:, k * WIDTH : (k + 3) * WIDTH])
 
             return carry
 
@@ -210,7 +206,7 @@
         encode(total[1 - here, n * chunk : n * chunk + chunk], theirs, (n,))
 
 
-def feature_kernel(i, nbr, lz, grad, keep, halo, wrows, *refs):
+def feature_kernel(i, nbr, lz, grad, keep, halo, kernel, *refs):
     out, field, view, acc = refs[-4:]
     ny = grad.shape[1]
     fill_field(i, grad, keep, halo, field)
@@ -221,14 +217,10 @@
         @pl.when(live)
         def _():
             fill_view(nbr, field, view, i, slot)
-            acc[...] = jnp.zeros_like(acc)
-
-            def offset(t, c2):
-                weights = wrows[pl.ds(pl.multiple_of(t * 3 * WIDTH, 3 * WIDTH), 3 * WIDTH), :]
-                acc[...] += jnp.dot(columns_at(view, t), weights, preferred_element_type=jnp.float32)
-                return c2
-
-            lax.fori_loop(0, 9, offset, 0)
+            weights = jnp.concatenate([kernel[k] for k in range(27)], axis=1)
+            acc[...] = lax.dot_general(
+                columns_of(view), weights, (((1,), (1,)), ((), ())), preferred_element_type=jnp.float32
+            )
 
             def emit(xl, c2):
                 x = EDGE * i + xl
@@ -365,14 +357,14 @@
     core, last = lax.optimization_barrier((core, grad[nx - 1 :] * keep[nx - 1 :]))
     top = shift(last, "gx", 1)
     bottom = shift(grad[:1] * keep[:1], "gx", -1)
-
-    def side(y):
-        return jnp.concatenate(
-            [top[:, y : y + 1], grad[:, y : y + 1] * keep[:, y : y + 1], bottom[:, y : y + 1]], axis=0
-        )
-
-    left = shift(side(ny - 1), "gy", 1)
-    right = shift(side(0), "gy", -1)
+    sides = [grad[:, y : y + 1] * keep[:, y : y + 1] for y in (0, ny - 1)]
+    top, bottom, keep, sides = lax.optimization_barrier((top, bottom, keep, sides))
+
+    def side(y, own):
+        return jnp.concatenate([top[:, y : y + 1], own, bottom[:, y : y + 1]], axis=0)
+
+    left = shift(side(ny - 1, sides[1]), "gy", 1)
+    right = shift(side(0, sides[0]), "gy", -1)
     terms = call(
         terms_kernel,
         "conv_terms",
@@ -381,7 +373,6 @@
         scalars=2,
         flops=2 * product,
     )(neighbours, leaf_z, grad, feat, keep)
-    wrows = jnp.transpose(kernel, (0, 2, 1)).reshape(27 * WIDTH, WIDTH)
     edges = (top, bottom, left, right)
     mine, theirs, halo = call(
         edge_kernel,
@@ -406,7 +397,7 @@
 
     def features_part(i, value, *before):
         late, value = lax.optimization_barrier((grad, value))
-        args = (neighbours, leaf_z, late, keep, halo, wrows)
+        args = (neighbours, leaf_z, late, keep, halo, kernel)
         return features_call(i, args, (field, view, acc), product, *before), value
 
     half = exchange(half, "gy")

time: 92 us -> 89.4 us (0.972)
  Pallas kernels: 24.1 us -> 16.8 us
  waiting for transfers between devices: 7.72 us -> 11.9 us
  other arithmetic: 4.01 us -> 5.47 us
  local copies, waits for them, and re-layouts: 6.77 us -> 5.58 us
    all_to_all x2, waiting for transfers between devices: 4.22 us -> 8.9 us  [exchange(): return lax.all_to_all(blocks, axis, 0, 0)]
    pallas_call x6, Pallas kernels: 13 us -> 8.56 us  [run(): pl.pallas_call(kernel, out_shape=out_shape, in_specs=[SMEM] * scalars + [...]
    pallas_call x2, Pallas kernels: 11 us -> 8.23 us  [features_call(): pl.pallas_call(lambda *refs: feature_kernel(i, *refs), grid=(1,), out_sha...]
    transpose x1 -> x0, local copies, waits for them, and re-layouts: 1.88 us -> none  [local(): wrows = jnp.transpose(kernel, (0, 2, 1)).reshape(27 * WIDTH, WIDTH)]
    unnamed x16 -> x20, local copies, waits for them, and re-layouts: 1.75 us -> 2.45 us
  transfers between devices with their start and end apart: 8 -> 8, of which waited for: 5 -> 4; matrix products, arithmetic and copies ran while one was open for 7% -> 5% of each run, Pallas kernels for 21% -> 14%
where the time goes in v5:
time: 89.4 us; the launch traced here: 88.7 us
  starting transfers between devices  30.2 us (34%)
  blocking collectives  17.9 us (20%)
  Pallas kernels  16.8 us (19%)
  waiting for transfers between devices  11.9 us (13%)
  local copies, waits for them, and re-layouts  5.58 us (6%)
  other arithmetic  5.47 us (6%)
  between operations  0.91 us (1%)
    all_to_all x1, blocking collectives, exchange(): return lax.all_to_all(blocks, axis, 0, 0)  17.9 us
    all_to_all x2, starting transfers between devices, exchange(): return lax.all_to_all(blocks, axis, 0, 0)  12.8 us
    ppermute x4, starting transfers between devices, shift(): return lax.ppermute(block, axis, pairs)  10.2 us
    all_to_all x2, waiting for transfers between devices, exchange(): return lax.all_to_all(blocks, axis, 0, 0)  8.9 us
    pallas_call x6, Pallas kernels, run(): pl.pallas_call(kernel, out_shape=out_shape, in_specs=[SMEM] * scalars + [...  8.56 us
    pallas_call x2, Pallas kernels, features_call(): pl.pallas_call(lambda *refs: feature_kernel(i, *refs), grid=(1,), out_sha...  8.23 us
    ppermute x1, starting transfers between devices, local(): other = lax.ppermute(total, 'dcn', [(0, 1), (1, 0)])  4.65 us
    ppermute x1, starting transfers between devices, local(): theirs = lax.ppermute(theirs, 'dcn', [(0, 1), (1, 0)])  2.61 us
  transfers between devices with their start and end apart: 8, of which 4 were waited for; matrix products, arithmetic and copies ran while one was open for 5% of the time, Pallas kernels for 14%

profile of v5, /device:TPU:1, one launch (start us, length us, event | category | flops | bytes accessed | tf_op | source)
XLA Modules:
  0.0 88.7 jit_solution(7988640928359524489)
XLA Ops:
  0.6 0.0 copy-start
  0.6 0.0 copy-start.8
  0.7 0.0 copy-start.9
  0.7 0.0 copy-start.5
  0.7 1.1 %convert_element_type.15 = bf16[1,16,16,2,8]{2,4,3,1,0:T(8,128)(2,1)S(1)} convert(s32[1,16,16,2,8]{2,4,3,1,0:T(8,128)} %param.8) | non-fusion elementwise | flops 4096 | bytes 24576 | tf_op jit(solution)/shard_map/convert_element_type | solution.py:339
  1.8 0.1 copy.17
  1.8 0.1 copy.16
  1.9 1.0 %bitcast_multiply_fusion = (bf16[1,16,2,8,128]{4,3,2,1,0:T(8,128)(2,1)S(1)}, bf16[1,16,2,8,128]{4,3,2,1,0:T(8,128)(2,1)S(1)}) fusion(bf16[1,16,16,2,8,128]{5,4,3,2,1,0:T(8,128)(2,1)} %param.7, bf16[16,2,8]{2,1,0:T(2,128)(2,1)S(1)} %copy.17, bf16[16,2,8]{2,1,0:T(2,128)(2,1)S(1)} %copy.16), kind=kLoop, calls=%fused_computation.4 | loop fusion | flops 65536 | bytes 263168 | tf_op jit(solution)/shard_map/mul | solution.py:359
  2.9 4.4 %collective-permute-start = (bf16[1,16,2,8,128]{4,3,2,1,0:T(8,128)(2,1)S(1)}, bf16[1,16,2,8,128]{4,3,2,1,0:T(8,128)(2,1)S(1)}, u32[]{:S(2)}, u32[]{:S(2)}) collective-permute-start(bf16[1,16,2,8,128]{4,3,2,1,0:T(8,128)(2,1)S(1)} %get-tuple-element.21), channel_id=1, source_target_pairs={{0,16},{16,32},{32,48},{48,64},{64,80},{80,96},{96,112},{1,17},{17... | collective-permute-start | bytes 196616 | tf_op jit(solution)/shard_map/ppermute | solution.py:352
  7.3 1.3 %collective-permute-start.1 = (bf16[1,16,2,8,128]{4,3,2,1,0:T(8,128)(2,1)S(1)}, bf16[1,16,2,8,128]{4,3,2,1,0:T(8,128)(2,1)S(1)}, u32[]{:S(2)}, u32[]{:S(2)}) collective-permute-start(bf16[1,16,2,8,128]{4,3,2,1,0:T(8,128)(2,1)S(1)} %get-tuple-element.40), channel_id=1, source_target_pairs={{16,0},{32,16},{48,32},{64,48},{80,64},{96,80},{112,96},{17,1},{33... | collective-permute-start | bytes 196616 | tf_op jit(solution)/shard_map/ppermute | solution.py:352
  8.6 0.9 %convert_bitcast_fusion = bf16[16,16,2,8]{1,3,2,0:T(8,128)(2,1)S(1)} fusion(s32[1,16,16,2,8]{2,4,3,1,0:T(8,128)} %param.8), kind=kLoop, calls=%fused_computation.11 | loop fusion | flops 4096 | bytes 24576 | tf_op jit(solution)/shard_map/convert_element_type | solution.py:339
  9.5 0.1 fusion.2
  9.6 0.2 copy.21
  9.8 0.1 copy.22
  9.9 0.2 copy.19
  10.1 0.1 copy.20
  10.2 1.6 %slice_multiply_fusion = (bf16[16,1,2,8,128]{4,3,2,1,0:T(8,128)(2,1)}, bf16[16,1,2,8,128]{4,3,2,1,0:T(8,128)(2,1)S(1)}) fusion(bf16[16,16,2,8,128]{4,3,2,1,0:T(8,128)(2,1)} %bitcast.17, bf16[16,2,8]{2,1,0:T(2,128)(2,1)S(1)} %copy.22, bf16[16,2,8]{2,1,0:T(2,128)(2,1)S(1)} %copy.20), kind=kLoop, calls=%fused_computation.2 | loop fusion | flops 65536 | bytes 263168 | tf_op jit(solution)/shard_map/mul | solution.py:360
  11.8 0.8 copy.18
  12.6 0.0 collective-permute-done.top
  12.6 0.0 collective-permute-done.1.bottom
  12.6 1.5 %broadcast_in_dim.25.keep.refs_3_ = bf16[16,16,2,8,128]{4,3,2,1,0:T(8,128)(2,1)S(1)} broadcast(bf16[16,16,2,8]{3,2,1,0:T(2,128)(2,1)} %copy.18), dimensions={0,1,2,3} | broadcast | bytes 1056768 | tf_op jit(solution)/shard_map/broadcast_in_dim | solution.py:339
  14.1 0.9 pad_maximum_fusion
  15.0 3.2 %collective-permute-start.2 = (bf16[18,1,2,8,128]{4,3,2,1,0:T(8,128)(2,1)S(1)}, bf16[18,1,2,8,128]{4,3,2,1,0:T(8,128)(2,1)S(1)}, u32[]{:S(2)}, u32[]{:S(2)}) collective-permute-start(bf16[18,1,2,8,128]{4,3,2,1,0:T(8,128)(2,1)S(1)} %pad_maximum_fusion), channel_id=1, source_target_pairs={{0,1},{1,2},{2,3},{3,4},{4,5},{5,6},{6,7},{7,8},{8,9},{9,10},{10,1... | collective-permute-start | bytes 221192 | tf_op jit(solution)/shard_map/ppermute | solution.py:352
  18.2 1.3 %collective-permute-start.3 = (bf16[18,1,2,8,128]{4,3,2,1,0:T(8,128)(2,1)S(1)}, bf16[18,1,2,8,128]{4,3,2,1,0:T(8,128)(2,1)S(1)}, u32[]{:S(2)}, u32[]{:S(2)}) collective-permute-start(bf16[18,1,2,8,128]{4,3,2,1,0:T(8,128)(2,1)S(1)} %pad_maximum_fusion.1), channel_id=1, source_target_pairs={{1,0},{2,1},{3,2},{4,3},{5,4},{6,5},{7,6},{8,7},{9,8},{10,9},{11,1... | collective-permute-start | bytes 221192 | tf_op jit(solution)/shard_map/ppermute | solution.py:352
  19.5 0.0 copy-done
  19.5 0.0 copy-done.8
  19.6 0.0 copy-done.9
  19.6 0.0 copy-done.5
  19.6 0.0 copy-start.6
  19.6 4.4 %conv_terms.1.before = f32[2,1792,128]{2,1,0:T(8,128)S(1)} custom-call(s32[1,2,2,2,27]{4,3,2,1,0:T(2,128)S(1)} %copy-done.8, s32[1,2,2,2]{3,2,1,0:T(2,128)S(1)} %copy-done.9, bf16[16,16,2,8,128]{4,3,2,1,0:T(8,128)(2,1)S(1)} %bitcast.18, bf16[16,16,2,8,128]{4,3,2,1,0:T(8,128)(2,1)S(1)} %bitcast.21, bf16[16,16,2,8,128]{4,3,2,1,0:T(8,128)(2,1)S(1)} %broadcast_in_dim.25.keep.refs_3_), custom_call_target="tpu_custom_call" | custom-call | flops 1811939328 | bytes 4194304 | tf_op jit(solution)/shard_map/conv_terms/pallas_call | solution.py:296
  24.0 0.0 collective-permute-done.2.left
  24.0 0.0 collective-permute-done.3.right
  24.0 0.0 copy-done.6
  24.0 2.1 %edge_terms.1 = (f32[1792,128]{1,0:T(8,128)S(1)}, s16[16,120,128]{2,1,0:T(8,128)(2,1)S(1)}, bf16[68,2,8,128]{3,2,1,0:T(8,128)(2,1)S(1)}) custom-call(s32[1,2,2,2,27]{4,3,2,1,0:T(2,128)S(1)} %copy-done.8, s32[1,2,2,2]{3,2,1,0:T(2,128)S(1)} %copy-done.9, s32[1]{0:T(128)} %bitcast.1.core, bf16[16,16,2,8,128]{4,3,2,1,0:T(8,128)(2,1)S(1)} %bitcast.22, ...), custom_call_target="tpu_custom_call" | custom-call | flops 226492416 | bytes 4194304 | tf_op jit(solution)/shard_map/edge_terms/pallas_call | solution.py:296
  26.1 0.0 copy-start.3
  26.1 2.6 %collective-permute-start.4 = (s16[16,120,128]{2,1,0:T(8,128)(2,1)S(1)}, s16[16,120,128]{2,1,0:T(8,128)(2,1)S(1)}, u32[]{:S(2)}, u32[]{:S(2)}) collective-permute-start(s16[16,120,128]{2,1,0:T(8,128)(2,1)S(1)} %get-tuple-element.28), channel_id=1, source_target_pairs={{0,128},{128,0},{1,129},{129,1},{2,130},{130,2},{3,131},{131,3},{4... | collective-permute-start | bytes 1474568 | tf_op jit(solution)/shard_map/ppermute | solution.py:395
  28.7 1.5 %collective-permute-done.4.theirs = s16[16,120,128]{2,1,0:T(8,128)(2,1)S(1)} collective-permute-done((s16[16,120,128]{2,1,0:T(8,128)(2,1)S(1)}, s16[16,120,128]{2,1,0:T(8,128)(2,1)S(1)}, u32[]{:S(2)}, u32[]{:S(2)}) %collective-permute-start.4) | collective-permute-done | bytes 491552 | tf_op jit(solution)/shard_map/ppermute | solution.py:395
  30.2 0.0 copy-start.1
  30.2 0.3 encode_half.1
  30.6 17.9 %all_to_all.15.c = s16[16,120,128]{2,1,0:T(8,128)(2,1)S(1)} all-to-all(s16[16,120,128]{2,1,0:T(8,128)(2,1)S(1)} %encode_half.1), channel_id=1, replica_groups=mesh['dcn'=2,'gx'=8,'gy'=16] {'gy'}, dimensions={0} | all-to-all | bytes 983040 | tf_op jit(solution)/shard_map/all_to_all | solution.py:332
  48.4 0.2 sum_piece.1
  48.6 0.0 copy-start.7
  48.6 0.7 copy-done.7
  49.3 9.3 %all-to-all-start.1 = ((s16[8,120,128]{2,1,0:T(8,128)(2,1)}), s16[8,120,128]{2,1,0:T(8,128)(2,1)S(1)}, u32[]{:S(2)}, u32[]{:S(2)}) async-start(s16[8,120,128]{2,1,0:T(8,128)(2,1)} %copy-done.7), calls=%async_computation.1 | async-start | bytes 491520 | tf_op jit(solution)/shard_map/all_to_all | solution.py:332
  58.6 0.0 copy-done.3
  58.6 0.0 copy-done.1
  58.6 4.1 %conv_features.2.refs_6_ = bf16[16,16,2,8,128]{4,3,2,1,0:T(8,128)(2,1)} custom-call(s32[1,2,2,2,27]{4,3,2,1,0:T(2,128)S(1)} %copy-done.8, s32[1,2,2,2]{3,2,1,0:T(2,128)S(1)} %copy-done.9, bf16[16,16,2,8,128]{4,3,2,1,0:T(8,128)(2,1)S(1)} %bitcast.19, bf16[16,16,2,8,128]{4,3,2,1,0:T(8,128)(2,1)S(1)} %broadcast_in_dim.25.keep.refs_3_, ...), custom_call_target="tpu_custom_call" | custom-call | flops 905969664 | bytes 4194304 | tf_op jit(solution)/shard_map/conv_features/pallas_call | solution.py:317
  62.7 5.1 %all-to-all-done.1.c = s16[8,120,128]{2,1,0:T(8,128)(2,1)S(1)} async-done(((s16[8,120,128]{2,1,0:T(8,128)(2,1)}), s16[8,120,128]{2,1,0:T(8,128)(2,1)S(1)}, u32[]{:S(2)}, u32[]{:S(2)}) %all-to-all-start.1) | async-done | bytes 245792 | tf_op jit(solution)/shard_map/all_to_all | solution.py:332
  67.8 0.2 sum_total.1
  68.0 0.0 copy-start.2
  68.0 0.8 copy-done.2
  68.8 3.6 %all-to-all-start.2 = ((s16[16,120,128]{2,1,0:T(8,128)(2,1)}), s16[16,120,128]{2,1,0:T(8,128)(2,1)S(1)}, u32[]{:S(2)}, u32[]{:S(2)}) async-start(s16[16,120,128]{2,1,0:T(8,128)(2,1)} %copy-done.2), calls=%async_computation.2 | async-start | bytes 983040 | tf_op jit(solution)/shard_map/all_to_all | solution.py:332
  72.4 0.0 copy-start.4
  72.4 0.9 %copy-done.4 = bf16[68,2,8,128]{3,2,1,0:T(8,128)(2,1)S(1)} copy-done((bf16[68,2,8,128]{3,2,1,0:T(8,128)(2,1)S(1)}, bf16[68,2,8,128]{3,2,1,0:T(8,128)(2,1)}, u32[]{:S(2)}) %copy-start.4) | copy-done | bytes 278552
  73.3 4.1 %conv_features.3 = bf16[16,16,2,8,128]{4,3,2,1,0:T(8,128)(2,1)} custom-call(s32[1,2,2,2,27]{4,3,2,1,0:T(2,128)S(1)} %copy-done.8, s32[1,2,2,2]{3,2,1,0:T(2,128)S(1)} %copy-done.9, bf16[16,16,2,8,128]{4,3,2,1,0:T(8,128)(2,1)S(1)} %bitcast.20, bf16[16,16,2,8,128]{4,3,2,1,0:T(8,128)(2,1)S(1)} %broadcast_in_dim.25.keep.refs_3_, ...), custom_call_target="tpu_custom_call", output_to_operand_aliasing={{}: (6, {})} | custom-call | flops 905969664 | bytes 4194304 | tf_op jit(solution)/shard_map/conv_features/pallas_call | solution.py:317
  77.4 3.8 %all-to-all-done.2.mine = s16[16,120,128]{2,1,0:T(8,128)(2,1)S(1)} async-done(((s16[16,120,128]{2,1,0:T(8,128)(2,1)}), s16[16,120,128]{2,1,0:T(8,128)(2,1)S(1)}, u32[]{:S(2)}, u32[]{:S(2)}) %all-to-all-start.2) | async-done | bytes 491552 | tf_op jit(solution)/shard_map/all_to_all | solution.py:332
  81.2 4.6 %collective-permute-start.5 = (s16[16,120,128]{2,1,0:T(8,128)(2,1)S(1)}, s16[16,120,128]{2,1,0:T(8,128)(2,1)S(1)}, u32[]{:S(2)}, u32[]{:S(2)}) collective-permute-start(s16[16,120,128]{2,1,0:T(8,128)(2,1)S(1)} %all-to-all-done.2.mine), channel_id=1, source_target_pairs={{0,128},{128,0},{1,129},{129,1},{2,130},{130,2},{3,131},{131,3},{4... | collective-permute-start | bytes 1474568 | tf_op jit(solution)/shard_map/ppermute | solution.py:410
  85.9 1.5 %collective-permute-done.5.theirs = s16[16,120,128]{2,1,0:T(8,128)(2,1)S(1)} collective-permute-done((s16[16,120,128]{2,1,0:T(8,128)(2,1)S(1)}, s16[16,120,128]{2,1,0:T(8,128)(2,1)S(1)}, u32[]{:S(2)}, u32[]{:S(2)}) %collective-permute-start.5) | collective-permute-done | bytes 491552 | tf_op jit(solution)/shard_map/ppermute | solution.py:410
  87.3 1.4 %decode_total.1 = f32[3456,128]{1,0:T(8,128)} custom-call(s32[1]{0:T(128)} %bitcast.1.core, s16[16,120,128]{2,1,0:T(8,128)(2,1)S(1)} %all-to-all-done.2.mine, s16[16,120,128]{2,1,0:T(8,128)(2,1)S(1)} %collective-permute-done.5.theirs), custom_call_target="tpu_custom_call" | custom-call | bytes 3145728 | tf_op jit(solution)/shard_map/decode_total/pallas_call | solution.py:296
  (3 shorter events, 0.0 us)
Async XLA Ops:
  0.6 18.9 %copy-start = (bf16[1,16,16,2,8,128]{5,4,3,2,1,0:T(8,128)(2,1)S(1)}, bf16[1,16,16,2,8,128]{5,4,3,2,1,0:T(8,128)(2,1)}, u32[]{:S(2)}) copy-start(bf16[1,16,16,2,8,128]{5,4,3,2,1,0:T(8,128)(2,1)} %param.7) | copy-start | bytes 3145732
  0.6 18.9 %copy-start.8 = (s32[1,2,2,2,27]{4,3,2,1,0:T(2,128)S(1)}, s32[1,2,2,2,27]{4,3,2,1,0:T(2,128)}, u32[]{:S(2)}) copy-start(s32[1,2,2,2,27]{4,3,2,1,0:T(2,128)} %refs_0_.3) | copy-start | bytes 2596
  0.7 18.9 %copy-start.9 = (s32[1,2,2,2]{3,2,1,0:T(2,128)S(1)}, s32[1,2,2,2]{3,2,1,0:T(2,128)}, u32[]{:S(2)}) copy-start(s32[1,2,2,2]{3,2,1,0:T(2,128)} %refs_1_.3) | copy-start | bytes 100
  0.7 18.9 %copy-start.5 = (bf16[1,16,16,2,8,128]{5,4,3,2,1,0:T(8,128)(2,1)S(1)}, bf16[1,16,16,2,8,128]{5,4,3,2,1,0:T(8,128)(2,1)}, u32[]{:S(2)}) copy-start(bf16[1,16,16,2,8,128]{5,4,3,2,1,0:T(8,128)(2,1)} %param.6) | copy-start | bytes 3145732
  2.9 9.7 %collective-permute-start = (bf16[1,16,2,8,128]{4,3,2,1,0:T(8,128)(2,1)S(1)}, bf16[1,16,2,8,128]{4,3,2,1,0:T(8,128)(2,1)S(1)}, u32[]{:S(2)}, u32[]{:S(2)}) collective-permute-start(bf16[1,16,2,8,128]{4,3,2,1,0:T(8,128)(2,1)S(1)} %get-tuple-element.21), channel_id=1, source_target_pairs={{0,16},{16,32},{32,48},{48,64},{64,80},{80,96},{96,112},{1,17},{17... | collective-permute-start | bytes 196616 | tf_op jit(solution)/shard_map/ppermute | solution.py:352
  7.3 5.3 %collective-permute-start.1 = (bf16[1,16,2,8,128]{4,3,2,1,0:T(8,128)(2,1)S(1)}, bf16[1,16,2,8,128]{4,3,2,1,0:T(8,128)(2,1)S(1)}, u32[]{:S(2)}, u32[]{:S(2)}) collective-permute-start(bf16[1,16,2,8,128]{4,3,2,1,0:T(8,128)(2,1)S(1)} %get-tuple-element.40), channel_id=1, source_target_pairs={{16,0},{32,16},{48,32},{64,48},{80,64},{96,80},{112,96},{17,1},{33... | collective-permute-start | bytes 196616 | tf_op jit(solution)/shard_map/ppermute | solution.py:352
  15.0 9.0 %collective-permute-start.2 = (bf16[18,1,2,8,128]{4,3,2,1,0:T(8,128)(2,1)S(1)}, bf16[18,1,2,8,128]{4,3,2,1,0:T(8,128)(2,1)S(1)}, u32[]{:S(2)}, u32[]{:S(2)}) collective-permute-start(bf16[18,1,2,8,128]{4,3,2,1,0:T(8,128)(2,1)S(1)} %pad_maximum_fusion), channel_id=1, source_target_pairs={{0,1},{1,2},{2,3},{3,4},{4,5},{5,6},{6,7},{7,8},{8,9},{9,10},{10,1... | collective-permute-start | bytes 221192 | tf_op jit(solution)/shard_map/ppermute | solution.py:352
  18.2 5.8 %collective-permute-start.3 = (bf16[18,1,2,8,128]{4,3,2,1,0:T(8,128)(2,1)S(1)}, bf16[18,1,2,8,128]{4,3,2,1,0:T(8,128)(2,1)S(1)}, u32[]{:S(2)}, u32[]{:S(2)}) collective-permute-start(bf16[18,1,2,8,128]{4,3,2,1,0:T(8,128)(2,1)S(1)} %pad_maximum_fusion.1), channel_id=1, source_target_pairs={{1,0},{2,1},{3,2},{4,3},{5,4},{6,5},{7,6},{8,7},{9,8},{10,9},{11,1... | collective-permute-start | bytes 221192 | tf_op jit(solution)/shard_map/ppermute | solution.py:352
  19.6 4.5 %copy-start.6 = (bf16[1,16,16,2,8,128]{5,4,3,2,1,0:T(8,128)(2,1)S(1)}, bf16[1,16,16,2,8,128]{5,4,3,2,1,0:T(8,128)(2,1)}, u32[]{:S(2)}) copy-start(bf16[1,16,16,2,8,128]{5,4,3,2,1,0:T(8,128)(2,1)} %param.6) | copy-start | bytes 3145732
  26.1 32.5 %copy-start.3 = (bf16[68,2,8,128]{3,2,1,0:T(8,128)(2,1)}, bf16[68,2,8,128]{3,2,1,0:T(8,128)(2,1)S(1)}, u32[]{:S(2)}) copy-start(bf16[68,2,8,128]{3,2,1,0:T(8,128)(2,1)S(1)} %get-tuple-element.31.refs_4_) | copy-start | bytes 835588
  26.1 4.1 %collective-permute-start.4 = (s16[16,120,128]{2,1,0:T(8,128)(2,1)S(1)}, s16[16,120,128]{2,1,0:T(8,128)(2,1)S(1)}, u32[]{:S(2)}, u32[]{:S(2)}) collective-permute-start(s16[16,120,128]{2,1,0:T(8,128)(2,1)S(1)} %get-tuple-element.28), channel_id=1, source_target_pairs={{0,128},{128,0},{1,129},{129,1},{2,130},{130,2},{3,131},{131,3},{4... | collective-permute-start | bytes 1474568 | tf_op jit(solution)/shard_map/ppermute | solution.py:395
  30.2 28.4 %copy-start.1 = (bf16[27,128,128]{2,1,0:T(8,128)(2,1)S(1)}, bf16[27,128,128]{2,1,0:T(8,128)(2,1)}, u32[]{:S(2)}) copy-start(bf16[27,128,128]{2,1,0:T(8,128)(2,1)} %refs_5_.3) | copy-start | bytes 2654212
  48.6 0.7 copy-start.7
  49.3 18.5 %all-to-all-start.1 = ((s16[8,120,128]{2,1,0:T(8,128)(2,1)}), s16[8,120,128]{2,1,0:T(8,128)(2,1)S(1)}, u32[]{:S(2)}, u32[]{:S(2)}) async-start(s16[8,120,128]{2,1,0:T(8,128)(2,1)} %copy-done.7), calls=%async_computation.1 | async-start | bytes 491520 | tf_op jit(solution)/shard_map/all_to_all | solution.py:332
  68.0 0.8 copy-start.2
  68.8 12.4 %all-to-all-start.2 = ((s16[16,120,128]{2,1,0:T(8,128)(2,1)}), s16[16,120,128]{2,1,0:T(8,128)(2,1)S(1)}, u32[]{:S(2)}, u32[]{:S(2)}) async-start(s16[16,120,128]{2,1,0:T(8,128)(2,1)} %copy-done.2), calls=%async_computation.2 | async-start | bytes 983040 | tf_op jit(solution)/shard_map/all_to_all | solution.py:332
  72.4 1.0 %copy-start.4 = (bf16[68,2,8,128]{3,2,1,0:T(8,128)(2,1)S(1)}, bf16[68,2,8,128]{3,2,1,0:T(8,128)(2,1)}, u32[]{:S(2)}) copy-start(bf16[68,2,8,128]{3,2,1,0:T(8,128)(2,1)} %copy-done.3) | copy-start | bytes 835588
  81.2 6.1 %collective-permute-start.5 = (s16[16,120,128]{2,1,0:T(8,128)(2,1)S(1)}, s16[16,120,128]{2,1,0:T(8,128)(2,1)S(1)}, u32[]{:S(2)}, u32[]{:S(2)}) collective-permute-start(s16[16,120,128]{2,1,0:T(8,128)(2,1)S(1)} %all-to-all-done.2.mine), channel_id=1, source_target_pairs={{0,128},{128,0},{1,129},{129,1},{2,130},{130,2},{3,131},{131,3},{4... | collective-permute-start | bytes 1474568 | tf_op jit(solution)/shard_map/ppermute | solution.py:410

commit v6 on v5

--- a/solution.py
+++ b/solution.py
@@ -40,17 +40,47 @@
     return jnp.logical_or(live_at(lz, i, 0, slot), live_at(lz, i, 1, slot))
 
 
-def kept(value, keep, live):
-    return value.astype(jnp.float32) * (keep.astype(jnp.float32) * live.astype(jnp.float32))
-
-
-def fill_field(i, grad, keep, halo, field):
+def kept(value, mask, live):
+    return value.astype(jnp.float32) * (mask * live.astype(jnp.float32))
+
+
+def mask_of(occ, x, slot, spots):
+    tile = occ[x, slot].astype(jnp.float32)
+    return [jnp.broadcast_to(tile[:, y : y + 1], (EDGE, WIDTH)) for y in spots]
+
+
+def pack_kernel(occ, first, last, start, end, top, bottom, left, right):
+    nx, ny = occ.shape[0], occ.shape[3]
+    for x, source, target in ((0, first, bottom), (nx - 1, last, top)):
+        for slot in range(2):
+            for y, mask in enumerate(mask_of(occ, x, slot, range(ny))):
+                target[0, y, slot] = (source[0, y, slot].astype(jnp.float32) * mask).astype(jnp.bfloat16)
+    for x in range(nx):
+        for slot in range(2):
+            low, high = mask_of(occ, x, slot, (0, ny - 1))
+            right[x, 0, slot] = (start[x, 0, slot].astype(jnp.float32) * low).astype(jnp.bfloat16)
+            left[x, 0, slot] = (end[x, 0, slot].astype(jnp.float32) * high).astype(jnp.bfloat16)
+
+
+def sides_kernel(top, bottom, left, right, left_side, right_side):
+    nx, ny = left.shape[0], top.shape[1]
+    for own, side, y in ((left, left_side, ny - 1), (right, right_side, 0)):
+        side[0, 0] = top[0, y]
+        side[1 : nx + 1] = own[...]
+        side[nx + 1, 0] = bottom[0, y]
+
+
+def fill_field(i, grad, occ, halo, field, masks):
     nx, ny = grad.shape[0], grad.shape[1]
     low, high = (1, VIEW) if i == 0 else (0, VIEW - 1)
 
     def fill(r, carry):
         x = EDGE * i - 1 + r
-        field[r, 1 : ny + 1, 0:2] = grad[x].astype(jnp.float32) * keep[x].astype(jnp.float32)
+        values = grad[x].astype(jnp.float32)
+        for slot in range(2):
+            for y, mask in enumerate(mask_of(occ, x, slot, range(ny))):
+                masks[r, y, slot] = mask
+                field[r, y + 1, slot] = values[y, slot] * mask
         return carry
 
     lax.fori_loop(low, high, fill, 0)
@@ -99,11 +129,11 @@
     return jnp.concatenate(pieces, axis=1)
 
 
-def pair_row(lz, feat, keep, i, x, slot):
+def pair_row(lz, feat, masks, i, x, slot):
     pair = []
     for j in range(2):
-        spot = (x, slice(EDGE * j, EDGE * j + EDGE), slot)
-        pair.append(kept(feat[spot], keep[spot], live_at(lz, i, j, slot)))
+        span = slice(EDGE * j, EDGE * j + EDGE)
+        pair.append(kept(feat[x, span, slot], masks[span], live_at(lz, i, j, slot)))
     return jnp.concatenate(pair, axis=1).reshape(EDGE * ROWS, WIDTH)
 
 
@@ -115,33 +145,33 @@
             total[core, start : start + 64] += part[s * 64 : s * 64 + 64, c * WIDTH : (c + 1) * WIDTH]
 
 
-def terms_kernel(nbr, lz, grad, feat, keep, terms, field, view, own):
-    terms[...] = jnp.zeros_like(terms)
-    for i in range(2):
-        fill_field(i, grad, keep, None, field)
-
-        def unit(slot, carry, i=i):
-            @pl.when(pair_live(lz, i, slot))
-            def _():
-                fill_view(nbr, field, view, i, slot)
-
-                def own_rows(xl, c2):
-                    own[xl] = pair_row(lz, feat, keep, i, EDGE * i + xl, slot).astype(jnp.bfloat16)
-                    return c2
-
-                lax.fori_loop(0, EDGE, own_rows, 0)
-                own_t = own[...].reshape(UNIT, WIDTH).T
-
-                part = jnp.dot(own_t, columns_of(view), preferred_element_type=jnp.float32)
-                for k in range(0, 27, 3):
-                    add_terms(terms, k, part[:, k * WIDTH : (k + 3) * WIDTH])
-
-            return carry
-
-        lax.fori_loop(0, 2, unit, 0)
-
-
-def edge_kernel(nbr, lz, core, feat, keep, top, bottom, left, right, before, mine, theirs, halo, total, strip, side, row_view, side_view):
+def terms_kernel(i, nbr, lz, grad, feat, occ, *refs):
+    *before, terms, field, masks, view, own = refs
+    terms[...] = before[0][...] if before else jnp.zeros_like(terms)
+    fill_field(i, grad, occ, None, field, masks)
+
+    def unit(slot, carry):
+        @pl.when(pair_live(lz, i, slot))
+        def _():
+            fill_view(nbr, field, view, i, slot)
+
+            def own_rows(xl, c2):
+                rows = pair_row(lz, feat, masks[xl + 1, :, slot], i, EDGE * i + xl, slot)
+                own[xl] = rows.astype(jnp.bfloat16)
+                return c2
+
+            lax.fori_loop(0, EDGE, own_rows, 0)
+            own_t = own[...].reshape(UNIT, WIDTH).T
+            part = jnp.dot(own_t, columns_of(view), preferred_element_type=jnp.float32)
+            for k in range(0, 27, 3):
+                add_terms(terms, k, part[:, k * WIDTH : (k + 3) * WIDTH])
+
+        return carry
+
+    lax.fori_loop(0, 2, unit, 0)
+
+
+def edge_kernel(nbr, lz, core, feat, occ, top, bottom, left, right, before, mine, theirs, halo, total, strip, side, row_view, side_view):
     nx, ny = feat.shape[0], feat.shape[1]
     total[...] = before[...]
     halo[0:ny] = top[0]
@@ -172,7 +202,9 @@
             for c in range(3):
                 both = jnp.concatenate([halves[0][c], halves[1][c]], axis=1)
                 row_view[c, start : start + count] = both.astype(jnp.bfloat16)
-        own_t = pair_row(lz, feat, keep, i, (0, nx - 1)[i], slot).T.astype(jnp.bfloat16)
+        x = (0, nx - 1)[i]
+        masks = jnp.stack(mask_of(occ, x, slot, range(ny)))
+        own_t = pair_row(lz, feat, masks, i, x, slot).T.astype(jnp.bfloat16)
         for b in range(3):
             pieces = [row_view[c, 2 - b : 2 - b + EDGE].reshape(EDGE * ROWS, WIDTH) for c in range(3)]
             product(own_t, pieces, 18 - 18 * i + 3 * b)
@@ -182,8 +214,10 @@
                 moved = shifted(*(side[j, span, s] for s in slots_of(nbr, i, j, slot, 9 * p + 6 * j)))
                 for c in range(3):
                     side_view[c, start : start + count] = moved[c]
-            spot = (slice(EDGE * i, EDGE * i + EDGE), (0, ny - 1)[j], slot)
-            own_t = kept(feat[spot], keep[spot], live_at(lz, i, j, slot)).reshape(EDGE * EDGE, WIDTH)
+            y = (0, ny - 1)[j]
+            masks = jnp.stack([mask_of(occ, EDGE * i + xl, slot, (y,))[0] for xl in range(EDGE)])
+            rows = feat[EDGE * i : EDGE * i + EDGE, y, slot]
+            own_t = kept(rows, masks, live_at(lz, i, j, slot)).reshape(EDGE * EDGE, WIDTH)
             own_t = own_t.T.astype(jnp.bfloat16)
             for a in range(3):
                 pieces = [side_view[c, 2 - a : 2 - a + EDGE].reshape(EDGE * EDGE, WIDTH) for c in range(3)]
@@ -206,10 +240,10 @@
         encode(total[1 - here, n * chunk : n * chunk + chunk], theirs, (n,))
 
 
-def feature_kernel(i, nbr, lz, grad, keep, halo, kernel, *refs):
-    out, field, view, acc = refs[-4:]
+def feature_kernel(i, nbr, lz, grad, occ, halo, kernel, *refs):
+    out, field, masks, view, acc = refs[-5:]
     ny = grad.shape[1]
-    fill_field(i, grad, keep, halo, field)
+    fill_field(i, grad, occ, halo, field, masks)
 
     def unit(slot, carry):
         live = pair_live(lz, i, slot)
@@ -223,12 +257,11 @@
             )
 
             def emit(xl, c2):
-                x = EDGE * i + xl
                 block = acc[pl.ds(pl.multiple_of(xl * EDGE * ROWS, EDGE * ROWS), EDGE * ROWS), :]
                 block = block.reshape(EDGE, 2, EDGE, WIDTH)
                 for j in range(2):
                     span = slice(EDGE * j, EDGE * j + EDGE)
-                    value = kept(block[:, j], keep[x, span, slot], live_at(lz, i, j, slot))
+                    value = kept(block[:, j], masks[xl + 1, span, slot], live_at(lz, i, j, slot))
                     out[xl, span, slot] = value.astype(jnp.bfloat16)
                 return c2
 
@@ -328,6 +361,25 @@
     )(*args)
 
 
+def pack_edges(occ, grad):
+    nx, ny = grad.shape[0], grad.shape[1]
+    row = (1,) + grad.shape[1:]
+    side = (nx, 1) + grad.shape[2:]
+    places = ((row, (0, 0)), (row, (nx - 1, 0)), (side, (0, 0)), (side, (0, ny - 1)))
+    specs = [pl.BlockSpec(shape, lambda g, at=at: at + (0, 0, 0)) for shape, at in places]
+    shapes = [jax.ShapeDtypeStruct(shape, jnp.bfloat16) for shape in (row, row, side, side)]
+    whole = [pl.BlockSpec(shape.shape, lambda g: (0, 0, 0, 0, 0)) for shape in shapes]
+    return pl.pallas_call(
+        pack_kernel,
+        grid=(1,),
+        out_shape=shapes,
+        in_specs=[pl.BlockSpec(occ.shape, lambda g: (0, 0, 0, 0))] + specs,
+        out_specs=whole,
+        cost_estimate=pl.CostEstimate(flops=0, bytes_accessed=1 << 20, transcendentals=0),
+        name="pack_edges",
+    )(occ, grad, grad, grad, grad)
+
+
 def exchange(blocks, axis):
     return lax.all_to_all(blocks, axis, 0, 0)
 
@@ -336,11 +388,12 @@
     nx, ny = grad_out.shape[1], grad_out.shape[2]
     grad = grad_out[0]
     feat = features[0]
-    keep = jnp.broadcast_to(occupancy[0].astype(jnp.bfloat16)[..., None], grad.shape)
+    occ = jnp.transpose(occupancy[0], (0, 2, 3, 1))
     gx, gy = lax.axis_size("gx"), lax.axis_size("gy")
     core = lax.axis_index("dcn").astype(jnp.int32).reshape(1)
     scale = 1.0 / math.sqrt(lax.axis_size("dcn") * gx * gy * nx * ny * 2 * EDGE)
     field = pltpu.VMEM((VIEW, ny + 2, 3, EDGE, WIDTH), jnp.float32)
+    masks = pltpu.VMEM((VIEW, ny, 2, EDGE, WIDTH), jnp.float32)
     view = pltpu.VMEM((3, VIEW, VIEW, ROWS, WIDTH), jnp.bfloat16)
     own = pltpu.VMEM((EDGE, EDGE * ROWS, WIDTH), jnp.bfloat16)
     acc = pltpu.VMEM((UNIT, WIDTH), jnp.float32)
@@ -354,25 +407,27 @@
     def coded(count):
         return jax.ShapeDtypeStruct((count, PADDED // gy + EDGE, WIDTH), jnp.int16)
 
-    core, last = lax.optimization_barrier((core, grad[nx - 1 :] * keep[nx - 1 :]))
+    def terms_of(i, *before):
+        return call(
+            lambda *refs: terms_kernel(i, *refs),
+            "conv_terms",
+            jax.ShapeDtypeStruct((2, PADDED, WIDTH), jnp.float32),
+            (field, masks, view, own),
+            scalars=2,
+            flops=product,
+        )(neighbours, leaf_z, grad, feat, occ, *before)
+
+    core, packed = lax.optimization_barrier((core, pack_edges(occ, grad)))
+    last, first, end, start = packed
     top = shift(last, "gx", 1)
-    bottom = shift(grad[:1] * keep[:1], "gx", -1)
-    sides = [grad[:, y : y + 1] * keep[:, y : y + 1] for y in (0, ny - 1)]
-    top, bottom, keep, sides = lax.optimization_barrier((top, bottom, keep, sides))
-
-    def side(y, own):
-        return jnp.concatenate([top[:, y : y + 1], own, bottom[:, y : y + 1]], axis=0)
-
-    left = shift(side(ny - 1, sides[1]), "gy", 1)
-    right = shift(side(0, sides[0]), "gy", -1)
-    terms = call(
-        terms_kernel,
-        "conv_terms",
-        jax.ShapeDtypeStruct((2, PADDED, WIDTH), jnp.float32),
-        (field, view, own),
-        scalars=2,
-        flops=2 * product,
-    )(neighbours, leaf_z, grad, feat, keep)
+    bottom = shift(first, "gx", -1)
+    terms = terms_of(0)
+    top, bottom, terms = lax.optimization_barrier((top, bottom, terms))
+    side = jax.ShapeDtypeStruct((nx + 2, 1, 2, EDGE, WIDTH), jnp.bfloat16)
+    end, start = call(sides_kernel, "pack_sides", (side, side), nbytes=1 << 17)(top, bottom, end, start)
+    left = shift(end, "gy", 1)
+    right = shift(start, "gy", -1)
+    terms = terms_of(1, terms)
     edges = (top, bottom, left, right)
     mine, theirs, halo = call(
         edge_kernel,
@@ -391,14 +446,14 @@
         ),
         scalars=3,
         flops=product // 4,
-    )(neighbours, leaf_z, core, feat, keep, *edges, terms)
+    )(neighbours, leaf_z, core, feat, occ, *edges, terms)
     theirs = lax.ppermute(theirs, "dcn", [(0, 1), (1, 0)])
     half = call(encode_half_kernel, "encode_half", coded(gy), nbytes=2 << 20)(mine, theirs)
 
     def features_part(i, value, *before):
         late, value = lax.optimization_barrier((grad, value))
-        args = (neighbours, leaf_z, late, keep, halo, kernel)
-        return features_call(i, args, (field, view, acc), product, *before), value
+        args = (neighbours, leaf_z, late, occ, halo, kernel)
+        return features_call(i, args, (field, masks, view, acc), product, *before), value
 
     half = exchange(half, "gy")
     piece = call(lambda c, o: sum_kernel(1.0, c, o), "sum_piece", coded(gx), nbytes=1 << 20)(half)

time: 89.4 us -> 86.4 us (0.966)
  Pallas kernels: 16.8 us -> 25.1 us
  local copies, waits for them, and re-layouts: 5.58 us -> 0.03 us
  other arithmetic: 5.47 us -> 0 us
    pallas_call x6 -> x8, Pallas kernels: 8.56 us -> 12.9 us  [run(): pl.pallas_call(kernel, out_shape=out_shape, in_specs=[SMEM] * scalars + [...]
    mul x2 -> x0, other arithmetic: 2.62 us -> none  [the longest x1 1.62 us: local(): sides = [grad[:, y:y + 1] * keep[:, y:y + 1] for y in (0, ny - 1)]]
    unnamed x20 -> x16, local copies, waits for them, and re-layouts: 2.45 us -> 0.03 us
    pallas_call x0 -> x1, Pallas kernels: none -> 2.06 us  [pack_edges(): pl.pallas_call(pack_kernel, grid=(1,), out_shape=shapes, in_specs=[pl.Blo...]
    convert_element_type x2 -> x0, other arithmetic: 1.98 us -> none  [local(): occupancy[0].astype(jnp.bfloat16)[..., None]]
    pallas_call x2, Pallas kernels: 8.23 us -> 10.2 us  [features_call(): pl.pallas_call(lambda *refs: feature_kernel(i, *refs), grid=(1,), out_sha...]
    broadcast_in_dim x4 -> x0, local copies, waits for them, and re-layouts: 1.69 us -> none  [local(): jnp.broadcast_to(occupancy[0].astype(jnp.bfloat16)[..., None], grad.shape)]
    all_to_all x2, waiting for transfers between devices: 8.9 us -> 7.93 us  [exchange(): return lax.all_to_all(blocks, axis, 0, 0)]
  transfers between devices with their start and end apart: 8 -> 8, of which waited for: 4 -> 6; matrix products, arithmetic and copies ran while one was open for 5% -> 0% of each run, Pallas kernels for 14% -> 20%
where the time goes in v6:
time: 86.4 us; the launch traced here: 86 us
  starting transfers between devices  30.5 us (35%)
  Pallas kernels  25.1 us (29%)
  blocking collectives  17.9 us (21%)
  waiting for transfers between devices  11.6 us (13%)
    all_to_all x1, blocking collectives, exchange(): return lax.all_to_all(blocks, axis, 0, 0)  17.9 us
    pallas_call x8, Pallas kernels, run(): pl.pallas_call(kernel, out_shape=out_shape, in_specs=[SMEM] * scalars + [...  12.9 us
    all_to_all x2, starting transfers between devices, exchange(): return lax.all_to_all(blocks, axis, 0, 0)  12.3 us
    pallas_call x2, Pallas kernels, features_call(): pl.pallas_call(lambda *refs: feature_kernel(i, *refs), grid=(1,), out_sha...  10.2 us
    ppermute x4, starting transfers between devices, shift(): return lax.ppermute(block, axis, pairs)  10.2 us
    all_to_all x2, waiting for transfers between devices, exchange(): return lax.all_to_all(blocks, axis, 0, 0)  7.93 us
    ppermute x1, starting transfers between devices, local(): other = lax.ppermute(total, 'dcn', [(0, 1), (1, 0)])  4.65 us
    ppermute x1, starting transfers between devices, local(): theirs = lax.ppermute(theirs, 'dcn', [(0, 1), (1, 0)])  3.44 us
  transfers between devices with their start and end apart: 8, of which 6 were waited for; matrix products, arithmetic and copies ran while one was open for 0% of the time, Pallas kernels for 20%

profile of v6, /device:TPU:1, one launch (start us, length us, event | category | flops | bytes accessed | tf_op | source)
XLA Modules:
  0.0 86.0 jit_solution(17712909776928900288)
XLA Ops:
  0.6 0.0 copy-start
  0.6 0.0 copy-start.1
  0.7 0.0 copy-start.2
  0.7 0.0 copy-start.4
  0.7 0.0 copy-start.7
  0.7 2.1 %pack_edges.1 = (bf16[1,16,2,8,128]{4,3,2,1,0:T(8,128)(2,1)}, bf16[1,16,2,8,128]{4,3,2,1,0:T(8,128)(2,1)}, bf16[16,1,2,8,128]{4,3,2,1,0:T(8,128)(2,1)}, bf16[16,1,2,8,128]{4,3,2,1,0:T(8,128)(2,1)}) custom-call(s32[16,2,8,16]{3,2,1,0:T(8,128)} %bitcast.19, bf16[16,16,2,8,128]{4,3,2,1,0:T(8,128)(2,1)} %bitcast.8, bf16[16,16,2,8,128]{4,3,2,1,0:T(8,128)(2,1)} %bitcast.9, ...), custom_call_target="tpu_custom_call" | custom-call | bytes 1048576 | tf_op jit(solution)/shard_map/pack_edges/pallas_call | solution.py:372
  2.8 4.4 %collective-permute-start = (bf16[1,16,2,8,128]{4,3,2,1,0:T(8,128)(2,1)}, bf16[1,16,2,8,128]{4,3,2,1,0:T(8,128)(2,1)S(1)}, u32[]{:S(2)}, u32[]{:S(2)}) collective-permute-start(bf16[1,16,2,8,128]{4,3,2,1,0:T(8,128)(2,1)} %get-tuple-element.32), channel_id=1, source_target_pairs={{0,16},{16,32},{32,48},{48,64},{64,80},{80,96},{96,112},{1,17},{17... | collective-permute-start | bytes 196616 | tf_op jit(solution)/shard_map/ppermute | solution.py:405
  7.1 1.3 %collective-permute-start.1 = (bf16[1,16,2,8,128]{4,3,2,1,0:T(8,128)(2,1)}, bf16[1,16,2,8,128]{4,3,2,1,0:T(8,128)(2,1)S(1)}, u32[]{:S(2)}, u32[]{:S(2)}) collective-permute-start(bf16[1,16,2,8,128]{4,3,2,1,0:T(8,128)(2,1)} %get-tuple-element.33), channel_id=1, source_target_pairs={{16,0},{32,16},{48,32},{64,48},{80,64},{96,80},{112,96},{17,1},{33... | collective-permute-start | bytes 196616 | tf_op jit(solution)/shard_map/ppermute | solution.py:405
  8.4 0.0 copy-done
  8.4 0.0 copy-done.1
  8.4 0.0 copy-done.2
  8.4 0.0 copy-done.4
  8.5 0.0 copy-done.7
  8.5 0.0 copy-start.5
  8.5 0.0 copy-start.6
  8.5 3.6 %conv_terms.2.refs_5_ = f32[2,1792,128]{2,1,0:T(8,128)S(1)} custom-call(s32[1,2,2,2,27]{4,3,2,1,0:T(2,128)S(1)} %copy-done.4, s32[1,2,2,2]{3,2,1,0:T(2,128)S(1)} %copy-done.7, bf16[16,16,2,8,128]{4,3,2,1,0:T(8,128)(2,1)S(1)} %bitcast.12, bf16[16,16,2,8,128]{4,3,2,1,0:T(8,128)(2,1)S(1)} %bitcast.16, s32[16,2,8,16]{3,2,1,0:T(8,128)S(1)} %bitcast.20), custom_call_target="tpu_custom_call" | custom-call | flops 905969664 | bytes 4194304 | tf_op jit(solution)/shard_map/conv_terms/pallas_call | solution.py:329
  12.1 0.0 collective-permute-done.top
  12.1 0.5 collective-permute-done.1.bottom
  12.5 0.0 copy-done.5
  12.5 0.0 copy-done.6
  12.5 3.2 %collective-permute-start.2 = (bf16[18,1,2,8,128]{4,3,2,1,0:T(8,128)(2,1)S(1)}, bf16[18,1,2,8,128]{4,3,2,1,0:T(8,128)(2,1)S(1)}, u32[]{:S(2)}, u32[]{:S(2)}) collective-permute-start(bf16[18,1,2,8,128]{4,3,2,1,0:T(8,128)(2,1)S(1)} %get-tuple-element.38), channel_id=1, source_target_pairs={{0,1},{1,2},{2,3},{3,4},{4,5},{5,6},{6,7},{7,8},{8,9},{9,10},{10,1... | collective-permute-start | bytes 221192 | tf_op jit(solution)/shard_map/ppermute | solution.py:405
  15.8 1.3 %collective-permute-start.3 = (bf16[18,1,2,8,128]{4,3,2,1,0:T(8,128)(2,1)S(1)}, bf16[18,1,2,8,128]{4,3,2,1,0:T(8,128)(2,1)S(1)}, u32[]{:S(2)}, u32[]{:S(2)}) collective-permute-start(bf16[18,1,2,8,128]{4,3,2,1,0:T(8,128)(2,1)S(1)} %get-tuple-element.39), channel_id=1, source_target_pairs={{1,0},{2,1},{3,2},{4,3},{5,4},{6,5},{7,6},{8,7},{9,8},{10,9},{11,1... | collective-permute-start | bytes 221192 | tf_op jit(solution)/shard_map/ppermute | solution.py:405
  17.1 3.6 %conv_terms.3.before = f32[2,1792,128]{2,1,0:T(8,128)S(1)} custom-call(s32[1,2,2,2,27]{4,3,2,1,0:T(2,128)S(1)} %copy-done.4, s32[1,2,2,2]{3,2,1,0:T(2,128)S(1)} %copy-done.7, bf16[16,16,2,8,128]{4,3,2,1,0:T(8,128)(2,1)S(1)} %bitcast.13, bf16[16,16,2,8,128]{4,3,2,1,0:T(8,128)(2,1)S(1)} %bitcast.17, s32[16,2,8,16]{3,2,1,0:T(8,128)S(1)} %bitcast.21, ...), custom_call_target="tpu_custom_call" | custom-call | flops 905969664 | bytes 4194304 | tf_op jit(solution)/shard_map/conv_terms/pallas_call | solution.py:329
  20.6 0.0 collective-permute-done.2.left
  20.6 0.2 collective-permute-done.3.right
  20.9 2.2 %edge_terms.1 = (f32[1792,128]{1,0:T(8,128)S(1)}, s16[16,120,128]{2,1,0:T(8,128)(2,1)S(1)}, bf16[68,2,8,128]{3,2,1,0:T(8,128)(2,1)S(1)}) custom-call(s32[1,2,2,2,27]{4,3,2,1,0:T(2,128)S(1)} %copy-done.4, s32[1,2,2,2]{3,2,1,0:T(2,128)S(1)} %copy-done.7, s32[1]{0:T(128)} %bitcast.1.core, bf16[16,16,2,8,128]{4,3,2,1,0:T(8,128)(2,1)S(1)} %bitcast.18, ...), custom_call_target="tpu_custom_call" | custom-call | flops 226492416 | bytes 4194304 | tf_op jit(solution)/shard_map/edge_terms/pallas_call | solution.py:329
  23.1 3.4 %collective-permute-start.4 = (s16[16,120,128]{2,1,0:T(8,128)(2,1)S(1)}, s16[16,120,128]{2,1,0:T(8,128)(2,1)S(1)}, u32[]{:S(2)}, u32[]{:S(2)}) collective-permute-start(s16[16,120,128]{2,1,0:T(8,128)(2,1)S(1)} %get-tuple-element.42), channel_id=1, source_target_pairs={{0,128},{128,0},{1,129},{129,1},{2,130},{130,2},{3,131},{131,3},{4... | collective-permute-start | bytes 1474568 | tf_op jit(solution)/shard_map/ppermute | solution.py:450
  26.5 1.5 %collective-permute-done.4.theirs = s16[16,120,128]{2,1,0:T(8,128)(2,1)S(1)} collective-permute-done((s16[16,120,128]{2,1,0:T(8,128)(2,1)S(1)}, s16[16,120,128]{2,1,0:T(8,128)(2,1)S(1)}, u32[]{:S(2)}, u32[]{:S(2)}) %collective-permute-start.4) | collective-permute-done | bytes 491552 | tf_op jit(solution)/shard_map/ppermute | solution.py:450
  28.0 0.0 copy-start.3
  28.0 0.3 encode_half.1
  28.3 17.9 %all_to_all.15.c = s16[16,120,128]{2,1,0:T(8,128)(2,1)S(1)} all-to-all(s16[16,120,128]{2,1,0:T(8,128)(2,1)S(1)} %encode_half.1), channel_id=1, replica_groups=mesh['dcn'=2,'gx'=8,'gy'=16] {'gy'}, dimensions={0} | all-to-all | bytes 983040 | tf_op jit(solution)/shard_map/all_to_all | solution.py:384
  46.2 0.9 %sum_piece.1 = s16[8,120,128]{2,1,0:T(8,128)(2,1)} custom-call(s16[16,120,128]{2,1,0:T(8,128)(2,1)S(1)} %all_to_all.15.c), custom_call_target="tpu_custom_call" | custom-call | bytes 1048576 | tf_op jit(solution)/shard_map/sum_piece/pallas_call | solution.py:329
  47.1 8.7 %all-to-all-start.1 = ((s16[8,120,128]{2,1,0:T(8,128)(2,1)}), s16[8,120,128]{2,1,0:T(8,128)(2,1)S(1)}, u32[]{:S(2)}, u32[]{:S(2)}) async-start(s16[8,120,128]{2,1,0:T(8,128)(2,1)} %sum_piece.1), calls=%async_computation.1 | async-start | bytes 491520 | tf_op jit(solution)/shard_map/all_to_all | solution.py:384
  55.8 0.0 copy-done.3
  55.8 5.1 %conv_features.2.refs_6_ = bf16[16,16,2,8,128]{4,3,2,1,0:T(8,128)(2,1)} custom-call(s32[1,2,2,2,27]{4,3,2,1,0:T(2,128)S(1)} %copy-done.4, s32[1,2,2,2]{3,2,1,0:T(2,128)S(1)} %copy-done.7, bf16[16,16,2,8,128]{4,3,2,1,0:T(8,128)(2,1)S(1)} %bitcast.14, s32[16,2,8,16]{3,2,1,0:T(8,128)S(1)} %bitcast.23, bf16[68,2,8,128]{3,2,1,0:T(8,128)(2,1)S(1)} %get-tuple-element.45.refs_4_, ...), custom_call_target="tpu_custom_call" | custom-call | flops 905969664 | bytes 4194304 | tf_op jit(solution)/shard_map/conv_features/pallas_call | solution.py:350
  60.9 4.2 %all-to-all-done.1.c = s16[8,120,128]{2,1,0:T(8,128)(2,1)S(1)} async-done(((s16[8,120,128]{2,1,0:T(8,128)(2,1)}), s16[8,120,128]{2,1,0:T(8,128)(2,1)S(1)}, u32[]{:S(2)}, u32[]{:S(2)}) %all-to-all-start.1) | async-done | bytes 245792 | tf_op jit(solution)/shard_map/all_to_all | solution.py:384
  65.1 0.9 %sum_total.1 = s16[16,120,128]{2,1,0:T(8,128)(2,1)} custom-call(s16[8,120,128]{2,1,0:T(8,128)(2,1)S(1)} %all-to-all-done.1.c), custom_call_target="tpu_custom_call" | custom-call | bytes 1048576 | tf_op jit(solution)/shard_map/sum_total/pallas_call | solution.py:329
  66.0 3.6 %all-to-all-start.2 = ((s16[16,120,128]{2,1,0:T(8,128)(2,1)}), s16[16,120,128]{2,1,0:T(8,128)(2,1)S(1)}, u32[]{:S(2)}, u32[]{:S(2)}) async-start(s16[16,120,128]{2,1,0:T(8,128)(2,1)} %sum_total.1), calls=%async_computation.2 | async-start | bytes 983040 | tf_op jit(solution)/shard_map/all_to_all | solution.py:384
  69.6 5.1 %conv_features.3 = bf16[16,16,2,8,128]{4,3,2,1,0:T(8,128)(2,1)} custom-call(s32[1,2,2,2,27]{4,3,2,1,0:T(2,128)S(1)} %copy-done.4, s32[1,2,2,2]{3,2,1,0:T(2,128)S(1)} %copy-done.7, bf16[16,16,2,8,128]{4,3,2,1,0:T(8,128)(2,1)S(1)} %bitcast.15, s32[16,2,8,16]{3,2,1,0:T(8,128)S(1)} %bitcast.24, ...), custom_call_target="tpu_custom_call", output_to_operand_aliasing={{}: (6, {})} | custom-call | flops 905969664 | bytes 4194304 | tf_op jit(solution)/shard_map/conv_features/pallas_call | solution.py:350
  74.7 3.8 %all-to-all-done.2.mine = s16[16,120,128]{2,1,0:T(8,128)(2,1)S(1)} async-done(((s16[16,120,128]{2,1,0:T(8,128)(2,1)}), s16[16,120,128]{2,1,0:T(8,128)(2,1)S(1)}, u32[]{:S(2)}, u32[]{:S(2)}) %all-to-all-start.2) | async-done | bytes 491552 | tf_op jit(solution)/shard_map/all_to_all | solution.py:384
  78.4 4.6 %collective-permute-start.5 = (s16[16,120,128]{2,1,0:T(8,128)(2,1)S(1)}, s16[16,120,128]{2,1,0:T(8,128)(2,1)S(1)}, u32[]{:S(2)}, u32[]{:S(2)}) collective-permute-start(s16[16,120,128]{2,1,0:T(8,128)(2,1)S(1)} %all-to-all-done.2.mine), channel_id=1, source_target_pairs={{0,128},{128,0},{1,129},{129,1},{2,130},{130,2},{3,131},{131,3},{4... | collective-permute-start | bytes 1474568 | tf_op jit(solution)/shard_map/ppermute | solution.py:465
  83.1 1.5 %collective-permute-done.5.theirs = s16[16,120,128]{2,1,0:T(8,128)(2,1)S(1)} collective-permute-done((s16[16,120,128]{2,1,0:T(8,128)(2,1)S(1)}, s16[16,120,128]{2,1,0:T(8,128)(2,1)S(1)}, u32[]{:S(2)}, u32[]{:S(2)}) %collective-permute-start.5) | collective-permute-done | bytes 491552 | tf_op jit(solution)/shard_map/ppermute | solution.py:465
  84.6 1.4 %decode_total.1 = f32[3456,128]{1,0:T(8,128)} custom-call(s32[1]{0:T(128)} %bitcast.1.core, s16[16,120,128]{2,1,0:T(8,128)(2,1)S(1)} %all-to-all-done.2.mine, s16[16,120,128]{2,1,0:T(8,128)(2,1)S(1)} %collective-permute-done.5.theirs), custom_call_target="tpu_custom_call" | custom-call | bytes 3145728 | tf_op jit(solution)/shard_map/decode_total/pallas_call | solution.py:329
  (1 shorter events, 0.0 us)
Async XLA Ops:
  0.6 7.8 %copy-start = (bf16[1,16,16,2,8,128]{5,4,3,2,1,0:T(8,128)(2,1)S(1)}, bf16[1,16,16,2,8,128]{5,4,3,2,1,0:T(8,128)(2,1)}, u32[]{:S(2)}) copy-start(bf16[1,16,16,2,8,128]{5,4,3,2,1,0:T(8,128)(2,1)} %param.7) | copy-start | bytes 3145732
  0.6 7.8 %copy-start.1 = (bf16[1,16,16,2,8,128]{5,4,3,2,1,0:T(8,128)(2,1)S(1)}, bf16[1,16,16,2,8,128]{5,4,3,2,1,0:T(8,128)(2,1)}, u32[]{:S(2)}) copy-start(bf16[1,16,16,2,8,128]{5,4,3,2,1,0:T(8,128)(2,1)} %param.6) | copy-start | bytes 3145732
  0.7 7.8 %copy-start.2 = (s32[1,16,16,2,8]{2,4,3,1,0:T(8,128)S(1)}, s32[1,16,16,2,8]{2,4,3,1,0:T(8,128)}, u32[]{:S(2)}) copy-start(s32[1,16,16,2,8]{2,4,3,1,0:T(8,128)} %param.8) | copy-start | bytes 49156
  0.7 7.8 %copy-start.4 = (s32[1,2,2,2,27]{4,3,2,1,0:T(2,128)S(1)}, s32[1,2,2,2,27]{4,3,2,1,0:T(2,128)}, u32[]{:S(2)}) copy-start(s32[1,2,2,2,27]{4,3,2,1,0:T(2,128)} %refs_0_.7) | copy-start | bytes 2596
  0.7 7.8 %copy-start.7 = (s32[1,2,2,2]{3,2,1,0:T(2,128)S(1)}, s32[1,2,2,2]{3,2,1,0:T(2,128)}, u32[]{:S(2)}) copy-start(s32[1,2,2,2]{3,2,1,0:T(2,128)} %refs_1_.7) | copy-start | bytes 100
  2.8 9.3 %collective-permute-start = (bf16[1,16,2,8,128]{4,3,2,1,0:T(8,128)(2,1)}, bf16[1,16,2,8,128]{4,3,2,1,0:T(8,128)(2,1)S(1)}, u32[]{:S(2)}, u32[]{:S(2)}) collective-permute-start(bf16[1,16,2,8,128]{4,3,2,1,0:T(8,128)(2,1)} %get-tuple-element.32), channel_id=1, source_target_pairs={{0,16},{16,32},{32,48},{48,64},{64,80},{80,96},{96,112},{1,17},{17... | collective-permute-start | bytes 196616 | tf_op jit(solution)/shard_map/ppermute | solution.py:405
  7.1 5.4 %collective-permute-start.1 = (bf16[1,16,2,8,128]{4,3,2,1,0:T(8,128)(2,1)}, bf16[1,16,2,8,128]{4,3,2,1,0:T(8,128)(2,1)S(1)}, u32[]{:S(2)}, u32[]{:S(2)}) collective-permute-start(bf16[1,16,2,8,128]{4,3,2,1,0:T(8,128)(2,1)} %get-tuple-element.33), channel_id=1, source_target_pairs={{16,0},{32,16},{48,32},{64,48},{80,64},{96,80},{112,96},{17,1},{33... | collective-permute-start | bytes 196616 | tf_op jit(solution)/shard_map/ppermute | solution.py:405
  8.5 4.1 %copy-start.5 = (bf16[16,1,2,8,128]{4,3,2,1,0:T(8,128)(2,1)S(1)}, bf16[16,1,2,8,128]{4,3,2,1,0:T(8,128)(2,1)}, u32[]{:S(2)}) copy-start(bf16[16,1,2,8,128]{4,3,2,1,0:T(8,128)(2,1)} %get-tuple-element.36.left) | copy-start | bytes 196612
  8.5 4.0 %copy-start.6 = (bf16[16,1,2,8,128]{4,3,2,1,0:T(8,128)(2,1)S(1)}, bf16[16,1,2,8,128]{4,3,2,1,0:T(8,128)(2,1)}, u32[]{:S(2)}) copy-start(bf16[16,1,2,8,128]{4,3,2,1,0:T(8,128)(2,1)} %get-tuple-element.37.right) | copy-start | bytes 196612
  12.5 8.1 %collective-permute-start.2 = (bf16[18,1,2,8,128]{4,3,2,1,0:T(8,128)(2,1)S(1)}, bf16[18,1,2,8,128]{4,3,2,1,0:T(8,128)(2,1)S(1)}, u32[]{:S(2)}, u32[]{:S(2)}) collective-permute-start(bf16[18,1,2,8,128]{4,3,2,1,0:T(8,128)(2,1)S(1)} %get-tuple-element.38), channel_id=1, source_target_pairs={{0,1},{1,2},{2,3},{3,4},{4,5},{5,6},{6,7},{7,8},{8,9},{9,10},{10,1... | collective-permute-start | bytes 221192 | tf_op jit(solution)/shard_map/ppermute | solution.py:405
  15.8 5.1 %collective-permute-start.3 = (bf16[18,1,2,8,128]{4,3,2,1,0:T(8,128)(2,1)S(1)}, bf16[18,1,2,8,128]{4,3,2,1,0:T(8,128)(2,1)S(1)}, u32[]{:S(2)}, u32[]{:S(2)}) collective-permute-start(bf16[18,1,2,8,128]{4,3,2,1,0:T(8,128)(2,1)S(1)} %get-tuple-element.39), channel_id=1, source_target_pairs={{1,0},{2,1},{3,2},{4,3},{5,4},{6,5},{7,6},{8,7},{9,8},{10,9},{11,1... | collective-permute-start | bytes 221192 | tf_op jit(solution)/shard_map/ppermute | solution.py:405
  23.1 4.9 %collective-permute-start.4 = (s16[16,120,128]{2,1,0:T(8,128)(2,1)S(1)}, s16[16,120,128]{2,1,0:T(8,128)(2,1)S(1)}, u32[]{:S(2)}, u32[]{:S(2)}) collective-permute-start(s16[16,120,128]{2,1,0:T(8,128)(2,1)S(1)} %get-tuple-element.42), channel_id=1, source_target_pairs={{0,128},{128,0},{1,129},{129,1},{2,130},{130,2},{3,131},{131,3},{4... | collective-permute-start | bytes 1474568 | tf_op jit(solution)/shard_map/ppermute | solution.py:450
  28.0 27.8 %copy-start.3 = (bf16[27,128,128]{2,1,0:T(8,128)(2,1)S(1)}, bf16[27,128,128]{2,1,0:T(8,128)(2,1)}, u32[]{:S(2)}) copy-start(bf16[27,128,128]{2,1,0:T(8,128)(2,1)} %refs_5_.3) | copy-start | bytes 2654212
  47.1 18.0 %all-to-all-start.1 = ((s16[8,120,128]{2,1,0:T(8,128)(2,1)}), s16[8,120,128]{2,1,0:T(8,128)(2,1)S(1)}, u32[]{:S(2)}, u32[]{:S(2)}) async-start(s16[8,120,128]{2,1,0:T(8,128)(2,1)} %sum_piece.1), calls=%async_computation.1 | async-start | bytes 491520 | tf_op jit(solution)/shard_map/all_to_all | solution.py:384
  66.0 12.4 %all-to-all-start.2 = ((s16[16,120,128]{2,1,0:T(8,128)(2,1)}), s16[16,120,128]{2,1,0:T(8,128)(2,1)S(1)}, u32[]{:S(2)}, u32[]{:S(2)}) async-start(s16[16,120,128]{2,1,0:T(8,128)(2,1)} %sum_total.1), calls=%async_computation.2 | async-start | bytes 983040 | tf_op jit(solution)/shard_map/all_to_all | solution.py:384
  78.4 6.1 %collective-permute-start.5 = (s16[16,120,128]{2,1,0:T(8,128)(2,1)S(1)}, s16[16,120,128]{2,1,0:T(8,128)(2,1)S(1)}, u32[]{:S(2)}, u32[]{:S(2)}) collective-permute-start(s16[16,120,128]{2,1,0:T(8,128)(2,1)S(1)} %all-to-all-done.2.mine), channel_id=1, source_target_pairs={{0,128},{128,0},{1,129},{129,1},{2,130},{130,2},{3,131},{131,3},{4... | collective-permute-start | bytes 1474568 | tf_op jit(solution)/shard_map/ppermute | solution.py:465

commit v7 on v6

--- a/solution.py
+++ b/solution.py
@@ -49,17 +49,20 @@
     return [jnp.broadcast_to(tile[:, y : y + 1], (EDGE, WIDTH)) for y in spots]
 
 
-def pack_kernel(occ, first, last, start, end, top, bottom, left, right):
+def pack_kernel(low, high, first, last, top, bottom):
+    for occ, source, target in ((low, first, bottom), (high, last, top)):
+        for slot in range(2):
+            for y, mask in enumerate(mask_of(occ, 0, slot, range(occ.shape[3]))):
+                target[0, y, slot] = (source[0, y, slot].astype(jnp.float32) * mask).astype(jnp.bfloat16)
+
+
+def own_sides_kernel(occ, grad, left, right):
     nx, ny = occ.shape[0], occ.shape[3]
-    for x, source, target in ((0, first, bottom), (nx - 1, last, top)):
-        for slot in range(2):
-            for y, mask in enumerate(mask_of(occ, x, slot, range(ny))):
-                target[0, y, slot] = (source[0, y, slot].astype(jnp.float32) * mask).astype(jnp.bfloat16)
     for x in range(nx):
         for slot in range(2):
-            low, high = mask_of(occ, x, slot, (0, ny - 1))
-            right[x, 0, slot] = (start[x, 0, slot].astype(jnp.float32) * low).astype(jnp.bfloat16)
-            left[x, 0, slot] = (end[x, 0, slot].astype(jnp.float32) * high).astype(jnp.bfloat16)
+            for target, y in ((left, ny - 1), (right, 0)):
+                mask = mask_of(occ, x, slot, (y,))[0]
+                target[x, 0, slot] = (grad[x, y, slot].astype(jnp.float32) * mask).astype(jnp.bfloat16)
 
 
 def sides_kernel(top, bottom, left, right, left_side, right_side):
@@ -74,16 +77,13 @@
     nx, ny = grad.shape[0], grad.shape[1]
     low, high = (1, VIEW) if i == 0 else (0, VIEW - 1)
 
-    def fill(r, carry):
+    for r in range(low, high):
         x = EDGE * i - 1 + r
         values = grad[x].astype(jnp.float32)
         for slot in range(2):
             for y, mask in enumerate(mask_of(occ, x, slot, range(ny))):
                 masks[r, y, slot] = mask
                 field[r, y + 1, slot] = values[y, slot] * mask
-        return carry
-
-    lax.fori_loop(low, high, fill, 0)
     outer = 0 if i == 0 else VIEW - 1
     field[:, :, 2] = jnp.zeros((VIEW, ny + 2, EDGE, WIDTH), jnp.float32)
     if halo is None:
@@ -109,14 +109,9 @@
                 both = jnp.concatenate([halves[0][c], halves[1][c]], axis=1)
                 view[c, xl, start : start + count] = both.astype(jnp.bfloat16)
 
-    view_rows(0, 0)
-
-    def middle(xl, carry):
-        view_rows(xl, 1)
-        return carry
-
-    lax.fori_loop(1, EDGE + 1, middle, 0)
-    view_rows(EDGE + 1, 2)
+    for p, (start, count) in enumerate(REGIONS):
+        for xl in range(start, start + count):
+            view_rows(xl, p)
 
 
 def columns_of(view):
@@ -155,12 +150,9 @@
         def _():
             fill_view(nbr, field, view, i, slot)
 
-            def own_rows(xl, c2):
+            for xl in range(EDGE):
                 rows = pair_row(lz, feat, masks[xl + 1, :, slot], i, EDGE * i + xl, slot)
                 own[xl] = rows.astype(jnp.bfloat16)
-                return c2
-
-            lax.fori_loop(0, EDGE, own_rows, 0)
             own_t = own[...].reshape(UNIT, WIDTH).T
             part = jnp.dot(own_t, columns_of(view), preferred_element_type=jnp.float32)
             for k in range(0, 27, 3):
@@ -189,9 +181,11 @@
     strip[:, :, 2] = jnp.zeros((2, ny + 2, EDGE, WIDTH), jnp.float32)
     side[:, :, 2] = jnp.zeros((2, nx + 2, EDGE, WIDTH), jnp.float32)
 
-    def product(own_t, pieces, first):
+    def product(own_t, pieces, firsts):
         columns = jnp.concatenate(pieces, axis=1).astype(jnp.bfloat16)
-        add_terms(total, first, jnp.dot(own_t, columns, preferred_element_type=jnp.float32))
+        part = jnp.dot(own_t, columns, preferred_element_type=jnp.float32)
+        for n, first in enumerate(firsts):
+            add_terms(total, first, part[:, 3 * n * WIDTH : 3 * (n + 1) * WIDTH])
 
     def unit(i, slot):
         for q, (start, count) in enumerate(REGIONS):
@@ -205,9 +199,10 @@
         x = (0, nx - 1)[i]
         masks = jnp.stack(mask_of(occ, x, slot, range(ny)))
         own_t = pair_row(lz, feat, masks, i, x, slot).T.astype(jnp.bfloat16)
-        for b in range(3):
-            pieces = [row_view[c, 2 - b : 2 - b + EDGE].reshape(EDGE * ROWS, WIDTH) for c in range(3)]
-            product(own_t, pieces, 18 - 18 * i + 3 * b)
+        pieces = [
+            row_view[c, 2 - b : 2 - b + EDGE].reshape(EDGE * ROWS, WIDTH) for b in range(3) for c in range(3)
+        ]
+        product(own_t, pieces, [18 - 18 * i + 3 * b for b in range(3)])
         for j in range(2):
             for p, (start, count) in enumerate(REGIONS):
                 span = pl.ds(EDGE * i + start, count)
@@ -219,9 +214,10 @@
             rows = feat[EDGE * i : EDGE * i + EDGE, y, slot]
             own_t = kept(rows, masks, live_at(lz, i, j, slot)).reshape(EDGE * EDGE, WIDTH)
             own_t = own_t.T.astype(jnp.bfloat16)
-            for a in range(3):
-                pieces = [side_view[c, 2 - a : 2 - a + EDGE].reshape(EDGE * EDGE, WIDTH) for c in range(3)]
-                product(own_t, pieces, 9 * a + 6 - 6 * j)
+            pieces = [
+                side_view[c, 2 - a : 2 - a + EDGE].reshape(EDGE * EDGE, WIDTH) for a in range(3) for c in range(3)
+            ]
+            product(own_t, pieces, [9 * a + 6 - 6 * j for a in range(3)])
 
     for i in range(2):
 
@@ -256,16 +252,12 @@
                 columns_of(view), weights, (((1,), (1,)), ((), ())), preferred_element_type=jnp.float32
             )
 
-            def emit(xl, c2):
-                block = acc[pl.ds(pl.multiple_of(xl * EDGE * ROWS, EDGE * ROWS), EDGE * ROWS), :]
-                block = block.reshape(EDGE, 2, EDGE, WIDTH)
+            for xl in range(EDGE):
+                block = acc[xl * EDGE * ROWS : (xl + 1) * EDGE * ROWS].reshape(EDGE, 2, EDGE, WIDTH)
                 for j in range(2):
                     span = slice(EDGE * j, EDGE * j + EDGE)
                     value = kept(block[:, j], masks[xl + 1, span, slot], live_at(lz, i, j, slot))
                     out[xl, span, slot] = value.astype(jnp.bfloat16)
-                return c2
-
-            lax.fori_loop(0, EDGE, emit, 0)
 
         @pl.when(jnp.logical_not(live))
         def _():
@@ -311,13 +303,20 @@
     encode(total * scale, again, range(again.shape[0]))
 
 
-def decode_kernel(core, mine, theirs, out):
-    chunk = mine.shape[1] - EDGE
-    here = core[0]
-    for base, coded in ((here * HALF, mine), ((1 - here) * HALF, theirs)):
-        for n in range(coded.shape[0]):
-            rows = min(chunk, HALF - n * chunk)
-            out[pl.ds(pl.multiple_of(base + n * chunk, EDGE), rows)] = decode(coded[n])[0:rows]
+def decode_kernel(flip, core, coded, *refs):
+    out, part, done = refs[-3:]
+    chunk = coded.shape[1] - EDGE
+    here = core[0] + flip * (1 - 2 * core[0])
+    copies = []
+    for n in range(coded.shape[0]):
+        rows = min(chunk, HALF - n * chunk)
+        spot = pl.ds(n * chunk, rows)
+        part[spot] = decode(coded[n])[0:rows]
+        target = out.at[pl.ds(pl.multiple_of(here * HALF + n * chunk, EDGE), rows)]
+        copies.append(pltpu.make_async_copy(part.at[spot], target, done.at[n]))
+        copies[-1].start()
+    for copy in copies:
+        copy.wait()
 
 
 SMEM = pl.BlockSpec(memory_space=pltpu.SMEM)
@@ -362,22 +361,36 @@
 
 
 def pack_edges(occ, grad):
-    nx, ny = grad.shape[0], grad.shape[1]
     row = (1,) + grad.shape[1:]
-    side = (nx, 1) + grad.shape[2:]
-    places = ((row, (0, 0)), (row, (nx - 1, 0)), (side, (0, 0)), (side, (0, ny - 1)))
-    specs = [pl.BlockSpec(shape, lambda g, at=at: at + (0, 0, 0)) for shape, at in places]
-    shapes = [jax.ShapeDtypeStruct(shape, jnp.bfloat16) for shape in (row, row, side, side)]
-    whole = [pl.BlockSpec(shape.shape, lambda g: (0, 0, 0, 0, 0)) for shape in shapes]
+    tile = (1,) + occ.shape[1:]
+    ends = (0, grad.shape[0] - 1)
+    tiles = [pl.BlockSpec(tile, lambda g, at=at: (at, 0, 0, 0)) for at in ends]
+    rows = [pl.BlockSpec(row, lambda g, at=at: (at, 0, 0, 0, 0)) for at in ends]
     return pl.pallas_call(
         pack_kernel,
         grid=(1,),
-        out_shape=shapes,
-        in_specs=[pl.BlockSpec(occ.shape, lambda g: (0, 0, 0, 0))] + specs,
-        out_specs=whole,
-        cost_estimate=pl.CostEstimate(flops=0, bytes_accessed=1 << 20, transcendentals=0),
+        out_shape=[jax.ShapeDtypeStruct(row, jnp.bfloat16)] * 2,
+        in_specs=tiles + rows,
+        out_specs=[pl.BlockSpec(row, lambda g: (0, 0, 0, 0, 0))] * 2,
+        cost_estimate=pl.CostEstimate(flops=0, bytes_accessed=1 << 18, transcendentals=0),
         name="pack_edges",
-    )(occ, grad, grad, grad, grad)
+    )(occ, occ, grad, grad)
+
+
+def decode_part(core, coded, *before):
+    anywhere = pl.BlockSpec(memory_space=pl.ANY)
+    flip = len(before)
+    return pl.pallas_call(
+        lambda *refs: decode_kernel(flip, *refs),
+        in_specs=[SMEM, VMEM] + [anywhere] * flip,
+        out_specs=anywhere,
+        out_shape=jax.ShapeDtypeStruct((2 * HALF, WIDTH), jnp.float32),
+        scratch_shapes=[pltpu.VMEM((HALF, WIDTH), jnp.float32), pltpu.SemaphoreType.DMA((coded.shape[0],))],
+        input_output_aliases={2: 0} if before else {},
+        compiler_params=pltpu.CompilerParams(vmem_limit_bytes=20 << 20),
+        cost_estimate=pl.CostEstimate(flops=0, bytes_accessed=3 << 19, transcendentals=0),
+        name="decode_half",
+    )(core, coded, *before)
 
 
 def exchange(blocks, axis):
@@ -418,9 +431,11 @@
         )(neighbours, leaf_z, grad, feat, occ, *before)
 
     core, packed = lax.optimization_barrier((core, pack_edges(occ, grad)))
-    last, first, end, start = packed
+    last, first = packed
     top = shift(last, "gx", 1)
     bottom = shift(first, "gx", -1)
+    own_side = jax.ShapeDtypeStruct((nx, 1, 2, EDGE, WIDTH), jnp.bfloat16)
+    end, start = call(own_sides_kernel, "own_sides", (own_side, own_side), nbytes=1 << 19)(occ, grad)
     terms = terms_of(0)
     top, bottom, terms = lax.optimization_barrier((top, bottom, terms))
     side = jax.ShapeDtypeStruct((nx + 2, 1, 2, EDGE, WIDTH), jnp.bfloat16)
@@ -463,13 +478,7 @@
     out, total = features_part(1, total, out)
     total, out = lax.optimization_barrier((exchange(total, "gy"), out))
     other = lax.ppermute(total, "dcn", [(0, 1), (1, 0)])
-    kernel_grad = call(
-        decode_kernel,
-        "decode_total",
-        jax.ShapeDtypeStruct((27 * WIDTH, WIDTH), jnp.float32),
-        scalars=1,
-        nbytes=3 << 20,
-    )(core, total, other)
+    kernel_grad = decode_part(core, other, decode_part(core, total))
     return out[None], kernel_grad.reshape(27, WIDTH, WIDTH)
 
 

time: 86.4 us -> 85.1 us (0.985)
  Pallas kernels: 25.1 us -> 22.3 us
  waiting for transfers between devices: 11.6 us -> 13.9 us
    pallas_call x8, Pallas kernels: 12.9 us -> 10 us  [run(): pl.pallas_call(kernel, out_shape=out_shape, in_specs=[SMEM] * scalars + [...]
    pallas_call x1 -> x3, Pallas kernels: 2.06 us -> 3.95 us  [the longest x2 2.08 us: decode_part(): pl.pallas_call(lambda *refs: decode_kernel(flip, *refs), in_specs=[SMEM,...]
    all_to_all x2, waiting for transfers between devices: 7.93 us -> 9.8 us  [exchange(): return lax.all_to_all(blocks, axis, 0, 0)]
    pallas_call x2, Pallas kernels: 10.2 us -> 8.3 us  [features_call(): pl.pallas_call(lambda *refs: feature_kernel(i, *refs), grid=(1,), out_sha...]
    ppermute x4, waiting for transfers between devices: 0.67 us -> 2.14 us  [shift(): return lax.ppermute(block, axis, pairs)]
    ppermute x1, waiting for transfers between devices: 1.49 us -> 0.44 us  [local(): other = lax.ppermute(total, 'dcn', [(0, 1), (1, 0)])]
  transfers between devices with their start and end apart: 8 -> 8, of which waited for: 6 -> 6; matrix products, arithmetic and copies ran while one was open for 0% -> 0% of each run, Pallas kernels for 20% -> 18%
where the time goes in v7:
time: 85.1 us; the launch traced here: 84.7 us
  starting transfers between devices  29.8 us (35%)
  Pallas kernels  22.3 us (26%)
  blocking collectives  17.9 us (21%)
  waiting for transfers between devices  13.9 us (16%)
    all_to_all x1, blocking collectives, exchange(): return lax.all_to_all(blocks, axis, 0, 0)  17.9 us
    all_to_all x2, starting transfers between devices, exchange(): return lax.all_to_all(blocks, axis, 0, 0)  11.6 us
    ppermute x4, starting transfers between devices, shift(): return lax.ppermute(block, axis, pairs)  10.2 us
    pallas_call x8, Pallas kernels, run(): pl.pallas_call(kernel, out_shape=out_shape, in_specs=[SMEM] * scalars + [...  10 us
    all_to_all x2, waiting for transfers between devices, exchange(): return lax.all_to_all(blocks, axis, 0, 0)  9.8 us
    pallas_call x2, Pallas kernels, features_call(): pl.pallas_call(lambda *refs: feature_kernel(i, *refs), grid=(1,), out_sha...  8.3 us
    ppermute x1, starting transfers between devices, local(): other = lax.ppermute(total, 'dcn', [(0, 1), (1, 0)])  4.65 us
    ppermute x1, starting transfers between devices, local(): theirs = lax.ppermute(theirs, 'dcn', [(0, 1), (1, 0)])  3.44 us
  transfers between devices with their start and end apart: 8, of which 6 were waited for; matrix products, arithmetic and copies ran while one was open for 0% of the time, Pallas kernels for 18%

profile of v7, /device:TPU:1, one launch (start us, length us, event | category | flops | bytes accessed | tf_op | source)
XLA Modules:
  0.0 84.7 jit_solution(15960954760972971289)
XLA Ops:
  0.6 0.0 copy-start.2
  0.6 0.0 copy-start
  0.7 0.0 copy-start.4
  0.7 0.0 copy-start.5
  0.7 0.0 copy-start.1
  0.7 1.9 %pack_edges.1 = (bf16[1,16,2,8,128]{4,3,2,1,0:T(8,128)(2,1)}, bf16[1,16,2,8,128]{4,3,2,1,0:T(8,128)(2,1)}) custom-call(s32[16,2,8,16]{3,2,1,0:T(8,128)} %bitcast.18, s32[16,2,8,16]{3,2,1,0:T(8,128)} %bitcast.19, bf16[16,16,2,8,128]{4,3,2,1,0:T(8,128)(2,1)} %bitcast.8, bf16[16,16,2,8,128]{4,3,2,1,0:T(8,128)(2,1)} %bitcast.9), custom_call_target="tpu_custom_call" | custom-call | bytes 262144 | tf_op jit(solution)/shard_map/pack_edges/pallas_call | solution.py:369
  2.6 4.4 %collective-permute-start = (bf16[1,16,2,8,128]{4,3,2,1,0:T(8,128)(2,1)}, bf16[1,16,2,8,128]{4,3,2,1,0:T(8,128)(2,1)S(1)}, u32[]{:S(2)}, u32[]{:S(2)}) collective-permute-start(bf16[1,16,2,8,128]{4,3,2,1,0:T(8,128)(2,1)} %get-tuple-element.28), channel_id=1, source_target_pairs={{0,16},{16,32},{32,48},{48,64},{64,80},{80,96},{96,112},{1,17},{17... | collective-permute-start | bytes 196616 | tf_op jit(solution)/shard_map/ppermute | solution.py:418
  6.9 1.3 %collective-permute-start.1 = (bf16[1,16,2,8,128]{4,3,2,1,0:T(8,128)(2,1)}, bf16[1,16,2,8,128]{4,3,2,1,0:T(8,128)(2,1)S(1)}, u32[]{:S(2)}, u32[]{:S(2)}) collective-permute-start(bf16[1,16,2,8,128]{4,3,2,1,0:T(8,128)(2,1)} %get-tuple-element.29), channel_id=1, source_target_pairs={{16,0},{32,16},{48,32},{64,48},{80,64},{96,80},{112,96},{17,1},{33... | collective-permute-start | bytes 196616 | tf_op jit(solution)/shard_map/ppermute | solution.py:418
  8.2 0.0 copy-done.2
  8.2 0.0 copy-done
  8.2 0.1 own_sides.1
  8.4 0.0 copy-done.4
  8.4 0.0 copy-done.5
  8.4 0.0 copy-done.1
  8.4 2.8 %conv_terms.2.refs_5_ = f32[2,1792,128]{2,1,0:T(8,128)S(1)} custom-call(s32[1,2,2,2,27]{4,3,2,1,0:T(2,128)S(1)} %copy-done.4, s32[1,2,2,2]{3,2,1,0:T(2,128)S(1)} %copy-done.5, bf16[16,16,2,8,128]{4,3,2,1,0:T(8,128)(2,1)S(1)} %bitcast.11, bf16[16,16,2,8,128]{4,3,2,1,0:T(8,128)(2,1)S(1)} %bitcast.15, s32[16,2,8,16]{3,2,1,0:T(8,128)S(1)} %bitcast.21), custom_call_target="tpu_custom_call" | custom-call | flops 905969664 | bytes 4194304 | tf_op jit(solution)/shard_map/conv_terms/pallas_call | solution.py:328
  11.2 0.0 collective-permute-done.top
  11.2 1.1 %collective-permute-done.1.bottom = bf16[1,16,2,8,128]{4,3,2,1,0:T(8,128)(2,1)S(1)} collective-permute-done((bf16[1,16,2,8,128]{4,3,2,1,0:T(8,128)(2,1)}, bf16[1,16,2,8,128]{4,3,2,1,0:T(8,128)(2,1)S(1)}, u32[]{:S(2)}, u32[]{:S(2)}) %collective-permute-start.1) | collective-permute-done | bytes 65568 | tf_op jit(solution)/shard_map/ppermute | solution.py:418
  12.3 3.2 %collective-permute-start.2 = (bf16[18,1,2,8,128]{4,3,2,1,0:T(8,128)(2,1)S(1)}, bf16[18,1,2,8,128]{4,3,2,1,0:T(8,128)(2,1)S(1)}, u32[]{:S(2)}, u32[]{:S(2)}) collective-permute-start(bf16[18,1,2,8,128]{4,3,2,1,0:T(8,128)(2,1)S(1)} %get-tuple-element.34), channel_id=1, source_target_pairs={{0,1},{1,2},{2,3},{3,4},{4,5},{5,6},{6,7},{7,8},{8,9},{9,10},{10,1... | collective-permute-start | bytes 221192 | tf_op jit(solution)/shard_map/ppermute | solution.py:418
  15.6 1.3 %collective-permute-start.3 = (bf16[18,1,2,8,128]{4,3,2,1,0:T(8,128)(2,1)S(1)}, bf16[18,1,2,8,128]{4,3,2,1,0:T(8,128)(2,1)S(1)}, u32[]{:S(2)}, u32[]{:S(2)}) collective-permute-start(bf16[18,1,2,8,128]{4,3,2,1,0:T(8,128)(2,1)S(1)} %get-tuple-element.35), channel_id=1, source_target_pairs={{1,0},{2,1},{3,2},{4,3},{5,4},{6,5},{7,6},{8,7},{9,8},{10,9},{11,1... | collective-permute-start | bytes 221192 | tf_op jit(solution)/shard_map/ppermute | solution.py:418
  16.9 2.8 %conv_terms.3.before = f32[2,1792,128]{2,1,0:T(8,128)S(1)} custom-call(s32[1,2,2,2,27]{4,3,2,1,0:T(2,128)S(1)} %copy-done.4, s32[1,2,2,2]{3,2,1,0:T(2,128)S(1)} %copy-done.5, bf16[16,16,2,8,128]{4,3,2,1,0:T(8,128)(2,1)S(1)} %bitcast.12, bf16[16,16,2,8,128]{4,3,2,1,0:T(8,128)(2,1)S(1)} %bitcast.16, s32[16,2,8,16]{3,2,1,0:T(8,128)S(1)} %bitcast.22, ...), custom_call_target="tpu_custom_call" | custom-call | flops 905969664 | bytes 4194304 | tf_op jit(solution)/shard_map/conv_terms/pallas_call | solution.py:328
  19.6 0.0 collective-permute-done.2.left
  19.7 1.0 %collective-permute-done.3.right = bf16[18,1,2,8,128]{4,3,2,1,0:T(8,128)(2,1)S(1)} collective-permute-done((bf16[18,1,2,8,128]{4,3,2,1,0:T(8,128)(2,1)S(1)}, bf16[18,1,2,8,128]{4,3,2,1,0:T(8,128)(2,1)S(1)}, u32[]{:S(2)}, u32[]{:S(2)}) %collective-permute-start.3) | collective-permute-done | bytes 73760 | tf_op jit(solution)/shard_map/ppermute | solution.py:418
  20.7 2.2 %edge_terms.1 = (f32[1792,128]{1,0:T(8,128)S(1)}, s16[16,120,128]{2,1,0:T(8,128)(2,1)S(1)}, bf16[68,2,8,128]{3,2,1,0:T(8,128)(2,1)S(1)}) custom-call(s32[1,2,2,2,27]{4,3,2,1,0:T(2,128)S(1)} %copy-done.4, s32[1,2,2,2]{3,2,1,0:T(2,128)S(1)} %copy-done.5, s32[1]{0:T(128)} %bitcast.1.core.refs_0_, bf16[16,16,2,8,128]{4,3,2,1,0:T(8,128)(2,1)S(1)} %bitcast.17, ...), custom_call_target="tpu_custom_call" | custom-call | flops 226492416 | bytes 4194304 | tf_op jit(solution)/shard_map/edge_terms/pallas_call | solution.py:328
  22.8 3.4 %collective-permute-start.4 = (s16[16,120,128]{2,1,0:T(8,128)(2,1)S(1)}, s16[16,120,128]{2,1,0:T(8,128)(2,1)S(1)}, u32[]{:S(2)}, u32[]{:S(2)}) collective-permute-start(s16[16,120,128]{2,1,0:T(8,128)(2,1)S(1)} %get-tuple-element.38), channel_id=1, source_target_pairs={{0,128},{128,0},{1,129},{129,1},{2,130},{130,2},{3,131},{131,3},{4... | collective-permute-start | bytes 1474568 | tf_op jit(solution)/shard_map/ppermute | solution.py:465
  26.3 1.5 %collective-permute-done.4.theirs = s16[16,120,128]{2,1,0:T(8,128)(2,1)S(1)} collective-permute-done((s16[16,120,128]{2,1,0:T(8,128)(2,1)S(1)}, s16[16,120,128]{2,1,0:T(8,128)(2,1)S(1)}, u32[]{:S(2)}, u32[]{:S(2)}) %collective-permute-start.4) | collective-permute-done | bytes 491552 | tf_op jit(solution)/shard_map/ppermute | solution.py:465
  27.8 0.0 copy-start.3
  27.8 0.3 encode_half.1
  28.1 17.9 %all_to_all.15.c = s16[16,120,128]{2,1,0:T(8,128)(2,1)S(1)} all-to-all(s16[16,120,128]{2,1,0:T(8,128)(2,1)S(1)} %encode_half.1), channel_id=1, replica_groups=mesh['dcn'=2,'gx'=8,'gy'=16] {'gy'}, dimensions={0} | all-to-all | bytes 983040 | tf_op jit(solution)/shard_map/all_to_all | solution.py:397
  46.0 0.9 %sum_piece.1 = s16[8,120,128]{2,1,0:T(8,128)(2,1)} custom-call(s16[16,120,128]{2,1,0:T(8,128)(2,1)S(1)} %all_to_all.15.c), custom_call_target="tpu_custom_call" | custom-call | bytes 1048576 | tf_op jit(solution)/shard_map/sum_piece/pallas_call | solution.py:328
  46.9 8.0 %all-to-all-start.1 = ((s16[8,120,128]{2,1,0:T(8,128)(2,1)}), s16[8,120,128]{2,1,0:T(8,128)(2,1)S(1)}, u32[]{:S(2)}, u32[]{:S(2)}) async-start(s16[8,120,128]{2,1,0:T(8,128)(2,1)} %sum_piece.1), calls=%async_computation.1 | async-start | bytes 491520 | tf_op jit(solution)/shard_map/all_to_all | solution.py:397
  54.9 0.0 copy-done.3
  54.9 4.1 %conv_features.2.refs_6_ = bf16[16,16,2,8,128]{4,3,2,1,0:T(8,128)(2,1)} custom-call(s32[1,2,2,2,27]{4,3,2,1,0:T(2,128)S(1)} %copy-done.4, s32[1,2,2,2]{3,2,1,0:T(2,128)S(1)} %copy-done.5, bf16[16,16,2,8,128]{4,3,2,1,0:T(8,128)(2,1)S(1)} %bitcast.13, s32[16,2,8,16]{3,2,1,0:T(8,128)S(1)} %bitcast.24, bf16[68,2,8,128]{3,2,1,0:T(8,128)(2,1)S(1)} %get-tuple-element.41.refs_4_, ...), custom_call_target="tpu_custom_call" | custom-call | flops 905969664 | bytes 4194304 | tf_op jit(solution)/shard_map/conv_features/pallas_call | solution.py:349
  59.1 5.1 %all-to-all-done.1.c = s16[8,120,128]{2,1,0:T(8,128)(2,1)S(1)} async-done(((s16[8,120,128]{2,1,0:T(8,128)(2,1)}), s16[8,120,128]{2,1,0:T(8,128)(2,1)S(1)}, u32[]{:S(2)}, u32[]{:S(2)}) %all-to-all-start.1) | async-done | bytes 245792 | tf_op jit(solution)/shard_map/all_to_all | solution.py:397
  64.2 0.9 %sum_total.1 = s16[16,120,128]{2,1,0:T(8,128)(2,1)} custom-call(s16[8,120,128]{2,1,0:T(8,128)(2,1)S(1)} %all-to-all-done.1.c), custom_call_target="tpu_custom_call" | custom-call | bytes 1048576 | tf_op jit(solution)/shard_map/sum_total/pallas_call | solution.py:328
  65.1 3.6 %all-to-all-start.2 = ((s16[16,120,128]{2,1,0:T(8,128)(2,1)}), s16[16,120,128]{2,1,0:T(8,128)(2,1)S(1)}, u32[]{:S(2)}, u32[]{:S(2)}) async-start(s16[16,120,128]{2,1,0:T(8,128)(2,1)} %sum_total.1), calls=%async_computation.2 | async-start | bytes 983040 | tf_op jit(solution)/shard_map/all_to_all | solution.py:397
  68.7 4.1 %conv_features.3 = bf16[16,16,2,8,128]{4,3,2,1,0:T(8,128)(2,1)} custom-call(s32[1,2,2,2,27]{4,3,2,1,0:T(2,128)S(1)} %copy-done.4, s32[1,2,2,2]{3,2,1,0:T(2,128)S(1)} %copy-done.5, bf16[16,16,2,8,128]{4,3,2,1,0:T(8,128)(2,1)S(1)} %bitcast.14, s32[16,2,8,16]{3,2,1,0:T(8,128)S(1)} %bitcast.25, ...), custom_call_target="tpu_custom_call", output_to_operand_aliasing={{}: (6, {})} | custom-call | flops 905969664 | bytes 4194304 | tf_op jit(solution)/shard_map/conv_features/pallas_call | solution.py:349
  72.8 4.7 %all-to-all-done.2.refs_1_ = s16[16,120,128]{2,1,0:T(8,128)(2,1)S(1)} async-done(((s16[16,120,128]{2,1,0:T(8,128)(2,1)}), s16[16,120,128]{2,1,0:T(8,128)(2,1)S(1)}, u32[]{:S(2)}, u32[]{:S(2)}) %all-to-all-start.2) | async-done | bytes 491552 | tf_op jit(solution)/shard_map/all_to_all | solution.py:397
  77.5 4.6 %collective-permute-start.5 = (s16[16,120,128]{2,1,0:T(8,128)(2,1)S(1)}, s16[16,120,128]{2,1,0:T(8,128)(2,1)S(1)}, u32[]{:S(2)}, u32[]{:S(2)}) collective-permute-start(s16[16,120,128]{2,1,0:T(8,128)(2,1)S(1)} %all-to-all-done.2.refs_1_), channel_id=1, source_target_pairs={{0,128},{128,0},{1,129},{129,1},{2,130},{130,2},{3,131},{131,3},{4... | collective-permute-start | bytes 1474568 | tf_op jit(solution)/shard_map/ppermute | solution.py:480
  82.2 1.0 %decode_half.2.refs_2_ = f32[3456,128]{1,0:T(8,128)} custom-call(s32[1]{0:T(128)} %bitcast.1.core.refs_0_, s16[16,120,128]{2,1,0:T(8,128)(2,1)S(1)} %all-to-all-done.2.refs_1_), custom_call_target="tpu_custom_call" | custom-call | bytes 1572864 | tf_op jit(solution)/shard_map/decode_half/pallas_call | solution.py:383
  83.2 0.4 collective-permute-done.5.refs_1_
  83.7 1.0 %decode_half.3 = f32[3456,128]{1,0:T(8,128)} custom-call(s32[1]{0:T(128)} %bitcast.1.core.refs_0_, s16[16,120,128]{2,1,0:T(8,128)(2,1)S(1)} %collective-permute-done.5.refs_1_, f32[3456,128]{1,0:T(8,128)} %decode_half.2.refs_2_), custom_call_target="tpu_custom_call", output_to_operand_aliasing={{}: (2, {})} | custom-call | bytes 1572864 | tf_op jit(solution)/shard_map/decode_half/pallas_call | solution.py:383
  (1 shorter events, 0.0 us)
Async XLA Ops:
  0.6 7.6 %copy-start.2 = (s32[1,16,16,2,8]{2,4,3,1,0:T(8,128)S(1)}, s32[1,16,16,2,8]{2,4,3,1,0:T(8,128)}, u32[]{:S(2)}) copy-start(s32[1,16,16,2,8]{2,4,3,1,0:T(8,128)} %param.8) | copy-start | bytes 49156
  0.6 7.6 %copy-start = (bf16[1,16,16,2,8,128]{5,4,3,2,1,0:T(8,128)(2,1)S(1)}, bf16[1,16,16,2,8,128]{5,4,3,2,1,0:T(8,128)(2,1)}, u32[]{:S(2)}) copy-start(bf16[1,16,16,2,8,128]{5,4,3,2,1,0:T(8,128)(2,1)} %param.7) | copy-start | bytes 3145732
  0.7 7.7 %copy-start.4 = (s32[1,2,2,2,27]{4,3,2,1,0:T(2,128)S(1)}, s32[1,2,2,2,27]{4,3,2,1,0:T(2,128)}, u32[]{:S(2)}) copy-start(s32[1,2,2,2,27]{4,3,2,1,0:T(2,128)} %refs_0_.7) | copy-start | bytes 2596
  0.7 7.7 %copy-start.5 = (s32[1,2,2,2]{3,2,1,0:T(2,128)S(1)}, s32[1,2,2,2]{3,2,1,0:T(2,128)}, u32[]{:S(2)}) copy-start(s32[1,2,2,2]{3,2,1,0:T(2,128)} %refs_1_.7) | copy-start | bytes 100
  0.7 7.7 %copy-start.1 = (bf16[1,16,16,2,8,128]{5,4,3,2,1,0:T(8,128)(2,1)S(1)}, bf16[1,16,16,2,8,128]{5,4,3,2,1,0:T(8,128)(2,1)}, u32[]{:S(2)}) copy-start(bf16[1,16,16,2,8,128]{5,4,3,2,1,0:T(8,128)(2,1)} %param.6) | copy-start | bytes 3145732
  2.6 8.6 %collective-permute-start = (bf16[1,16,2,8,128]{4,3,2,1,0:T(8,128)(2,1)}, bf16[1,16,2,8,128]{4,3,2,1,0:T(8,128)(2,1)S(1)}, u32[]{:S(2)}, u32[]{:S(2)}) collective-permute-start(bf16[1,16,2,8,128]{4,3,2,1,0:T(8,128)(2,1)} %get-tuple-element.28), channel_id=1, source_target_pairs={{0,16},{16,32},{32,48},{48,64},{64,80},{80,96},{96,112},{1,17},{17... | collective-permute-start | bytes 196616 | tf_op jit(solution)/shard_map/ppermute | solution.py:418
  6.9 5.4 %collective-permute-start.1 = (bf16[1,16,2,8,128]{4,3,2,1,0:T(8,128)(2,1)}, bf16[1,16,2,8,128]{4,3,2,1,0:T(8,128)(2,1)S(1)}, u32[]{:S(2)}, u32[]{:S(2)}) collective-permute-start(bf16[1,16,2,8,128]{4,3,2,1,0:T(8,128)(2,1)} %get-tuple-element.29), channel_id=1, source_target_pairs={{16,0},{32,16},{48,32},{64,48},{80,64},{96,80},{112,96},{17,1},{33... | collective-permute-start | bytes 196616 | tf_op jit(solution)/shard_map/ppermute | solution.py:418
  12.3 7.3 %collective-permute-start.2 = (bf16[18,1,2,8,128]{4,3,2,1,0:T(8,128)(2,1)S(1)}, bf16[18,1,2,8,128]{4,3,2,1,0:T(8,128)(2,1)S(1)}, u32[]{:S(2)}, u32[]{:S(2)}) collective-permute-start(bf16[18,1,2,8,128]{4,3,2,1,0:T(8,128)(2,1)S(1)} %get-tuple-element.34), channel_id=1, source_target_pairs={{0,1},{1,2},{2,3},{3,4},{4,5},{5,6},{6,7},{7,8},{8,9},{9,10},{10,1... | collective-permute-start | bytes 221192 | tf_op jit(solution)/shard_map/ppermute | solution.py:418
  15.6 5.1 %collective-permute-start.3 = (bf16[18,1,2,8,128]{4,3,2,1,0:T(8,128)(2,1)S(1)}, bf16[18,1,2,8,128]{4,3,2,1,0:T(8,128)(2,1)S(1)}, u32[]{:S(2)}, u32[]{:S(2)}) collective-permute-start(bf16[18,1,2,8,128]{4,3,2,1,0:T(8,128)(2,1)S(1)} %get-tuple-element.35), channel_id=1, source_target_pairs={{1,0},{2,1},{3,2},{4,3},{5,4},{6,5},{7,6},{8,7},{9,8},{10,9},{11,1... | collective-permute-start | bytes 221192 | tf_op jit(solution)/shard_map/ppermute | solution.py:418
  22.8 4.9 %collective-permute-start.4 = (s16[16,120,128]{2,1,0:T(8,128)(2,1)S(1)}, s16[16,120,128]{2,1,0:T(8,128)(2,1)S(1)}, u32[]{:S(2)}, u32[]{:S(2)}) collective-permute-start(s16[16,120,128]{2,1,0:T(8,128)(2,1)S(1)} %get-tuple-element.38), channel_id=1, source_target_pairs={{0,128},{128,0},{1,129},{129,1},{2,130},{130,2},{3,131},{131,3},{4... | collective-permute-start | bytes 1474568 | tf_op jit(solution)/shard_map/ppermute | solution.py:465
  27.8 27.1 %copy-start.3 = (bf16[27,128,128]{2,1,0:T(8,128)(2,1)S(1)}, bf16[27,128,128]{2,1,0:T(8,128)(2,1)}, u32[]{:S(2)}) copy-start(bf16[27,128,128]{2,1,0:T(8,128)(2,1)} %refs_5_.3) | copy-start | bytes 2654212
  46.9 17.3 %all-to-all-start.1 = ((s16[8,120,128]{2,1,0:T(8,128)(2,1)}), s16[8,120,128]{2,1,0:T(8,128)(2,1)S(1)}, u32[]{:S(2)}, u32[]{:S(2)}) async-start(s16[8,120,128]{2,1,0:T(8,128)(2,1)} %sum_piece.1), calls=%async_computation.1 | async-start | bytes 491520 | tf_op jit(solution)/shard_map/all_to_all | solution.py:397
  65.1 12.4 %all-to-all-start.2 = ((s16[16,120,128]{2,1,0:T(8,128)(2,1)}), s16[16,120,128]{2,1,0:T(8,128)(2,1)S(1)}, u32[]{:S(2)}, u32[]{:S(2)}) async-start(s16[16,120,128]{2,1,0:T(8,128)(2,1)} %sum_total.1), calls=%async_computation.2 | async-start | bytes 983040 | tf_op jit(solution)/shard_map/all_to_all | solution.py:397
  77.5 6.1 %collective-permute-start.5 = (s16[16,120,128]{2,1,0:T(8,128)(2,1)S(1)}, s16[16,120,128]{2,1,0:T(8,128)(2,1)S(1)}, u32[]{:S(2)}, u32[]{:S(2)}) collective-permute-start(s16[16,120,128]{2,1,0:T(8,128)(2,1)S(1)} %all-to-all-done.2.refs_1_), channel_id=1, source_target_pairs={{0,128},{128,0},{1,129},{129,1},{2,130},{130,2},{3,131},{131,3},{4... | collective-permute-start | bytes 1474568 | tf_op jit(solution)/shard_map/ppermute | solution.py:480

commit v8 on v7

--- a/solution.py
+++ b/solution.py
@@ -141,8 +141,10 @@
 
 
 def terms_kernel(i, nbr, lz, grad, feat, occ, *refs):
-    *before, terms, field, masks, view, own = refs
-    terms[...] = before[0][...] if before else jnp.zeros_like(terms)
+    *before, terms, field, masks, view, own, strip, row_view = refs
+    terms[...] = before[2][...] if before else jnp.zeros_like(terms)
+    if before:
+        row_edges(nbr, lz, feat, occ, before[0], before[1], terms, strip, row_view)
     fill_field(i, grad, occ, None, field, masks)
 
     def unit(slot, carry):
@@ -163,29 +165,20 @@
     lax.fori_loop(0, 2, unit, 0)
 
 
-def edge_kernel(nbr, lz, core, feat, occ, top, bottom, left, right, before, mine, theirs, halo, total, strip, side, row_view, side_view):
+def product(total, own_t, pieces, firsts):
+    columns = jnp.concatenate(pieces, axis=1).astype(jnp.bfloat16)
+    part = jnp.dot(own_t, columns, preferred_element_type=jnp.float32)
+    for n, first in enumerate(firsts):
+        add_terms(total, first, part[:, 3 * n * WIDTH : 3 * (n + 1) * WIDTH])
+
+
+def row_edges(nbr, lz, feat, occ, top, bottom, total, strip, row_view):
     nx, ny = feat.shape[0], feat.shape[1]
-    total[...] = before[...]
-    halo[0:ny] = top[0]
-    halo[ny : 2 * ny] = bottom[0]
-    halo[2 * ny : 2 * ny + nx + 2] = left[:, 0]
-    halo[2 * ny + nx + 2 :] = right[:, 0]
     for i in range(2):
-        spot = (0, nx + 1)[i]
         strip[i, 1 : ny + 1, 0:2] = (top, bottom)[i][0].astype(jnp.float32)
-        strip[i, 0, 0:2] = left[spot, 0].astype(jnp.float32)
-        strip[i, ny + 1, 0:2] = right[spot, 0].astype(jnp.float32)
-        side[i, 1 : nx + 1, 0:2] = (left, right)[i][1 : nx + 1, 0].astype(jnp.float32)
-        for end in (0, nx + 1):
-            side[i, end, 0:2] = jnp.zeros((2, EDGE, WIDTH), jnp.float32)
+        for end in (0, ny + 1):
+            strip[i, end, 0:2] = jnp.zeros((2, EDGE, WIDTH), jnp.float32)
     strip[:, :, 2] = jnp.zeros((2, ny + 2, EDGE, WIDTH), jnp.float32)
-    side[:, :, 2] = jnp.zeros((2, nx + 2, EDGE, WIDTH), jnp.float32)
-
-    def product(own_t, pieces, firsts):
-        columns = jnp.concatenate(pieces, axis=1).astype(jnp.bfloat16)
-        part = jnp.dot(own_t, columns, preferred_element_type=jnp.float32)
-        for n, first in enumerate(firsts):
-            add_terms(total, first, part[:, 3 * n * WIDTH : 3 * (n + 1) * WIDTH])
 
     def unit(i, slot):
         for q, (start, count) in enumerate(REGIONS):
@@ -202,7 +195,36 @@
         pieces = [
             row_view[c, 2 - b : 2 - b + EDGE].reshape(EDGE * ROWS, WIDTH) for b in range(3) for c in range(3)
         ]
-        product(own_t, pieces, [18 - 18 * i + 3 * b for b in range(3)])
+        product(total, own_t, pieces, [18 - 18 * i + 3 * b for b in range(3)])
+
+    for_live(lz, unit)
+
+
+def for_live(lz, unit):
+    for i in range(2):
+
+        def slots(slot, carry, i=i):
+            @pl.when(pair_live(lz, i, slot))
+            def _():
+                unit(i, slot)
+
+            return carry
+
+        lax.fori_loop(0, 2, slots, 0)
+
+
+def edge_kernel(nbr, lz, core, feat, occ, top, bottom, left, right, before, mine, theirs, halo, total, side, side_view):
+    nx, ny = feat.shape[0], feat.shape[1]
+    total[...] = before[...]
+    halo[0:ny] = top[0]
+    halo[ny : 2 * ny] = bottom[0]
+    halo[2 * ny : 2 * ny + nx + 2] = left[:, 0]
+    halo[2 * ny + nx + 2 :] = right[:, 0]
+    for j in range(2):
+        side[j, :, 0:2] = (left, right)[j][:, 0].astype(jnp.float32)
+    side[:, :, 2] = jnp.zeros((2, nx + 2, EDGE, WIDTH), jnp.float32)
+
+    def unit(i, slot):
         for j in range(2):
             for p, (start, count) in enumerate(REGIONS):
                 span = pl.ds(EDGE * i + start, count)
@@ -217,18 +239,9 @@
             pieces = [
                 side_view[c, 2 - a : 2 - a + EDGE].reshape(EDGE * EDGE, WIDTH) for a in range(3) for c in range(3)
             ]
-            product(own_t, pieces, [9 * a + 6 - 6 * j for a in range(3)])
-
-    for i in range(2):
-
-        def slots(slot, carry, i=i):
-            @pl.when(pair_live(lz, i, slot))
-            def _():
-                unit(i, slot)
-
-            return carry
-
-        lax.fori_loop(0, 2, slots, 0)
+            product(total, own_t, pieces, [9 * a + 6 - 6 * j for a in range(3)])
+
+    for_live(lz, unit)
     here = core[0]
     chunk = theirs.shape[1] - EDGE
     mine[...] = total[here]
@@ -410,6 +423,8 @@
     view = pltpu.VMEM((3, VIEW, VIEW, ROWS, WIDTH), jnp.bfloat16)
     own = pltpu.VMEM((EDGE, EDGE * ROWS, WIDTH), jnp.bfloat16)
     acc = pltpu.VMEM((UNIT, WIDTH), jnp.float32)
+    strip = pltpu.VMEM((2, ny + 2, 3, EDGE, WIDTH), jnp.float32)
+    row_view = pltpu.VMEM((3, VIEW, ROWS, WIDTH), jnp.bfloat16)
     product = 2 * 2 * 512 * 27 * WIDTH * WIDTH
 
     def shift(block, axis, step):
@@ -425,7 +440,7 @@
             lambda *refs: terms_kernel(i, *refs),
             "conv_terms",
             jax.ShapeDtypeStruct((2, PADDED, WIDTH), jnp.float32),
-            (field, masks, view, own),
+            (field, masks, view, own, strip, row_view),
             scalars=2,
             flops=product,
         )(neighbours, leaf_z, grad, feat, occ, *before)
@@ -442,7 +457,7 @@
     end, start = call(sides_kernel, "pack_sides", (side, side), nbytes=1 << 17)(top, bottom, end, start)
     left = shift(end, "gy", 1)
     right = shift(start, "gy", -1)
-    terms = terms_of(1, terms)
+    terms = terms_of(1, top, bottom, terms)
     edges = (top, bottom, left, right)
     mine, theirs, halo = call(
         edge_kernel,
@@ -454,9 +469,7 @@
         ),
         (
             pltpu.VMEM((2, PADDED, WIDTH), jnp.float32),
-            pltpu.VMEM((2, ny + 2, 3, EDGE, WIDTH), jnp.float32),
             pltpu.VMEM((2, nx + 2, 3, EDGE, WIDTH), jnp.float32),
-            pltpu.VMEM((3, VIEW, ROWS, WIDTH), jnp.bfloat16),
             pltpu.VMEM((3, VIEW, EDGE, WIDTH), jnp.float32),
         ),
         scalars=3,

time: 85.1 us -> 85.1 us (level)
  waiting for transfers between devices: 13.9 us -> 13 us
  transfers between devices with their start and end apart: 8 -> 8, of which waited for: 6 -> 6; matrix products, arithmetic and copies ran while one was open for 0% -> 0% of each run, Pallas kernels for 18% -> 19%
where the time goes in v8:
time: 85.1 us; the launch traced here: 84.5 us
  starting transfers between devices  29.8 us (35%)
  Pallas kernels  22.9 us (27%)
  blocking collectives  17.9 us (21%)
  waiting for transfers between devices  13 us (15%)
    all_to_all x1, blocking collectives, exchange(): return lax.all_to_all(blocks, axis, 0, 0)  17.9 us
    all_to_all x2, starting transfers between devices, exchange(): return lax.all_to_all(blocks, axis, 0, 0)  11.6 us
    pallas_call x8, Pallas kernels, run(): pl.pallas_call(kernel, out_shape=out_shape, in_specs=[SMEM] * scalars + [...  10.6 us
    ppermute x4, starting transfers between devices, shift(): return lax.ppermute(block, axis, pairs)  10.2 us
    all_to_all x2, waiting for transfers between devices, exchange(): return lax.all_to_all(blocks, axis, 0, 0)  9.8 us
    pallas_call x2, Pallas kernels, features_call(): pl.pallas_call(lambda *refs: feature_kernel(i, *refs), grid=(1,), out_sha...  8.3 us
    ppermute x1, starting transfers between devices, local(): other = lax.ppermute(total, 'dcn', [(0, 1), (1, 0)])  4.65 us
    ppermute x1, starting transfers between devices, local(): theirs = lax.ppermute(theirs, 'dcn', [(0, 1), (1, 0)])  3.44 us
  transfers between devices with their start and end apart: 8, of which 6 were waited for; matrix products, arithmetic and copies ran while one was open for 0% of the time, Pallas kernels for 19%

profile of v8, /device:TPU:1, one launch (start us, length us, event | category | flops | bytes accessed | tf_op | source)
XLA Modules:
  0.0 84.5 jit_solution(1204769433504274256)
XLA Ops:
  0.6 0.0 copy-start.2
  0.6 0.0 copy-start
  0.7 0.0 copy-start.4
  0.7 0.0 copy-start.5
  0.7 0.0 copy-start.1
  0.7 1.9 %pack_edges.1 = (bf16[1,16,2,8,128]{4,3,2,1,0:T(8,128)(2,1)}, bf16[1,16,2,8,128]{4,3,2,1,0:T(8,128)(2,1)}) custom-call(s32[16,2,8,16]{3,2,1,0:T(8,128)} %bitcast.18, s32[16,2,8,16]{3,2,1,0:T(8,128)} %bitcast.19, bf16[16,16,2,8,128]{4,3,2,1,0:T(8,128)(2,1)} %bitcast.8, bf16[16,16,2,8,128]{4,3,2,1,0:T(8,128)(2,1)} %bitcast.9), custom_call_target="tpu_custom_call" | custom-call | bytes 262144 | tf_op jit(solution)/shard_map/pack_edges/pallas_call | solution.py:382
  2.6 4.4 %collective-permute-start = (bf16[1,16,2,8,128]{4,3,2,1,0:T(8,128)(2,1)}, bf16[1,16,2,8,128]{4,3,2,1,0:T(8,128)(2,1)S(1)}, u32[]{:S(2)}, u32[]{:S(2)}) collective-permute-start(bf16[1,16,2,8,128]{4,3,2,1,0:T(8,128)(2,1)} %get-tuple-element.28), channel_id=1, source_target_pairs={{0,16},{16,32},{32,48},{48,64},{64,80},{80,96},{96,112},{1,17},{17... | collective-permute-start | bytes 196616 | tf_op jit(solution)/shard_map/ppermute | solution.py:433
  6.9 1.3 %collective-permute-start.1 = (bf16[1,16,2,8,128]{4,3,2,1,0:T(8,128)(2,1)}, bf16[1,16,2,8,128]{4,3,2,1,0:T(8,128)(2,1)S(1)}, u32[]{:S(2)}, u32[]{:S(2)}) collective-permute-start(bf16[1,16,2,8,128]{4,3,2,1,0:T(8,128)(2,1)} %get-tuple-element.29), channel_id=1, source_target_pairs={{16,0},{32,16},{48,32},{64,48},{80,64},{96,80},{112,96},{17,1},{33... | collective-permute-start | bytes 196616 | tf_op jit(solution)/shard_map/ppermute | solution.py:433
  8.2 0.0 copy-done.2
  8.2 0.0 copy-done
  8.2 0.1 own_sides.1
  8.4 0.0 copy-done.4
  8.4 0.0 copy-done.5
  8.4 0.0 copy-done.1
  8.4 2.8 %conv_terms.2.refs_7_ = f32[2,1792,128]{2,1,0:T(8,128)S(1)} custom-call(s32[1,2,2,2,27]{4,3,2,1,0:T(2,128)S(1)} %copy-done.4, s32[1,2,2,2]{3,2,1,0:T(2,128)S(1)} %copy-done.5, bf16[16,16,2,8,128]{4,3,2,1,0:T(8,128)(2,1)S(1)} %bitcast.11, bf16[16,16,2,8,128]{4,3,2,1,0:T(8,128)(2,1)S(1)} %bitcast.15, s32[16,2,8,16]{3,2,1,0:T(8,128)S(1)} %bitcast.21), custom_call_target="tpu_custom_call" | custom-call | flops 905969664 | bytes 4194304 | tf_op jit(solution)/shard_map/conv_terms/pallas_call | solution.py:341
  11.2 0.0 collective-permute-done.top.refs_5_
  11.2 1.1 %collective-permute-done.1.bottom.refs_6_ = bf16[1,16,2,8,128]{4,3,2,1,0:T(8,128)(2,1)S(1)} collective-permute-done((bf16[1,16,2,8,128]{4,3,2,1,0:T(8,128)(2,1)}, bf16[1,16,2,8,128]{4,3,2,1,0:T(8,128)(2,1)S(1)}, u32[]{:S(2)}, u32[]{:S(2)}) %collective-permute-start.1) | collective-permute-done | bytes 65568 | tf_op jit(solution)/shard_map/ppermute | solution.py:433
  12.3 3.2 %collective-permute-start.2 = (bf16[18,1,2,8,128]{4,3,2,1,0:T(8,128)(2,1)S(1)}, bf16[18,1,2,8,128]{4,3,2,1,0:T(8,128)(2,1)S(1)}, u32[]{:S(2)}, u32[]{:S(2)}) collective-permute-start(bf16[18,1,2,8,128]{4,3,2,1,0:T(8,128)(2,1)S(1)} %get-tuple-element.34), channel_id=1, source_target_pairs={{0,1},{1,2},{2,3},{3,4},{4,5},{5,6},{6,7},{7,8},{8,9},{9,10},{10,1... | collective-permute-start | bytes 221192 | tf_op jit(solution)/shard_map/ppermute | solution.py:433
  15.6 1.3 %collective-permute-start.3 = (bf16[18,1,2,8,128]{4,3,2,1,0:T(8,128)(2,1)S(1)}, bf16[18,1,2,8,128]{4,3,2,1,0:T(8,128)(2,1)S(1)}, u32[]{:S(2)}, u32[]{:S(2)}) collective-permute-start(bf16[18,1,2,8,128]{4,3,2,1,0:T(8,128)(2,1)S(1)} %get-tuple-element.35), channel_id=1, source_target_pairs={{1,0},{2,1},{3,2},{4,3},{5,4},{6,5},{7,6},{8,7},{9,8},{10,9},{11,1... | collective-permute-start | bytes 221192 | tf_op jit(solution)/shard_map/ppermute | solution.py:433
  16.9 3.6 %conv_terms.3.before = f32[2,1792,128]{2,1,0:T(8,128)S(1)} custom-call(s32[1,2,2,2,27]{4,3,2,1,0:T(2,128)S(1)} %copy-done.4, s32[1,2,2,2]{3,2,1,0:T(2,128)S(1)} %copy-done.5, bf16[16,16,2,8,128]{4,3,2,1,0:T(8,128)(2,1)S(1)} %bitcast.12, bf16[16,16,2,8,128]{4,3,2,1,0:T(8,128)(2,1)S(1)} %bitcast.16, s32[16,2,8,16]{3,2,1,0:T(8,128)S(1)} %bitcast.22, ...), custom_call_target="tpu_custom_call" | custom-call | flops 905969664 | bytes 4194304 | tf_op jit(solution)/shard_map/conv_terms/pallas_call | solution.py:341
  20.5 0.0 collective-permute-done.2.left
  20.5 0.2 collective-permute-done.3.right
  20.7 1.9 %edge_terms.1 = (f32[1792,128]{1,0:T(8,128)S(1)}, s16[16,120,128]{2,1,0:T(8,128)(2,1)S(1)}, bf16[68,2,8,128]{3,2,1,0:T(8,128)(2,1)S(1)}) custom-call(s32[1,2,2,2,27]{4,3,2,1,0:T(2,128)S(1)} %copy-done.4, s32[1,2,2,2]{3,2,1,0:T(2,128)S(1)} %copy-done.5, s32[1]{0:T(128)} %bitcast.1.core.refs_0_, bf16[16,16,2,8,128]{4,3,2,1,0:T(8,128)(2,1)S(1)} %bitcast.17, ...), custom_call_target="tpu_custom_call" | custom-call | flops 226492416 | bytes 4194304 | tf_op jit(solution)/shard_map/edge_terms/pallas_call | solution.py:341
  22.6 3.4 %collective-permute-start.4 = (s16[16,120,128]{2,1,0:T(8,128)(2,1)S(1)}, s16[16,120,128]{2,1,0:T(8,128)(2,1)S(1)}, u32[]{:S(2)}, u32[]{:S(2)}) collective-permute-start(s16[16,120,128]{2,1,0:T(8,128)(2,1)S(1)} %get-tuple-element.38), channel_id=1, source_target_pairs={{0,128},{128,0},{1,129},{129,1},{2,130},{130,2},{3,131},{131,3},{4... | collective-permute-start | bytes 1474568 | tf_op jit(solution)/shard_map/ppermute | solution.py:478
  26.0 1.5 %collective-permute-done.4.theirs = s16[16,120,128]{2,1,0:T(8,128)(2,1)S(1)} collective-permute-done((s16[16,120,128]{2,1,0:T(8,128)(2,1)S(1)}, s16[16,120,128]{2,1,0:T(8,128)(2,1)S(1)}, u32[]{:S(2)}, u32[]{:S(2)}) %collective-permute-start.4) | collective-permute-done | bytes 491552 | tf_op jit(solution)/shard_map/ppermute | solution.py:478
  27.5 0.0 copy-start.3
  27.5 0.3 encode_half.1
  27.9 17.9 %all_to_all.15.c = s16[16,120,128]{2,1,0:T(8,128)(2,1)S(1)} all-to-all(s16[16,120,128]{2,1,0:T(8,128)(2,1)S(1)} %encode_half.1), channel_id=1, replica_groups=mesh['dcn'=2,'gx'=8,'gy'=16] {'gy'}, dimensions={0} | all-to-all | bytes 983040 | tf_op jit(solution)/shard_map/all_to_all | solution.py:410
  45.7 0.9 %sum_piece.1 = s16[8,120,128]{2,1,0:T(8,128)(2,1)} custom-call(s16[16,120,128]{2,1,0:T(8,128)(2,1)S(1)} %all_to_all.15.c), custom_call_target="tpu_custom_call" | custom-call | bytes 1048576 | tf_op jit(solution)/shard_map/sum_piece/pallas_call | solution.py:341
  46.6 8.0 %all-to-all-start.1 = ((s16[8,120,128]{2,1,0:T(8,128)(2,1)}), s16[8,120,128]{2,1,0:T(8,128)(2,1)S(1)}, u32[]{:S(2)}, u32[]{:S(2)}) async-start(s16[8,120,128]{2,1,0:T(8,128)(2,1)} %sum_piece.1), calls=%async_computation.1 | async-start | bytes 491520 | tf_op jit(solution)/shard_map/all_to_all | solution.py:410
  54.7 0.0 copy-done.3
  54.7 4.1 %conv_features.2.refs_6_ = bf16[16,16,2,8,128]{4,3,2,1,0:T(8,128)(2,1)} custom-call(s32[1,2,2,2,27]{4,3,2,1,0:T(2,128)S(1)} %copy-done.4, s32[1,2,2,2]{3,2,1,0:T(2,128)S(1)} %copy-done.5, bf16[16,16,2,8,128]{4,3,2,1,0:T(8,128)(2,1)S(1)} %bitcast.13, s32[16,2,8,16]{3,2,1,0:T(8,128)S(1)} %bitcast.24, bf16[68,2,8,128]{3,2,1,0:T(8,128)(2,1)S(1)} %get-tuple-element.41.refs_4_, ...), custom_call_target="tpu_custom_call" | custom-call | flops 905969664 | bytes 4194304 | tf_op jit(solution)/shard_map/conv_features/pallas_call | solution.py:362
  58.8 5.1 %all-to-all-done.1.c = s16[8,120,128]{2,1,0:T(8,128)(2,1)S(1)} async-done(((s16[8,120,128]{2,1,0:T(8,128)(2,1)}), s16[8,120,128]{2,1,0:T(8,128)(2,1)S(1)}, u32[]{:S(2)}, u32[]{:S(2)}) %all-to-all-start.1) | async-done | bytes 245792 | tf_op jit(solution)/shard_map/all_to_all | solution.py:410
  63.9 0.9 %sum_total.1 = s16[16,120,128]{2,1,0:T(8,128)(2,1)} custom-call(s16[8,120,128]{2,1,0:T(8,128)(2,1)S(1)} %all-to-all-done.1.c), custom_call_target="tpu_custom_call" | custom-call | bytes 1048576 | tf_op jit(solution)/shard_map/sum_total/pallas_call | solution.py:341
  64.9 3.6 %all-to-all-start.2 = ((s16[16,120,128]{2,1,0:T(8,128)(2,1)}), s16[16,120,128]{2,1,0:T(8,128)(2,1)S(1)}, u32[]{:S(2)}, u32[]{:S(2)}) async-start(s16[16,120,128]{2,1,0:T(8,128)(2,1)} %sum_total.1), calls=%async_computation.2 | async-start | bytes 983040 | tf_op jit(solution)/shard_map/all_to_all | solution.py:410
  68.4 4.2 %conv_features.3 = bf16[16,16,2,8,128]{4,3,2,1,0:T(8,128)(2,1)} custom-call(s32[1,2,2,2,27]{4,3,2,1,0:T(2,128)S(1)} %copy-done.4, s32[1,2,2,2]{3,2,1,0:T(2,128)S(1)} %copy-done.5, bf16[16,16,2,8,128]{4,3,2,1,0:T(8,128)(2,1)S(1)} %bitcast.14, s32[16,2,8,16]{3,2,1,0:T(8,128)S(1)} %bitcast.25, ...), custom_call_target="tpu_custom_call", output_to_operand_aliasing={{}: (6, {})} | custom-call | flops 905969664 | bytes 4194304 | tf_op jit(solution)/shard_map/conv_features/pallas_call | solution.py:362
  72.6 4.7 %all-to-all-done.2.refs_1_ = s16[16,120,128]{2,1,0:T(8,128)(2,1)S(1)} async-done(((s16[16,120,128]{2,1,0:T(8,128)(2,1)}), s16[16,120,128]{2,1,0:T(8,128)(2,1)S(1)}, u32[]{:S(2)}, u32[]{:S(2)}) %all-to-all-start.2) | async-done | bytes 491552 | tf_op jit(solution)/shard_map/all_to_all | solution.py:410
  77.3 4.6 %collective-permute-start.5 = (s16[16,120,128]{2,1,0:T(8,128)(2,1)S(1)}, s16[16,120,128]{2,1,0:T(8,128)(2,1)S(1)}, u32[]{:S(2)}, u32[]{:S(2)}) collective-permute-start(s16[16,120,128]{2,1,0:T(8,128)(2,1)S(1)} %all-to-all-done.2.refs_1_), channel_id=1, source_target_pairs={{0,128},{128,0},{1,129},{129,1},{2,130},{130,2},{3,131},{131,3},{4... | collective-permute-start | bytes 1474568 | tf_op jit(solution)/shard_map/ppermute | solution.py:493
  81.9 1.0 %decode_half.2.refs_2_ = f32[3456,128]{1,0:T(8,128)} custom-call(s32[1]{0:T(128)} %bitcast.1.core.refs_0_, s16[16,120,128]{2,1,0:T(8,128)(2,1)S(1)} %all-to-all-done.2.refs_1_), custom_call_target="tpu_custom_call" | custom-call | bytes 1572864 | tf_op jit(solution)/shard_map/decode_half/pallas_call | solution.py:396
  83.0 0.4 collective-permute-done.5.refs_1_
  83.4 1.0 %decode_half.3 = f32[3456,128]{1,0:T(8,128)} custom-call(s32[1]{0:T(128)} %bitcast.1.core.refs_0_, s16[16,120,128]{2,1,0:T(8,128)(2,1)S(1)} %collective-permute-done.5.refs_1_, f32[3456,128]{1,0:T(8,128)} %decode_half.2.refs_2_), custom_call_target="tpu_custom_call", output_to_operand_aliasing={{}: (2, {})} | custom-call | bytes 1572864 | tf_op jit(solution)/shard_map/decode_half/pallas_call | solution.py:396
  (1 shorter events, 0.0 us)
Async XLA Ops:
  0.6 7.6 %copy-start.2 = (s32[1,16,16,2,8]{2,4,3,1,0:T(8,128)S(1)}, s32[1,16,16,2,8]{2,4,3,1,0:T(8,128)}, u32[]{:S(2)}) copy-start(s32[1,16,16,2,8]{2,4,3,1,0:T(8,128)} %param.8) | copy-start | bytes 49156
  0.6 7.6 %copy-start = (bf16[1,16,16,2,8,128]{5,4,3,2,1,0:T(8,128)(2,1)S(1)}, bf16[1,16,16,2,8,128]{5,4,3,2,1,0:T(8,128)(2,1)}, u32[]{:S(2)}) copy-start(bf16[1,16,16,2,8,128]{5,4,3,2,1,0:T(8,128)(2,1)} %param.7) | copy-start | bytes 3145732
  0.7 7.7 %copy-start.4 = (s32[1,2,2,2,27]{4,3,2,1,0:T(2,128)S(1)}, s32[1,2,2,2,27]{4,3,2,1,0:T(2,128)}, u32[]{:S(2)}) copy-start(s32[1,2,2,2,27]{4,3,2,1,0:T(2,128)} %refs_0_.7) | copy-start | bytes 2596
  0.7 7.7 %copy-start.5 = (s32[1,2,2,2]{3,2,1,0:T(2,128)S(1)}, s32[1,2,2,2]{3,2,1,0:T(2,128)}, u32[]{:S(2)}) copy-start(s32[1,2,2,2]{3,2,1,0:T(2,128)} %refs_1_.7) | copy-start | bytes 100
  0.7 7.7 %copy-start.1 = (bf16[1,16,16,2,8,128]{5,4,3,2,1,0:T(8,128)(2,1)S(1)}, bf16[1,16,16,2,8,128]{5,4,3,2,1,0:T(8,128)(2,1)}, u32[]{:S(2)}) copy-start(bf16[1,16,16,2,8,128]{5,4,3,2,1,0:T(8,128)(2,1)} %param.6) | copy-start | bytes 3145732
  2.6 8.6 %collective-permute-start = (bf16[1,16,2,8,128]{4,3,2,1,0:T(8,128)(2,1)}, bf16[1,16,2,8,128]{4,3,2,1,0:T(8,128)(2,1)S(1)}, u32[]{:S(2)}, u32[]{:S(2)}) collective-permute-start(bf16[1,16,2,8,128]{4,3,2,1,0:T(8,128)(2,1)} %get-tuple-element.28), channel_id=1, source_target_pairs={{0,16},{16,32},{32,48},{48,64},{64,80},{80,96},{96,112},{1,17},{17... | collective-permute-start | bytes 196616 | tf_op jit(solution)/shard_map/ppermute | solution.py:433
  6.9 5.4 %collective-permute-start.1 = (bf16[1,16,2,8,128]{4,3,2,1,0:T(8,128)(2,1)}, bf16[1,16,2,8,128]{4,3,2,1,0:T(8,128)(2,1)S(1)}, u32[]{:S(2)}, u32[]{:S(2)}) collective-permute-start(bf16[1,16,2,8,128]{4,3,2,1,0:T(8,128)(2,1)} %get-tuple-element.29), channel_id=1, source_target_pairs={{16,0},{32,16},{48,32},{64,48},{80,64},{96,80},{112,96},{17,1},{33... | collective-permute-start | bytes 196616 | tf_op jit(solution)/shard_map/ppermute | solution.py:433
  12.3 8.1 %collective-permute-start.2 = (bf16[18,1,2,8,128]{4,3,2,1,0:T(8,128)(2,1)S(1)}, bf16[18,1,2,8,128]{4,3,2,1,0:T(8,128)(2,1)S(1)}, u32[]{:S(2)}, u32[]{:S(2)}) collective-permute-start(bf16[18,1,2,8,128]{4,3,2,1,0:T(8,128)(2,1)S(1)} %get-tuple-element.34), channel_id=1, source_target_pairs={{0,1},{1,2},{2,3},{3,4},{4,5},{5,6},{6,7},{7,8},{8,9},{9,10},{10,1... | collective-permute-start | bytes 221192 | tf_op jit(solution)/shard_map/ppermute | solution.py:433
  15.6 5.1 %collective-permute-start.3 = (bf16[18,1,2,8,128]{4,3,2,1,0:T(8,128)(2,1)S(1)}, bf16[18,1,2,8,128]{4,3,2,1,0:T(8,128)(2,1)S(1)}, u32[]{:S(2)}, u32[]{:S(2)}) collective-permute-start(bf16[18,1,2,8,128]{4,3,2,1,0:T(8,128)(2,1)S(1)} %get-tuple-element.35), channel_id=1, source_target_pairs={{1,0},{2,1},{3,2},{4,3},{5,4},{6,5},{7,6},{8,7},{9,8},{10,9},{11,1... | collective-permute-start | bytes 221192 | tf_op jit(solution)/shard_map/ppermute | solution.py:433
  22.6 4.9 %collective-permute-start.4 = (s16[16,120,128]{2,1,0:T(8,128)(2,1)S(1)}, s16[16,120,128]{2,1,0:T(8,128)(2,1)S(1)}, u32[]{:S(2)}, u32[]{:S(2)}) collective-permute-start(s16[16,120,128]{2,1,0:T(8,128)(2,1)S(1)} %get-tuple-element.38), channel_id=1, source_target_pairs={{0,128},{128,0},{1,129},{129,1},{2,130},{130,2},{3,131},{131,3},{4... | collective-permute-start | bytes 1474568 | tf_op jit(solution)/shard_map/ppermute | solution.py:478
  27.5 27.1 %copy-start.3 = (bf16[27,128,128]{2,1,0:T(8,128)(2,1)S(1)}, bf16[27,128,128]{2,1,0:T(8,128)(2,1)}, u32[]{:S(2)}) copy-start(bf16[27,128,128]{2,1,0:T(8,128)(2,1)} %refs_5_.3) | copy-start | bytes 2654212
  46.6 17.3 %all-to-all-start.1 = ((s16[8,120,128]{2,1,0:T(8,128)(2,1)}), s16[8,120,128]{2,1,0:T(8,128)(2,1)S(1)}, u32[]{:S(2)}, u32[]{:S(2)}) async-start(s16[8,120,128]{2,1,0:T(8,128)(2,1)} %sum_piece.1), calls=%async_computation.1 | async-start | bytes 491520 | tf_op jit(solution)/shard_map/all_to_all | solution.py:410
  64.9 12.4 %all-to-all-start.2 = ((s16[16,120,128]{2,1,0:T(8,128)(2,1)}), s16[16,120,128]{2,1,0:T(8,128)(2,1)S(1)}, u32[]{:S(2)}, u32[]{:S(2)}) async-start(s16[16,120,128]{2,1,0:T(8,128)(2,1)} %sum_total.1), calls=%async_computation.2 | async-start | bytes 983040 | tf_op jit(solution)/shard_map/all_to_all | solution.py:410
  77.3 6.1 %collective-permute-start.5 = (s16[16,120,128]{2,1,0:T(8,128)(2,1)S(1)}, s16[16,120,128]{2,1,0:T(8,128)(2,1)S(1)}, u32[]{:S(2)}, u32[]{:S(2)}) collective-permute-start(s16[16,120,128]{2,1,0:T(8,128)(2,1)S(1)} %all-to-all-done.2.refs_1_), channel_id=1, source_target_pairs={{0,128},{128,0},{1,129},{129,1},{2,130},{130,2},{3,131},{131,3},{4... | collective-permute-start | bytes 1474568 | tf_op jit(solution)/shard_map/ppermute | solution.py:493
